TPU v7x, 256 devices: a whole 4x4x8 slice. The times are simulated.
256 devices in a mesh: blk: 8 (over x, z_lo), pair: 32 (over y, z_hi, core).
Axes of the slice: x: 4, y: 4, z: 8 (z_hi: 4, z_lo: 2; z = z_hi * 2 + z_lo), core: 2. Of those that a mesh axis runs over, the one named last changes fastest.
Arguments:
- panels: bfloat16 [192, 384, 4608], P('pair', None, 'blk'), may hold values from -0.875 to 0.875
- pattern: int32 [192, 8], P('pair', 'blk'), may hold values 0 or 1
- point_inverse: float32 [192, 9, 128], P('pair'), as said below
- camera_hessian: float32 [4608, 576], P('blk'), as said below
- damping: int32 [4608], P('blk'), may hold values from 0 to 3
- camera_grad: float32 [4608], P('blk'), may hold values from -6 to 6
- point_grad: float32 [192, 384], P('pair'), may hold values from -6 to 6
Outputs:
- schur: float32 [4608, 4608], P('pair', 'blk')
- reduced_rhs: float32 [4608], P('blk')
Inputs may be any that keep to these rules, and one draw needn't show every extreme that they name: point_inverse is symmetric in its 3 x 3 entries with a positive diagonal. camera_hessian blocks are symmetric with a positive diagonal.
All inputs are finite; a program needn't handle non-finite values. No bound on the sum of `pattern` on one device may be relied on, other than what follows from the above.
Results may differ from a plain program's by a relative error of at most 0.003.
Values may be sent and summed in bfloat16 or wider, within the bound.
No kernel may reach another device: no remote copies, remote signals or barrier semaphores. Data moves between devices by JAX's collectives and lax.ppermute only.
A program may use at most 128 MiB of HBM per device.

v0:
```python
import jax
import jax.numpy as jnp
from jax import lax
from jax.sharding import Mesh
from jax.sharding import PartitionSpec as P

BLK = ("blk_0", "blk_1")


def gathered_by_axis(array, axes, dim):
    filled = array
    for number in range(len(axes) - 1, -1, -1):
        filled = lax.all_gather(filled, axes[number], axis=dim, tiled=True)
    return filled


def copy_for_each(array, axis):
    copies = jnp.broadcast_to(array, (lax.axis_size(axis), *array.shape))
    return lax.all_to_all(copies, axis, split_axis=0, concat_axis=0, tiled=True)


def of_everyone(array, axis):
    everything = copy_for_each(array, axis)
    return jnp.sum(everything, axis=0)


def apply_inverse(inverse, shaped):
    parts = []
    for row in range(3):
        total = inverse[:, row * 3, :, None] * shaped[:, 0]
        total = total + inverse[:, row * 3 + 1, :, None] * shaped[:, 1]
        total = total + inverse[:, row * 3 + 2, :, None] * shaped[:, 2]
        parts.append(total)
    return jnp.stack(parts, axis=1)


def shards(panels, pattern, point_inverse, camera_hessian, damping, camera_grad, point_grad):
    block_count = panels.shape[0]
    camera_width = panels.shape[2]
    point_count = point_inverse.shape[2]
    panel_rows = block_count * 3 * point_count
    masked = panels * pattern.astype(jnp.bfloat16)[:, :, None]
    shaped = masked.astype(jnp.float32).reshape(block_count, 3, point_count, camera_width)
    scaled = (
        apply_inverse(point_inverse, shaped).astype(jnp.bfloat16).reshape(panel_rows, camera_width)
    )
    flat_panels = masked.reshape(panel_rows, camera_width)
    my_block = lax.axis_index(BLK)
    gathered = gathered_by_axis(scaled, BLK, 1)
    total_rows = gathered.shape[1]
    owners = lax.axis_size("pair")
    own_rows = total_rows // owners
    piece = lax.psum_scatter(
        -lax.dot_general(
            gathered, flat_panels, (((0,), (0,)), ((), ())), preferred_element_type=jnp.float32
        ),
        "pair",
        scatter_dimension=0,
        tiled=True,
    )
    diag_vals = jnp.diagonal(camera_hessian)
    levels = 0.1 * jnp.power(2.0, damping.astype(jnp.float32))
    damped = (
        camera_hessian + jnp.eye(camera_width, dtype=jnp.float32) * (levels * diag_vals)[:, None]
    )
    row_start = lax.axis_index("pair") * own_rows
    offset = jnp.clip(row_start - my_block * camera_width, 0, camera_width - own_rows)
    hessian_rows = lax.dynamic_slice_in_dim(damped, offset, own_rows, 0)
    inside = row_start // camera_width == my_block
    schur = piece + jnp.where(inside, hessian_rows, jnp.zeros_like(hessian_rows))
    grads = point_grad.reshape(block_count, 3, point_count)
    point_step = apply_inverse(point_inverse, grads[:, :, :, None])[..., 0]
    point_step = point_step.astype(jnp.bfloat16).reshape(panel_rows)
    local_terms = jnp.dot(point_step, flat_panels, preferred_element_type=jnp.float32)
    summed = of_everyone(local_terms, "pair")
    reduced_rhs = camera_grad - summed
    return (schur, reduced_rhs)


def solution(mesh):
    finer = Mesh(mesh.devices.reshape(4, 2, mesh.shape["pair"]), ("blk_0", "blk_1", "pair"))
    in_specs = (
        P("pair", None, BLK),
        P("pair", BLK),
        P("pair", None, None),
        P(BLK, None),
        P(BLK),
        P(BLK),
        P("pair", None),
    )
    out_specs = (P("pair", BLK), P(BLK))
    return jax.shard_map(
        shards, mesh=finer, in_specs=in_specs, out_specs=out_specs, check_vma=False
    )
```

profile of v0, /device:TPU:59, one launch (start us, length us, event | category | flops | bytes accessed | tf_op | source)
XLA Modules:
  0.0 468.0 jit_solution(11076051308997908275)
XLA Ops:
  7.2 0.0 all-gather.3.cloned.1.call-start
  7.2 0.8 slice_bitcast_fusion.8
  8.0 0.7 convert_bitcast_fusion
  8.7 2.1 broadcast_multiply_fusion
  10.8 4.4 copy.23
  15.2 3.9 add_convert_fusion.2
  19.1 2.1 pad_maximum_fusion
  21.2 4.5 copy.24
  25.8 0.0 all-gather.3.cloned.1.call-update
  25.8 0.0 all-gather.5.cloned.1.call-start
  25.8 75.6 %all-gather.3.cloned.1.call-done = bf16[2304,1152]{0,1:T(8,128)(2,1)} async-done(((bf16[2304,576]{0,1:T(8,128)(2,1)}), bf16[2304,1152]{0,1:T(8,128)(2,1)}) %all-gather.3.cloned.1.call-update) | async-done | bytes 5308432 | tf_op jit(solution)/shard_map/all_gather | solution.py:13
  101.4 0.0 all-gather.5.cloned.1.call-update
  101.5 0.0 reduce-scatter.2.cloned.1.call-start
  101.5 3.6 copy.25
  105.1 193.2 %all-gather.5.cloned.1.call-done = bf16[2304,4608]{0,1:T(8,128)(2,1)} async-done(((bf16[2304,1152]{0,1:T(8,128)(2,1)}), bf16[2304,4608]{0,1:T(8,128)(2,1)}) %all-gather.5.cloned.1.call-update) | async-done | bytes 21233680 | tf_op jit(solution)/shard_map/all_gather | solution.py:13
  298.3 22.2 %convolution_negate_fusion = f32[4608,576]{1,0:T(8,128)} fusion(bf16[2304,4608]{0,1:T(8,128)(2,1)} %all-gather.5.cloned.1.call-done, bf16[2304,576]{1,0:T(8,128)(2,1)} %bitcast.79), kind=kOutput, calls=%fused_computation.1 | convolution fusion | flops 12233244672 | bytes 34504704 | tf_op jit(solution)/shard_map/dot_general | solution.py:54
  320.5 0.0 copy-start.1
  320.5 0.0 copy-start.2
  320.5 0.0 reduce-scatter.2.cloned.1.call-update
  320.5 0.0 copy-start
  320.6 0.7 copy-done.1
  321.3 0.0 copy-done.2
  321.4 2.3 convolution_reduce_fusion
  323.7 0.7 broadcast_in_dim.13
  324.4 9.7 %all-to-all-start = ((f32[32,1,576]{2,1,0:T(1,128)}), f32[32,1,576]{2,1,0:T(1,128)S(1)}, u32[]{:S(2)}, u32[]{:S(2)}) async-start(f32[32,1,576]{2,1,0:T(1,128)} %broadcast_in_dim.13), calls=%async_computation.1 | async-start | bytes 163840 | tf_op jit(solution)/shard_map/all_to_all | solution.py:19
  334.2 0.0 copy-done
  334.2 0.0 copy-start.3
  334.2 0.0 copy-start.4
  334.2 4.9 %gather_fusion = f32[576]{0:T(1024)S(1)} fusion(f32[576,576]{1,0:T(8,128)S(1)} %copy-done, s32[576]{0:T(1024)S(1)} %or_reduce_fusion), kind=kCustom, calls=%fused_computation | custom fusion | bytes 9216 | tf_op jit(solution)/shard_map/jit(diagonal)/cond/branch_0_fun/gather | solution.py:61
  339.1 0.0 copy-done.3
  339.2 0.1 dynamic-slice
  339.2 3.4 all-to-all-done
  342.6 0.1 reduce_sum.9
  342.7 0.0 copy-done.4
  342.7 0.6 sub.12
  343.3 116.3 %reduce-scatter.2.cloned.1.call-done = f32[144,576]{1,0:T(8,128)} async-done(((f32[4608,576]{1,0:T(8,128)}), f32[144,576]{1,0:T(8,128)}) %reduce-scatter.2.cloned.1.call-update) | async-done | bytes 331792 | tf_op jit(solution)/shard_map/reduce_scatter | solution.py:53
  459.6 1.9 fusion.1
  (6 shorter events, 0.1 us)
Async XLA Ops:
  7.2 94.3 %all-gather.3.cloned.1.call-start = ((), (), s32[]{:S(2)}) async-start(), calls=%async_computation.2 | async-start | bytes 7962624 | tf_op jit(solution)/shard_map/all_gather | solution.py:13
  25.8 272.5 %all-gather.5.cloned.1.call-start = ((), (), s32[]{:S(2)}) async-start(), calls=%async_computation.3 | async-start | bytes 26542080 | tf_op jit(solution)/shard_map/all_gather | solution.py:13
  101.5 358.1 %reduce-scatter.2.cloned.1.call-start = ((), (), s32[]{:S(2)}) async-start(), calls=%async_computation.4 | async-start | bytes 12165120 | tf_op jit(solution)/shard_map/reduce_scatter | solution.py:53
  320.5 0.8 copy-start.1
  320.5 0.8 copy-start.2
  320.5 13.6 %copy-start = (f32[576,576]{1,0:T(8,128)S(1)}, f32[576,576]{1,0:T(8,128)}, u32[]{:S(2)}) copy-start(f32[576,576]{1,0:T(8,128)} %param.10) | copy-start | bytes 3981316
  324.4 18.3 %all-to-all-start = ((f32[32,1,576]{2,1,0:T(1,128)}), f32[32,1,576]{2,1,0:T(1,128)S(1)}, u32[]{:S(2)}, u32[]{:S(2)}) async-start(f32[32,1,576]{2,1,0:T(1,128)} %broadcast_in_dim.13), calls=%async_computation.1 | async-start | bytes 163840 | tf_op jit(solution)/shard_map/all_to_all | solution.py:19
  334.2 5.0 %copy-start.3 = (s32[576]{0:T(1024)S(1)}, s32[576]{0:T(1024)}, u32[]{:S(2)}) copy-start(s32[576]{0:T(1024)} %param.11) | copy-start | bytes 6916
  334.2 8.5 %copy-start.4 = (f32[576]{0:T(1024)S(1)}, f32[576]{0:T(1024)}, u32[]{:S(2)}) copy-start(f32[576]{0:T(1024)} %param.12) | copy-start | bytes 6916
Sparse Core Ops, SparseCore 0:
  25.9 75.4 all-gather.2
  103.3 194.9 all-gather.4
  320.7 138.8 reduce-scatter.1
where the time goes:
time: 471 us; the launch traced here: 468 us
  waiting for transfers between devices  389 us (83%)
  matrix products  24.5 us (5%)
  local copies, waits for them, and re-layouts  19.9 us (4%)
  between operations  13.9 us (3%)
  other arithmetic  11.3 us (2%)
  starting transfers between devices  9.83 us (2%)
    all_gather x2, waiting for transfers between devices, gathered_by_axis(): filled = lax.all_gather(filled, axes[number], axis=dim, tiled=True)  269 us
    reduce_scatter x1, waiting for transfers between devices, shards(): lax.psum_scatter(-lax.dot_general(gathered, flat_panels, (((0,), (0,)), (...  116 us
    dot_general x1, matrix products, shards(): lax.dot_general(gathered, flat_panels, (((0,), (0,)), ((), ())), preferre...  22.2 us
    all_to_all x1, starting transfers between devices, copy_for_each(): return lax.all_to_all(copies, axis, split_axis=0, concat_axis=0, tiled=True)  9.71 us
  transfers between devices with their start and end apart: 4, of which 4 were waited for; matrix products, arithmetic and copies ran while one was open for 3% of the time, Pallas kernels for 0%

commit v1 on v0

v1 whole, which is shorter than its diff:
```python
import functools

import jax
import jax.numpy as jnp
from jax import lax
from jax.experimental import pallas as pl
from jax.experimental.pallas import tpu as pltpu
from jax.sharding import Mesh
from jax.sharding import PartitionSpec as P

X, L, Y, H, C = 4, 2, 4, 4, 2
BLK = ("x", "l")
PAIR = ("y", "h", "c")
CHUNKS = 3
F32 = jnp.float32
BF16 = jnp.bfloat16


def rotate(array, axis, size, step):
    return lax.ppermute(array, axis, [(i, (i + step) % size) for i in range(size)])


def apply_inverse(inverse, shaped):
    parts = []
    for row in range(3):
        total = inverse[:, row * 3] * shaped[:, 0]
        total = total + inverse[:, row * 3 + 1] * shaped[:, 1]
        total = total + inverse[:, row * 3 + 2] * shaped[:, 2]
        parts.append(total)
    return jnp.stack(parts, axis=1)


def product_kernel(first, last, *refs):
    where_ref, own_ref, mate_ref, next_ref, far_ref, inv_ref = refs[:6]
    refs = refs[6:]
    if not first:
        before_ref, refs = refs[0], refs[1:]
    if last:
        send_ref, keep_ref, scaled_ref, sums_ref = refs
    else:
        sums_ref, scaled_ref = refs
    blocks, width, rows = own_ref.shape
    points = inv_ref.shape[2]
    for block in range(blocks):
        for side, ref in enumerate((own_ref, mate_ref)):
            parts = [
                ref[block, :, c * points : (c + 1) * points].astype(F32) for c in range(3)
            ]
            for a in range(3):
                total = inv_ref[block, 3 * a : 3 * a + 1, :] * parts[0]
                total = total + inv_ref[block, 3 * a + 1 : 3 * a + 2, :] * parts[1]
                total = total + inv_ref[block, 3 * a + 2 : 3 * a + 3, :] * parts[2]
                at = block * rows + a * points
                scaled_ref[side * width : (side + 1) * width, at : at + points] = (
                    total.astype(BF16)
                )
    total_width = 2 * width
    half_start = pl.multiple_of(where_ref[1] * rows, rows)
    for start in range(0, total_width, 256):
        stop = min(start + 256, total_width)
        columns = slice(start, stop)
        for kind in range(3):
            if kind < 2:
                ref = own_ref if kind == 0 else next_ref
                left = jnp.concatenate([ref[b] for b in range(blocks)], axis=1)
                right = scaled_ref[columns, :]
            else:
                left = far_ref[0]
                right = scaled_ref[columns, pl.ds(half_start, rows)]
            term = lax.dot_general(
                left, right, (((1,), (1,)), ((), ())), preferred_element_type=F32
            ).reshape(2, 2, width // 4, stop - start)
            if not first:
                term = term + before_ref[kind, :, :, :, columns]
            if last:
                sums_ref[kind, :, :, :, columns] = term
                core = where_ref[0]
                for i in range(2):
                    send_ref[kind, i, :, columns] = sums_ref[
                        kind, i, 1 - core, :, columns
                    ].astype(BF16)
                    keep_ref[kind, i, :, columns] = sums_ref[
                        kind, i, core, :, columns
                    ].astype(BF16)
            else:
                sums_ref[kind, :, :, :, columns] = term


def product(first, last, where, own, mate, following, far, inverse, before=None):
    blocks, width, rows = own.shape
    sums = (3, 2, 2, width // 4, 2 * width)
    half = (3, 2, width // 4, 2 * width)
    vmem = pl.BlockSpec(memory_space=pltpu.VMEM)
    scaled = pltpu.VMEM((2 * width, blocks * rows), BF16)
    if last:
        out_shape = (jax.ShapeDtypeStruct(half, BF16), jax.ShapeDtypeStruct(half, BF16))
        out_specs = (vmem, vmem)
        scratch = [scaled, pltpu.VMEM(sums, F32)]
    else:
        out_shape = jax.ShapeDtypeStruct(sums, F32)
        out_specs = vmem
        scratch = [scaled]
    operands = [where, own, mate, following, far, inverse]
    specs = [pl.BlockSpec(memory_space=pltpu.SMEM)] + [vmem] * 5
    if not first:
        operands.append(before)
        specs.append(vmem)
    flops = 2 * width * 2 * width * rows * (2 * blocks + 1)
    return pl.pallas_call(
        functools.partial(product_kernel, first, last),
        out_shape=out_shape,
        in_specs=specs,
        out_specs=out_specs,
        scratch_shapes=scratch,
        compiler_params=pltpu.CompilerParams(vmem_limit_bytes=48 * 2**20),
        cost_estimate=pl.CostEstimate(
            flops=flops, bytes_accessed=16 * 2**20, transcendentals=0
        ),
        name="product",
    )(*operands)


def shards(panels, pattern, point_inverse, camera_hessian, damping, camera_grad, point_grad):
    count = panels.shape[0]
    width = panels.shape[2]
    points = point_inverse.shape[2]
    x, l = lax.axis_index("x"), lax.axis_index("l")
    y, h, c = lax.axis_index("y"), lax.axis_index("h"), lax.axis_index("c")
    upper = x // 2
    masked = jnp.transpose(panels, (0, 2, 1)) * pattern.astype(BF16)[:, :, None]

    size = count // CHUNKS
    chunks = []
    for n in range(CHUNKS):
        own = masked[n * size : (n + 1) * size]
        mate = rotate(own, "l", L, 1)
        following = rotate(own, "x", X, -1)
        sent = lax.dynamic_slice_in_dim(masked, n * size + 1 - upper, 1, 0)
        far = rotate(rotate(sent, "x", X, 1), "x", X, 1)
        chunks.append((own, mate, following, far, point_inverse[n * size : (n + 1) * size]))

    grads = point_grad.reshape(count, 3, points)
    step = apply_inverse(point_inverse, grads).astype(BF16).astype(F32)
    step = step.reshape(count, 1, 3 * points)
    terms = jnp.sum(masked.astype(F32) * step, axis=(0, 2))
    terms = terms + rotate(terms, "c", C, 1)
    terms = terms + sum(rotate(terms, "y", Y, k) for k in range(1, Y))
    terms = terms + sum(rotate(terms, "h", H, k) for k in range(1, H))
    reduced_rhs = camera_grad - terms

    where = jnp.stack([c, upper]).astype(jnp.int32)
    sums = None
    for n, chunk in enumerate(chunks):
        sums = product(n == 0, n == CHUNKS - 1, where, *chunk, before=sums)
    send, keep = sums
    other = rotate(send, "c", C, 1)

    def of_kind(kind):
        at = jnp.minimum(kind, 2)
        return lax.dynamic_index_in_dim(keep, at, 0, False).astype(
            F32
        ) + lax.dynamic_index_in_dim(other, at, 0, False).astype(F32)

    kind = (y - x) % Y
    held = jnp.where(kind < 3, of_kind(kind), 0.0)
    for k in range(1, Y):
        pairs = [
            (a * Y + b, a * Y + (b + k) % Y)
            for a in range(X)
            for b in range(Y)
            if (b + k - a) % Y < 3
        ]
        piece = of_kind((y + k - x) % Y).astype(BF16)
        held = held + lax.ppermute(piece, ("x", "y"), pairs).astype(F32)

    pieces = held.reshape(2, width // 4, 2, width)
    total = jnp.zeros((width // 4, width), F32)
    for m in range(4):
        pairs = [
            (a * H + b, ((b ^ m) & 1) * H + 2 * a + ((b ^ m) >> 1))
            for a in range(L)
            for b in range(H)
        ]
        picked = h ^ m
        row = lax.dynamic_index_in_dim(pieces, picked // 2, 0, False)
        side = (picked % 2) ^ l
        piece = jnp.where(side == 0, row[:, 0], row[:, 1]).astype(BF16)
        total = total + lax.ppermute(piece, ("l", "h"), pairs).astype(F32)

    quarter = width // 4
    turned = total.T.reshape(4, quarter, quarter).astype(BF16)
    low = (h % 2) * 2 + c
    mirrored = []
    for m in range(4):
        pairs = []
        for a in range(X):
            for e in range(Y):
                if (e - a) % Y not in (1, 2):
                    continue
                for l0 in range(L):
                    for h0 in range(H):
                        for c0 in range(C):
                            to = ((h0 % 2) * 2 + c0) ^ m
                            source = (((a * L + l0) * Y + e) * H + h0) * C + c0
                            target = (
                                ((e * L + h0 // 2) * Y + a) * H + 2 * l0 + to // 2
                            ) * C + to % 2
                            pairs.append((source, target))
        piece = lax.dynamic_index_in_dim(turned, low ^ m, 0, False)
        mirrored.append(lax.ppermute(piece, ("x", "l", "y", "h", "c"), pairs))
    mirrored = jnp.stack(mirrored)
    mirror = jnp.concatenate(
        [lax.dynamic_index_in_dim(mirrored, low ^ q, 0, False) for q in range(4)], axis=1
    )

    levels = 0.1 * jnp.power(2.0, damping.astype(F32))
    on_diagonal = jnp.eye(width, dtype=bool)
    damped = camera_hessian + jnp.where(on_diagonal, camera_hessian * levels[:, None], 0.0)
    own_rows = lax.dynamic_slice_in_dim(damped, low * quarter, quarter, 0)
    inside = jnp.logical_and(x == y, h // 2 == l)
    schur = jnp.where(inside, own_rows, 0.0) - (total + mirror.astype(F32))
    return (schur, reduced_rhs)


def solution(mesh):
    finer = Mesh(mesh.devices.reshape(X, L, Y, H, C), ("x", "l", "y", "h", "c"))
    in_specs = (
        P(PAIR, None, BLK),
        P(PAIR, BLK),
        P(PAIR, None, None),
        P(BLK, None),
        P(BLK),
        P(BLK),
        P(PAIR, None),
    )
    out_specs = (P(PAIR, BLK), P(BLK))
    return jax.shard_map(
        shards, mesh=finer, in_specs=in_specs, out_specs=out_specs, check_vma=False
    )
```

time: 471 us -> 202 us (0.43)
  waiting for transfers between devices: 389 us -> 78.1 us
  starting transfers between devices: 9.83 us -> 71.7 us
  Pallas kernels: 0 us -> 29.6 us
  matrix products: 24.5 us -> 0 us
  between operations: 13.9 us -> 1.05 us
  local copies, waits for them, and re-layouts: 19.9 us -> 8.56 us
    all_gather x2 -> x0, waiting for transfers between devices: 269 us -> none  [gathered_by_axis(): filled = lax.all_gather(filled, axes[number], axis=dim, tiled=True)]
    reduce_scatter x1 -> x0, waiting for transfers between devices: 116 us -> none  [shards(): lax.psum_scatter(-lax.dot_general(gathered, flat_panels, (((0,), (0,)), (...]
    ppermute x0 -> x31, waiting for transfers between devices: none -> 78.1 us  [the longest x20 44.6 us: rotate(): lax.ppermute(array, axis, [(i, (i + step) % size) for i in range(size)])]
    ppermute x0 -> x31, starting transfers between devices: none -> 71.7 us  [the longest x4 28.5 us: shards(): mirrored.append(lax.ppermute(piece, ('x', 'l', 'y', 'h', 'c'), pairs))]
    pallas_call x0 -> x3, Pallas kernels: none -> 29.6 us  [product(): pl.pallas_call(functools.partial(product_kernel, first, last), out_shape=...]
    dot_general x2 -> x0, matrix products: 24.5 us -> none  [the longest x1 22.2 us: shards(): lax.dot_general(gathered, flat_panels, (((0,), (0,)), ((), ())), preferre...]
    all_to_all x1 -> x0, starting transfers between devices: 9.71 us -> none  [copy_for_each(): return lax.all_to_all(copies, axis, split_axis=0, concat_axis=0, tiled=True)]
    another operation x4 -> x3, other arithmetic: 6.05 us -> 0.99 us
  transfers between devices with their start and end apart: 4 -> 31, of which waited for: 4 -> 13; matrix products, arithmetic and copies ran while one was open for 3% -> 4% of each run, Pallas kernels for 0% -> 10%
where the time goes in v1:
time: 202 us; the launch traced here: 201 us
  waiting for transfers between devices  78.1 us (39%)
  starting transfers between devices  71.7 us (35%)
  Pallas kernels  29.6 us (15%)
  other arithmetic  12.4 us (6%)
  local copies, waits for them, and re-layouts  8.56 us (4%)
    ppermute x20, waiting for transfers between devices, rotate(): lax.ppermute(array, axis, [(i, (i + step) % size) for i in range(size)])  44.6 us
    pallas_call x3, Pallas kernels, product(): pl.pallas_call(functools.partial(product_kernel, first, last), out_shape=...  29.6 us
    ppermute x4, starting transfers between devices, shards(): mirrored.append(lax.ppermute(piece, ('x', 'l', 'y', 'h', 'c'), pairs))  28.5 us
    ppermute x20, starting transfers between devices, rotate(): lax.ppermute(array, axis, [(i, (i + step) % size) for i in range(size)])  25 us
    ppermute x3, waiting for transfers between devices, shards(): held = held + lax.ppermute(piece, ('x', 'y'), pairs).astype(F32)  22.4 us
    ppermute x4, starting transfers between devices, shards(): total = total + lax.ppermute(piece, ('l', 'h'), pairs).astype(F32)  10.2 us
    ppermute x4, waiting for transfers between devices, shards(): mirrored.append(lax.ppermute(piece, ('x', 'l', 'y', 'h', 'c'), pairs))  8.2 us
    ppermute x3, starting transfers between devices, shards(): held = held + lax.ppermute(piece, ('x', 'y'), pairs).astype(F32)  7.98 us
  transfers between devices with their start and end apart: 31, of which 13 were waited for; matrix products, arithmetic and copies ran while one was open for 4% of the time, Pallas kernels for 10%

profile of v1, /device:TPU:59, one launch (start us, length us, event | category | flops | bytes accessed | tf_op | source)
XLA Modules:
  0.0 201.4 jit_solution(14853890076083991720)
XLA Ops:
  1.3 0.8 add_convert_fusion.5
  2.2 2.7 %multiply_reduce_fusion = (f32[576]{0:T(1024)S(1)}, bf16[6,384,576]{1,2,0:T(8,128)(2,1)S(1)}) fusion(f32[6,384]{1,0:T(8,128)S(1)} %fusion.13, bf16[6,384,576]{1,2,0:T(8,128)(2,1)} %param.7, bf16[6]{0:T(256)(128)(2,1)S(1)} %convert_bitcast_fusion.1), kind=kLoop, calls=%fused_computation | loop fusion | flops 5307840 | bytes 5319948 | tf_op jit(solution)/shard_map/reduce_sum | solution.py:145
  5.0 1.3 collective-permute-start.10
  7.0 1.2 collective-permute-start.6
  8.3 0.9 collective-permute-start.2
  9.2 7.0 %collective-permute-done.10 = bf16[1,576,384]{2,1,0:T(8,128)(2,1)S(1)} collective-permute-done((bf16[1,576,384]{2,1,0:T(8,128)(2,1)S(1)}, bf16[1,576,384]{2,1,0:T(8,128)(2,1)S(1)}, u32[]{:S(2)}, u32[]{:S(2)}) %collective-permute-start.10) | collective-permute-done | bytes 442400 | tf_op jit(solution)/shard_map/ppermute | solution.py:20
  16.2 1.2 collective-permute-start.11
  17.4 8.4 %collective-permute-done.6 = bf16[1,576,384]{2,1,0:T(8,128)(2,1)} collective-permute-done((bf16[1,576,384]{2,1,0:T(8,128)(2,1)S(1)}, bf16[1,576,384]{2,1,0:T(8,128)(2,1)}, u32[]{:S(2)}, u32[]{:S(2)}) %collective-permute-start.6) | collective-permute-done | bytes 442400 | tf_op jit(solution)/shard_map/ppermute | solution.py:20
  25.7 9.5 %collective-permute-done.2 = bf16[1,576,384]{2,1,0:T(8,128)(2,1)} collective-permute-done((bf16[1,576,384]{2,1,0:T(8,128)(2,1)S(1)}, bf16[1,576,384]{2,1,0:T(8,128)(2,1)}, u32[]{:S(2)}, u32[]{:S(2)}) %collective-permute-start.2) | collective-permute-done | bytes 442400 | tf_op jit(solution)/shard_map/ppermute | solution.py:20
  35.2 1.5 collective-permute-start.5
  36.7 8.0 %collective-permute-done.11.refs_4_ = bf16[1,576,384]{2,1,0:T(8,128)(2,1)S(1)} collective-permute-done((bf16[1,576,384]{2,1,0:T(8,128)(2,1)S(1)}, bf16[1,576,384]{2,1,0:T(8,128)(2,1)S(1)}, u32[]{:S(2)}, u32[]{:S(2)}) %collective-permute-start.11) | collective-permute-done | bytes 442400 | tf_op jit(solution)/shard_map/ppermute | solution.py:20
  44.7 0.8 copy-done.2
  45.5 1.2 collective-permute-start.7
  46.7 0.9 copy-done
  47.9 0.9 fusion.15
  48.9 7.2 %collective-permute-done.7.refs_4_ = bf16[1,576,384]{2,1,0:T(8,128)(2,1)} collective-permute-done((bf16[1,576,384]{2,1,0:T(8,128)(2,1)}, bf16[1,576,384]{2,1,0:T(8,128)(2,1)}, u32[]{:S(2)}, u32[]{:S(2)}) %collective-permute-start.7) | collective-permute-done | bytes 442400 | tf_op jit(solution)/shard_map/ppermute | solution.py:20
  56.1 1.2 collective-permute-start.3
  57.3 1.2 copy-done.1
  58.5 1.0 copy-done.3
  59.5 7.9 %product.3.refs_6_ = f32[3,2,2,144,1152]{4,3,2,1,0:T(8,128)} custom-call(s32[2]{0:T(128)S(1)} %pad_add_fusion.refs_0_, bf16[2,576,384]{2,1,0:T(8,128)(2,1)S(1)} %get-tuple-element.14.refs_1_, bf16[2,576,384]{2,1,0:T(8,128)(2,1)S(1)} %collective-permute-done.8.refs_2_, bf16[2,576,384]{2,1,0:T(8,128)(2,1)S(1)} %copy-done.1, ...), custom_call_target="tpu_custom_call" | custom-call | flops 2548039680 | bytes 16777216 | tf_op jit(solution)/shard_map/product/pallas_call | solution.py:109
  67.4 11.3 %product.4.refs_6_ = f32[3,2,2,144,1152]{4,3,2,1,0:T(8,128)} custom-call(s32[2]{0:T(128)S(1)} %pad_add_fusion.refs_0_, bf16[2,576,384]{2,1,0:T(8,128)(2,1)S(1)} %get-tuple-element.15.refs_1_, bf16[2,576,384]{2,1,0:T(8,128)(2,1)} %collective-permute-done.4.refs_2_, bf16[2,576,384]{2,1,0:T(8,128)(2,1)} %collective-permute-done.5.refs_3_, ...), custom_call_target="tpu_custom_call" | custom-call | flops 2548039680 | bytes 16777216 | tf_op jit(solution)/shard_map/product/pallas_call | solution.py:109
  78.7 10.4 %product.5 = (bf16[3,2,144,1152]{3,2,1,0:T(8,128)(2,1)S(1)}, bf16[3,2,144,1152]{3,2,1,0:T(8,128)(2,1)}) custom-call(s32[2]{0:T(128)S(1)} %pad_add_fusion.refs_0_, bf16[2,576,384]{2,1,0:T(8,128)(2,1)S(1)} %get-tuple-element.16.refs_1_, bf16[2,576,384]{2,1,0:T(8,128)(2,1)} %collective-permute-done.refs_2_, ...), custom_call_target="tpu_custom_call" | custom-call | flops 2548039680 | bytes 16777216 | tf_op jit(solution)/shard_map/product/pallas_call | solution.py:109
  89.1 2.5 %collective-permute-start.12 = (bf16[3,2,144,1152]{3,2,1,0:T(8,128)(2,1)S(1)}, bf16[3,2,144,1152]{3,2,1,0:T(8,128)(2,1)}, u32[]{:S(2)}, u32[]{:S(2)}) collective-permute-start(bf16[3,2,144,1152]{3,2,1,0:T(8,128)(2,1)S(1)} %get-tuple-element.5), channel_id=1, source_target_pairs={{0,1},{1,0},{2,3},{3,2},{4,5},{5,4},{6,7},{7,6},{8,9},{9,8},{10,11... | collective-permute-start | bytes 5971976 | tf_op jit(solution)/shard_map/ppermute | solution.py:20
  91.7 3.8 %collective-permute-done.12 = bf16[3,2,144,1152]{3,2,1,0:T(8,128)(2,1)} collective-permute-done((bf16[3,2,144,1152]{3,2,1,0:T(8,128)(2,1)S(1)}, bf16[3,2,144,1152]{3,2,1,0:T(8,128)(2,1)}, u32[]{:S(2)}, u32[]{:S(2)}) %collective-permute-start.12) | collective-permute-done | bytes 1990688 | tf_op jit(solution)/shard_map/ppermute | solution.py:20
  95.4 3.4 %fusion.2 = (bf16[2,144,1152]{2,1,0:T(8,128)(2,1)}, bf16[2,144,1152]{2,1,0:T(8,128)(2,1)S(1)}, bf16[2,144,1152]{2,1,0:T(8,128)(2,1)S(1)}) fusion(bf16[3,2,144,1152]{3,2,1,0:T(8,128)(2,1)} %collective-permute-done.12, s32[]{:T(128)S(6)} %select_n.183, bf16[3,2,144,1152]{3,2,1,0:T(8,128)(2,1)} %get-tuple-element.4, s32[]{:T(128)S(6)} %select_n.187, ...), kind=kLoop, calls=%fused_computation.12 | loop fusion | flops 3981312 | bytes 5971980 | tf_op jit(solution)/shard_map/convert_element_type | solution.py:173
  98.8 1.3 collective-permute-start.13
  100.1 4.8 %collective-permute-start.14 = (bf16[2,144,1152]{2,1,0:T(8,128)(2,1)S(1)}, bf16[2,144,1152]{2,1,0:T(8,128)(2,1)S(1)}, u32[]{:S(2)}, u32[]{:S(2)}) collective-permute-start(bf16[2,144,1152]{2,1,0:T(8,128)(2,1)S(1)} %get-tuple-element.10), channel_id=1, source_target_pairs={{0,16},{16,0},{24,8},{64,80},{72,88},{88,72},{128,144},{136,152},{... | collective-permute-start | bytes 1990664 | tf_op jit(solution)/shard_map/ppermute | solution.py:174
  104.9 1.9 collective-permute-start.15
  106.8 1.0 collective-permute-start.24
  108.0 0.7 collective-permute-done.24
  108.7 3.0 %collective-permute-start.25 = (f32[576]{0:T(1024)S(1)}, f32[576]{0:T(1024)S(1)}, u32[]{:S(2)}, u32[]{:S(2)}) collective-permute-start(f32[576]{0:T(1024)S(1)} %add.236), channel_id=1, source_target_pairs={{0,8},{8,16},{16,24},{24,0},{1,9},{9,17},{17,25},{25,1},{2,10},{10... | collective-permute-start | bytes 6920 | tf_op jit(solution)/shard_map/ppermute | solution.py:20
  111.7 5.4 %collective-permute-done.13 = bf16[2,144,1152]{2,1,0:T(8,128)(2,1)S(1)} collective-permute-done((bf16[2,144,1152]{2,1,0:T(8,128)(2,1)}, bf16[2,144,1152]{2,1,0:T(8,128)(2,1)S(1)}, u32[]{:S(2)}, u32[]{:S(2)}) %collective-permute-start.13) | collective-permute-done | bytes 663584 | tf_op jit(solution)/shard_map/ppermute | solution.py:174
  117.6 2.1 %collective-permute-done.14 = bf16[2,144,1152]{2,1,0:T(8,128)(2,1)S(1)} collective-permute-done((bf16[2,144,1152]{2,1,0:T(8,128)(2,1)S(1)}, bf16[2,144,1152]{2,1,0:T(8,128)(2,1)S(1)}, u32[]{:S(2)}, u32[]{:S(2)}) %collective-permute-start.14) | collective-permute-done | bytes 663584 | tf_op jit(solution)/shard_map/ppermute | solution.py:174
  119.7 15.0 %collective-permute-done.15 = bf16[2,144,1152]{2,1,0:T(8,128)(2,1)S(1)} collective-permute-done((bf16[2,144,1152]{2,1,0:T(8,128)(2,1)S(1)}, bf16[2,144,1152]{2,1,0:T(8,128)(2,1)S(1)}, u32[]{:S(2)}, u32[]{:S(2)}) %collective-permute-start.15) | collective-permute-done | bytes 663584 | tf_op jit(solution)/shard_map/ppermute | solution.py:174
  134.7 1.8 fusion.1
  137.1 1.0 constant_dynamic-slice_fusion.7
  138.3 6.1 %collective-permute-start.17 = (bf16[144,576]{1,0:T(8,128)(2,1)S(1)}, bf16[144,576]{1,0:T(8,128)(2,1)S(1)}, u32[]{:S(2)}, u32[]{:S(2)}) collective-permute-start(bf16[144,576]{1,0:T(8,128)(2,1)S(1)} %fusion.10), channel_id=1, source_target_pairs={{0,32},{2,0},{4,34},{6,2},{32,36},{34,4},{36,38},{38,6},{1,33},{3,... | collective-permute-start | bytes 497672 | tf_op jit(solution)/shard_map/ppermute | solution.py:188
  144.7 1.9 collective-permute-start.16
  146.7 2.1 %collective-permute-start.19 = (bf16[144,576]{1,0:T(8,128)(2,1)S(1)}, bf16[144,576]{1,0:T(8,128)(2,1)S(1)}, u32[]{:S(2)}, u32[]{:S(2)}) collective-permute-start(bf16[144,576]{1,0:T(8,128)(2,1)S(1)} %fusion.12), channel_id=1, source_target_pairs={{0,34},{2,2},{4,32},{6,0},{32,38},{34,6},{36,36},{38,4},{1,35},{3,... | collective-permute-start | bytes 497672 | tf_op jit(solution)/shard_map/ppermute | solution.py:188
  148.8 6.2 %collective-permute-start.28 = (f32[576]{0:T(1024)S(1)}, f32[576]{0:T(1024)S(1)}, u32[]{:S(2)}, u32[]{:S(2)}) collective-permute-start(f32[576]{0:T(1024)S(1)} %add_add_fusion), channel_id=1, source_target_pairs={{0,2},{2,4},{4,6},{6,0},{1,3},{3,5},{5,7},{7,1},{8,10},{10,12},{12... | collective-permute-start | bytes 6920 | tf_op jit(solution)/shard_map/ppermute | solution.py:20
  155.0 2.5 %collective-permute-start.29 = (f32[576]{0:T(1024)S(1)}, f32[576]{0:T(1024)S(1)}, u32[]{:S(2)}, u32[]{:S(2)}) collective-permute-start(f32[576]{0:T(1024)S(1)} %add_add_fusion), channel_id=1, source_target_pairs={{0,4},{2,6},{4,0},{6,2},{1,5},{3,7},{5,1},{7,3},{8,12},{10,14},{12... | collective-permute-start | bytes 6920 | tf_op jit(solution)/shard_map/ppermute | solution.py:20
  157.5 2.9 %collective-permute-done.18 = bf16[144,576]{1,0:T(8,128)(2,1)S(1)} collective-permute-done((bf16[144,576]{1,0:T(8,128)(2,1)S(1)}, bf16[144,576]{1,0:T(8,128)(2,1)S(1)}, u32[]{:S(2)}, u32[]{:S(2)}) %collective-permute-start.18) | collective-permute-done | bytes 165920 | tf_op jit(solution)/shard_map/ppermute | solution.py:188
  161.5 11.5 %collective-permute-start.20 = (bf16[144,144]{1,0:T(8,128)(2,1)S(1)}, bf16[144,144]{1,0:T(8,128)(2,1)S(1)}, u32[]{:S(2)}, u32[]{:S(2)}) collective-permute-start(bf16[144,144]{1,0:T(8,128)(2,1)S(1)} %bitcast.79), channel_id=1, source_target_pairs={{8,64},{9,65},{10,66},{11,67},{12,96},{13,97},{14,98},{15,99},{40,... | collective-permute-start | bytes 124424 | tf_op jit(solution)/shard_map/ppermute | solution.py:210
  173.1 4.9 %collective-permute-start.21 = (bf16[144,144]{1,0:T(8,128)(2,1)S(1)}, bf16[144,144]{1,0:T(8,128)(2,1)S(1)}, u32[]{:S(2)}, u32[]{:S(2)}) collective-permute-start(bf16[144,144]{1,0:T(8,128)(2,1)S(1)} %bitcast.80), channel_id=1, source_target_pairs={{8,65},{9,64},{10,67},{11,66},{12,97},{13,96},{14,99},{15,98},{40,... | collective-permute-start | bytes 124424 | tf_op jit(solution)/shard_map/ppermute | solution.py:210
  178.3 7.4 %collective-permute-start.22 = (bf16[144,144]{1,0:T(8,128)(2,1)S(1)}, bf16[144,144]{1,0:T(8,128)(2,1)S(1)}, u32[]{:S(2)}, u32[]{:S(2)}) collective-permute-start(bf16[144,144]{1,0:T(8,128)(2,1)S(1)} %bitcast.82), channel_id=1, source_target_pairs={{8,66},{9,67},{10,64},{11,65},{12,98},{13,99},{14,96},{15,97},{40,... | collective-permute-start | bytes 124424 | tf_op jit(solution)/shard_map/ppermute | solution.py:210
  185.8 4.7 %collective-permute-start.23 = (bf16[144,144]{1,0:T(8,128)(2,1)S(1)}, bf16[144,144]{1,0:T(8,128)(2,1)S(1)}, u32[]{:S(2)}, u32[]{:S(2)}) collective-permute-start(bf16[144,144]{1,0:T(8,128)(2,1)S(1)} %bitcast.81), channel_id=1, source_target_pairs={{8,67},{9,66},{10,65},{11,64},{12,99},{13,98},{14,97},{15,96},{40,... | collective-permute-start | bytes 124424 | tf_op jit(solution)/shard_map/ppermute | solution.py:210
  191.3 8.0 %collective-permute-done.23 = bf16[144,144]{1,0:T(8,128)(2,1)S(1)} collective-permute-done((bf16[144,144]{1,0:T(8,128)(2,1)S(1)}, bf16[144,144]{1,0:T(8,128)(2,1)S(1)}, u32[]{:S(2)}, u32[]{:S(2)}) %collective-permute-start.23) | collective-permute-done | bytes 41504 | tf_op jit(solution)/shard_map/ppermute | solution.py:210
  199.4 2.0 %add_subtract_fusion = f32[144,576]{1,0:T(8,128)} fusion(f32[576,576]{1,0:T(8,128)} %param.10, s32[]{:T(128)S(6)} %select_n.170, f32[144]{0:T(256)S(1)} %dynamic-slice.12, bf16[144,144]{1,0:T(8,128)(2,1)S(1)} %get-tuple-element.22, bf16[144,144]{1,0:T(8,128)(2,1)S(1)} %get-tuple-element.23, bf16[144,144]{1,0:T(8,128)(2,1)S(1)} %get-tuple-element.24, ...), kind=kLoop, calls=%fused_computation.27 | loop fusion | flops 1907712 | bytes 1495104 | tf_op jit(solution)/shard_map/sub | solution.py:221
  (67 shorter events, 6.1 us)
Async XLA Ops:
  5.0 11.1 %collective-permute-start.10 = (bf16[1,576,384]{2,1,0:T(8,128)(2,1)S(1)}, bf16[1,576,384]{2,1,0:T(8,128)(2,1)S(1)}, u32[]{:S(2)}, u32[]{:S(2)}) collective-permute-start(bf16[1,576,384]{2,1,0:T(8,128)(2,1)S(1)} %get-tuple-element.11), channel_id=1, source_target_pairs={{0,64},{64,128},{128,192},{192,0},{1,65},{65,129},{129,193},{193,1... | collective-permute-start | bytes 1327112 | tf_op jit(solution)/shard_map/ppermute | solution.py:20
  6.6 40.1 %collective-permute-start.8 = (bf16[2,576,384]{2,1,0:T(8,128)(2,1)S(1)}, bf16[2,576,384]{2,1,0:T(8,128)(2,1)S(1)}, u32[]{:S(2)}, u32[]{:S(2)}) collective-permute-start(bf16[2,576,384]{2,1,0:T(8,128)(2,1)S(1)} %get-tuple-element.14.refs_1_), channel_id=1, source_target_pairs={{0,32},{32,0},{1,33},{33,1},{2,34},{34,2},{3,35},{35,3},{4,36},{36... | collective-permute-start | bytes 2654216 | tf_op jit(solution)/shard_map/ppermute | solution.py:20
  6.7 40.0 %collective-permute-start.9 = (bf16[2,576,384]{2,1,0:T(8,128)(2,1)S(1)}, bf16[2,576,384]{2,1,0:T(8,128)(2,1)S(1)}, u32[]{:S(2)}, u32[]{:S(2)}) collective-permute-start(bf16[2,576,384]{2,1,0:T(8,128)(2,1)S(1)} %get-tuple-element.14.refs_1_), channel_id=1, source_target_pairs={{0,192},{64,0},{128,64},{192,128},{1,193},{65,1},{129,65},{193,129... | collective-permute-start | bytes 2654216 | tf_op jit(solution)/shard_map/ppermute | solution.py:20
  7.0 18.7 %collective-permute-start.6 = (bf16[1,576,384]{2,1,0:T(8,128)(2,1)S(1)}, bf16[1,576,384]{2,1,0:T(8,128)(2,1)}, u32[]{:S(2)}, u32[]{:S(2)}) collective-permute-start(bf16[1,576,384]{2,1,0:T(8,128)(2,1)S(1)} %get-tuple-element.12), channel_id=1, source_target_pairs={{0,64},{64,128},{128,192},{192,0},{1,65},{65,129},{129,193},{193,1... | collective-permute-start | bytes 1327112 | tf_op jit(solution)/shard_map/ppermute | solution.py:20
  8.3 27.0 %collective-permute-start.2 = (bf16[1,576,384]{2,1,0:T(8,128)(2,1)S(1)}, bf16[1,576,384]{2,1,0:T(8,128)(2,1)}, u32[]{:S(2)}, u32[]{:S(2)}) collective-permute-start(bf16[1,576,384]{2,1,0:T(8,128)(2,1)S(1)} %get-tuple-element.13), channel_id=1, source_target_pairs={{0,64},{64,128},{128,192},{192,0},{1,65},{65,129},{129,193},{193,1... | collective-permute-start | bytes 1327112 | tf_op jit(solution)/shard_map/ppermute | solution.py:20
  16.2 28.5 %collective-permute-start.11 = (bf16[1,576,384]{2,1,0:T(8,128)(2,1)S(1)}, bf16[1,576,384]{2,1,0:T(8,128)(2,1)S(1)}, u32[]{:S(2)}, u32[]{:S(2)}) collective-permute-start(bf16[1,576,384]{2,1,0:T(8,128)(2,1)S(1)} %collective-permute-done.10), channel_id=1, source_target_pairs={{0,64},{64,128},{128,192},{192,0},{1,65},{65,129},{129,193},{193,1... | collective-permute-start | bytes 1327112 | tf_op jit(solution)/shard_map/ppermute | solution.py:20
  25.7 41.7 %collective-permute-start.4 = (bf16[2,576,384]{2,1,0:T(8,128)(2,1)S(1)}, bf16[2,576,384]{2,1,0:T(8,128)(2,1)}, u32[]{:S(2)}, u32[]{:S(2)}) collective-permute-start(bf16[2,576,384]{2,1,0:T(8,128)(2,1)S(1)} %get-tuple-element.15.refs_1_), channel_id=1, source_target_pairs={{0,32},{32,0},{1,33},{33,1},{2,34},{34,2},{3,35},{35,3},{4,36},{36... | collective-permute-start | bytes 2654216 | tf_op jit(solution)/shard_map/ppermute | solution.py:20
  35.2 32.2 %collective-permute-start.5 = (bf16[2,576,384]{2,1,0:T(8,128)(2,1)S(1)}, bf16[2,576,384]{2,1,0:T(8,128)(2,1)}, u32[]{:S(2)}, u32[]{:S(2)}) collective-permute-start(bf16[2,576,384]{2,1,0:T(8,128)(2,1)S(1)} %get-tuple-element.15.refs_1_), channel_id=1, source_target_pairs={{0,192},{64,0},{128,64},{192,128},{1,193},{65,1},{129,65},{193,129... | collective-permute-start | bytes 2654216 | tf_op jit(solution)/shard_map/ppermute | solution.py:20
  44.7 0.8 copy-start.2
  45.5 10.6 %collective-permute-start.7 = (bf16[1,576,384]{2,1,0:T(8,128)(2,1)}, bf16[1,576,384]{2,1,0:T(8,128)(2,1)}, u32[]{:S(2)}, u32[]{:S(2)}) collective-permute-start(bf16[1,576,384]{2,1,0:T(8,128)(2,1)} %collective-permute-done.6), channel_id=1, source_target_pairs={{0,64},{64,128},{128,192},{192,0},{1,65},{65,129},{129,193},{193,1... | collective-permute-start | bytes 1327112 | tf_op jit(solution)/shard_map/ppermute | solution.py:20
  46.7 32.0 %collective-permute-start = (bf16[2,576,384]{2,1,0:T(8,128)(2,1)S(1)}, bf16[2,576,384]{2,1,0:T(8,128)(2,1)}, u32[]{:S(2)}, u32[]{:S(2)}) collective-permute-start(bf16[2,576,384]{2,1,0:T(8,128)(2,1)S(1)} %get-tuple-element.16.refs_1_), channel_id=1, source_target_pairs={{0,32},{32,0},{1,33},{33,1},{2,34},{34,2},{3,35},{35,3},{4,36},{36... | collective-permute-start | bytes 2654216 | tf_op jit(solution)/shard_map/ppermute | solution.py:20
  46.7 0.9 copy-start
  47.6 31.1 %collective-permute-start.1 = (bf16[2,576,384]{2,1,0:T(8,128)(2,1)S(1)}, bf16[2,576,384]{2,1,0:T(8,128)(2,1)}, u32[]{:S(2)}, u32[]{:S(2)}) collective-permute-start(bf16[2,576,384]{2,1,0:T(8,128)(2,1)S(1)} %get-tuple-element.16.refs_1_), channel_id=1, source_target_pairs={{0,192},{64,0},{128,64},{192,128},{1,193},{65,1},{129,65},{193,129... | collective-permute-start | bytes 2654216 | tf_op jit(solution)/shard_map/ppermute | solution.py:20
  56.1 22.6 %collective-permute-start.3 = (bf16[1,576,384]{2,1,0:T(8,128)(2,1)}, bf16[1,576,384]{2,1,0:T(8,128)(2,1)S(1)}, u32[]{:S(2)}, u32[]{:S(2)}) collective-permute-start(bf16[1,576,384]{2,1,0:T(8,128)(2,1)} %collective-permute-done.2), channel_id=1, source_target_pairs={{0,64},{64,128},{128,192},{192,0},{1,65},{65,129},{129,193},{193,1... | collective-permute-start | bytes 1327112 | tf_op jit(solution)/shard_map/ppermute | solution.py:20
  57.3 1.2 copy-start.1
  58.5 1.0 copy-start.3
  89.1 6.3 %collective-permute-start.12 = (bf16[3,2,144,1152]{3,2,1,0:T(8,128)(2,1)S(1)}, bf16[3,2,144,1152]{3,2,1,0:T(8,128)(2,1)}, u32[]{:S(2)}, u32[]{:S(2)}) collective-permute-start(bf16[3,2,144,1152]{3,2,1,0:T(8,128)(2,1)S(1)} %get-tuple-element.5), channel_id=1, source_target_pairs={{0,1},{1,0},{2,3},{3,2},{4,5},{5,4},{6,7},{7,6},{8,9},{9,8},{10,11... | collective-permute-start | bytes 5971976 | tf_op jit(solution)/shard_map/ppermute | solution.py:20
  95.4 12.4 %copy-start.4 = (s32[576]{0:T(1024)S(1)}, s32[576]{0:T(1024)}, u32[]{:S(2)}) copy-start(s32[576]{0:T(1024)} %param.11) | copy-start | bytes 6916
  98.8 18.2 %collective-permute-start.13 = (bf16[2,144,1152]{2,1,0:T(8,128)(2,1)}, bf16[2,144,1152]{2,1,0:T(8,128)(2,1)S(1)}, u32[]{:S(2)}, u32[]{:S(2)}) collective-permute-start(bf16[2,144,1152]{2,1,0:T(8,128)(2,1)} %get-tuple-element.8), channel_id=1, source_target_pairs={{0,8},{8,16},{24,0},{64,72},{72,80},{80,88},{136,144},{144,152},{1... | collective-permute-start | bytes 1990664 | tf_op jit(solution)/shard_map/ppermute | solution.py:174
  100.1 19.5 %collective-permute-start.14 = (bf16[2,144,1152]{2,1,0:T(8,128)(2,1)S(1)}, bf16[2,144,1152]{2,1,0:T(8,128)(2,1)S(1)}, u32[]{:S(2)}, u32[]{:S(2)}) collective-permute-start(bf16[2,144,1152]{2,1,0:T(8,128)(2,1)S(1)} %get-tuple-element.10), channel_id=1, source_target_pairs={{0,16},{16,0},{24,8},{64,80},{72,88},{88,72},{128,144},{136,152},{... | collective-permute-start | bytes 1990664 | tf_op jit(solution)/shard_map/ppermute | solution.py:174
  104.9 29.8 %collective-permute-start.15 = (bf16[2,144,1152]{2,1,0:T(8,128)(2,1)S(1)}, bf16[2,144,1152]{2,1,0:T(8,128)(2,1)S(1)}, u32[]{:S(2)}, u32[]{:S(2)}) collective-permute-start(bf16[2,144,1152]{2,1,0:T(8,128)(2,1)S(1)} %get-tuple-element.9), channel_id=1, source_target_pairs={{8,0},{16,8},{24,16},{64,88},{80,72},{88,80},{128,152},{136,128},{... | collective-permute-start | bytes 1990664 | tf_op jit(solution)/shard_map/ppermute | solution.py:174
  106.8 1.8 collective-permute-start.24
  108.7 36.0 %collective-permute-start.25 = (f32[576]{0:T(1024)S(1)}, f32[576]{0:T(1024)S(1)}, u32[]{:S(2)}, u32[]{:S(2)}) collective-permute-start(f32[576]{0:T(1024)S(1)} %add.236), channel_id=1, source_target_pairs={{0,8},{8,16},{16,24},{24,0},{1,9},{9,17},{17,25},{25,1},{2,10},{10... | collective-permute-start | bytes 6920 | tf_op jit(solution)/shard_map/ppermute | solution.py:20
  111.7 35.0 %collective-permute-start.26 = (f32[576]{0:T(1024)S(1)}, f32[576]{0:T(1024)S(1)}, u32[]{:S(2)}, u32[]{:S(2)}) collective-permute-start(f32[576]{0:T(1024)S(1)} %add.236), channel_id=1, source_target_pairs={{0,16},{8,24},{16,0},{24,8},{1,17},{9,25},{17,1},{25,9},{2,18},{10... | collective-permute-start | bytes 6920 | tf_op jit(solution)/shard_map/ppermute | solution.py:20
  117.0 31.7 %collective-permute-start.27 = (f32[576]{0:T(1024)S(1)}, f32[576]{0:T(1024)S(1)}, u32[]{:S(2)}, u32[]{:S(2)}) collective-permute-start(f32[576]{0:T(1024)S(1)} %add.236), channel_id=1, source_target_pairs={{0,24},{8,0},{16,8},{24,16},{1,25},{9,1},{17,9},{25,17},{2,26},{10... | collective-permute-start | bytes 6920 | tf_op jit(solution)/shard_map/ppermute | solution.py:20
  138.3 16.8 %collective-permute-start.17 = (bf16[144,576]{1,0:T(8,128)(2,1)S(1)}, bf16[144,576]{1,0:T(8,128)(2,1)S(1)}, u32[]{:S(2)}, u32[]{:S(2)}) collective-permute-start(bf16[144,576]{1,0:T(8,128)(2,1)S(1)} %fusion.10), channel_id=1, source_target_pairs={{0,32},{2,0},{4,34},{6,2},{32,36},{34,4},{36,38},{38,6},{1,33},{3,... | collective-permute-start | bytes 497672 | tf_op jit(solution)/shard_map/ppermute | solution.py:188
  144.4 16.0 %collective-permute-start.18 = (bf16[144,576]{1,0:T(8,128)(2,1)S(1)}, bf16[144,576]{1,0:T(8,128)(2,1)S(1)}, u32[]{:S(2)}, u32[]{:S(2)}) collective-permute-start(bf16[144,576]{1,0:T(8,128)(2,1)S(1)} %fusion.11), channel_id=1, source_target_pairs={{0,2},{2,34},{4,0},{6,32},{32,6},{34,38},{36,4},{38,36},{1,3},{3,3... | collective-permute-start | bytes 497672 | tf_op jit(solution)/shard_map/ppermute | solution.py:188
  144.7 15.7 %collective-permute-start.16 = (bf16[144,576]{1,0:T(8,128)(2,1)S(1)}, bf16[144,576]{1,0:T(8,128)(2,1)S(1)}, u32[]{:S(2)}, u32[]{:S(2)}) collective-permute-start(bf16[144,576]{1,0:T(8,128)(2,1)S(1)} %fusion.9), channel_id=1, source_target_pairs={{0,0},{2,32},{4,2},{6,34},{32,4},{34,36},{36,6},{38,38},{1,1},{3,3... | collective-permute-start | bytes 497672 | tf_op jit(solution)/shard_map/ppermute | solution.py:188
  146.7 13.7 %collective-permute-start.19 = (bf16[144,576]{1,0:T(8,128)(2,1)S(1)}, bf16[144,576]{1,0:T(8,128)(2,1)S(1)}, u32[]{:S(2)}, u32[]{:S(2)}) collective-permute-start(bf16[144,576]{1,0:T(8,128)(2,1)S(1)} %fusion.12), channel_id=1, source_target_pairs={{0,34},{2,2},{4,32},{6,0},{32,38},{34,6},{36,36},{38,4},{1,35},{3,... | collective-permute-start | bytes 497672 | tf_op jit(solution)/shard_map/ppermute | solution.py:188
  148.8 29.5 %collective-permute-start.28 = (f32[576]{0:T(1024)S(1)}, f32[576]{0:T(1024)S(1)}, u32[]{:S(2)}, u32[]{:S(2)}) collective-permute-start(f32[576]{0:T(1024)S(1)} %add_add_fusion), channel_id=1, source_target_pairs={{0,2},{2,4},{4,6},{6,0},{1,3},{3,5},{5,7},{7,1},{8,10},{10,12},{12... | collective-permute-start | bytes 6920 | tf_op jit(solution)/shard_map/ppermute | solution.py:20
  155.0 30.7 %collective-permute-start.29 = (f32[576]{0:T(1024)S(1)}, f32[576]{0:T(1024)S(1)}, u32[]{:S(2)}, u32[]{:S(2)}) collective-permute-start(f32[576]{0:T(1024)S(1)} %add_add_fusion), channel_id=1, source_target_pairs={{0,4},{2,6},{4,0},{6,2},{1,5},{3,7},{5,1},{7,3},{8,12},{10,14},{12... | collective-permute-start | bytes 6920 | tf_op jit(solution)/shard_map/ppermute | solution.py:20
  160.4 30.0 %collective-permute-start.30 = (f32[576]{0:T(1024)S(1)}, f32[576]{0:T(1024)S(1)}, u32[]{:S(2)}, u32[]{:S(2)}) collective-permute-start(f32[576]{0:T(1024)S(1)} %add_add_fusion), channel_id=1, source_target_pairs={{0,6},{2,0},{4,2},{6,4},{1,7},{3,1},{5,3},{7,5},{8,14},{10,8},{12,... | collective-permute-start | bytes 6920 | tf_op jit(solution)/shard_map/ppermute | solution.py:20
  160.5 29.9 %copy-start.5 = (f32[576]{0:T(1024)S(1)}, f32[576]{0:T(1024)}, u32[]{:S(2)}) copy-start(f32[576]{0:T(1024)} %param.12) | copy-start | bytes 6916
  161.5 29.5 %collective-permute-start.20 = (bf16[144,144]{1,0:T(8,128)(2,1)S(1)}, bf16[144,144]{1,0:T(8,128)(2,1)S(1)}, u32[]{:S(2)}, u32[]{:S(2)}) collective-permute-start(bf16[144,144]{1,0:T(8,128)(2,1)S(1)} %bitcast.79), channel_id=1, source_target_pairs={{8,64},{9,65},{10,66},{11,67},{12,96},{13,97},{14,98},{15,99},{40,... | collective-permute-start | bytes 124424 | tf_op jit(solution)/shard_map/ppermute | solution.py:210
  173.1 17.9 %collective-permute-start.21 = (bf16[144,144]{1,0:T(8,128)(2,1)S(1)}, bf16[144,144]{1,0:T(8,128)(2,1)S(1)}, u32[]{:S(2)}, u32[]{:S(2)}) collective-permute-start(bf16[144,144]{1,0:T(8,128)(2,1)S(1)} %bitcast.80), channel_id=1, source_target_pairs={{8,65},{9,64},{10,67},{11,66},{12,97},{13,96},{14,99},{15,98},{40,... | collective-permute-start | bytes 124424 | tf_op jit(solution)/shard_map/ppermute | solution.py:210
  178.3 13.0 %collective-permute-start.22 = (bf16[144,144]{1,0:T(8,128)(2,1)S(1)}, bf16[144,144]{1,0:T(8,128)(2,1)S(1)}, u32[]{:S(2)}, u32[]{:S(2)}) collective-permute-start(bf16[144,144]{1,0:T(8,128)(2,1)S(1)} %bitcast.82), channel_id=1, source_target_pairs={{8,66},{9,67},{10,64},{11,65},{12,98},{13,99},{14,96},{15,97},{40,... | collective-permute-start | bytes 124424 | tf_op jit(solution)/shard_map/ppermute | solution.py:210
  185.8 13.5 %collective-permute-start.23 = (bf16[144,144]{1,0:T(8,128)(2,1)S(1)}, bf16[144,144]{1,0:T(8,128)(2,1)S(1)}, u32[]{:S(2)}, u32[]{:S(2)}) collective-permute-start(bf16[144,144]{1,0:T(8,128)(2,1)S(1)} %bitcast.81), channel_id=1, source_target_pairs={{8,67},{9,66},{10,65},{11,64},{12,99},{13,98},{14,97},{15,96},{40,... | collective-permute-start | bytes 124424 | tf_op jit(solution)/shard_map/ppermute | solution.py:210

commit v2 on v1

v2 whole, which is shorter than its diff:
```python
import functools

import jax
import jax.numpy as jnp
from jax import lax
from jax.experimental import pallas as pl
from jax.experimental.pallas import tpu as pltpu
from jax.sharding import Mesh
from jax.sharding import PartitionSpec as P

X, L, Y, H, C = 4, 2, 4, 4, 2
BLK = ("x", "l")
PAIR = ("y", "h", "c")
CHUNKS = (4, 2)
F32 = jnp.float32
BF16 = jnp.bfloat16


def rotate(array, axis, size, step):
    return lax.ppermute(array, axis, [(i, (i + step) % size) for i in range(size)])


def small_call(kernel, out_shape, scalars, operands, scratch=()):
    vmem = pl.BlockSpec(memory_space=pltpu.VMEM)
    smem = pl.BlockSpec(memory_space=pltpu.SMEM)
    return pl.pallas_call(
        kernel,
        out_shape=out_shape,
        in_specs=[smem] + [vmem] * len(operands),
        out_specs=jax.tree.map(lambda _: vmem, out_shape),
        scratch_shapes=list(scratch),
        compiler_params=pltpu.CompilerParams(vmem_limit_bytes=24 * 2**20),
        cost_estimate=pl.CostEstimate(flops=10**6, bytes_accessed=2**22, transcendentals=0),
    )(jnp.stack(scalars).astype(jnp.int32), *operands)


def pieces_kernel(which_ref, own_ref, a_ref, b_ref, c_ref, *rest):
    outs, cut_ref = rest[:4], rest[4]
    width = own_ref.shape[2] // 2
    half = width // 2
    for i in range(2):
        total = own_ref[i].astype(F32) + a_ref[i].astype(F32)
        total = total + b_ref[i].astype(F32) + c_ref[i].astype(F32)
        for n in range(4):
            cut_ref[n, :, i * half : (i + 1) * half] = total[:, n * half : (n + 1) * half]
    for m in range(4):
        outs[m][...] = cut_ref[which_ref[m]].astype(BF16)


def turn_kernel(which_ref, *refs):
    ins, (kept_ref, swap_ref, turned_keep_ref, turned_send_ref, turned_ref) = refs[:4], refs[4:]
    quarter, width = ins[0].shape
    half = width // 2
    odd, core = which_ref[0] == 1, which_ref[1]
    wide = ins[0][...].astype(F32) + ins[1][...].astype(F32)
    wide = wide + ins[2][...].astype(F32) + ins[3][...].astype(F32)
    low, high = wide[:, :half], wide[:, half:]
    kept_ref[...] = jnp.where(odd, high, low)
    swap_ref[...] = jnp.where(odd, low, high).astype(BF16)
    shape = (width, width)
    same = lax.broadcasted_iota(jnp.int32, shape, 0) == lax.broadcasted_iota(jnp.int32, shape, 1)
    turned = lax.dot_general(
        same.astype(F32).astype(BF16),
        wide.astype(BF16),
        (((1,), (1,)), ((), ())),
        preferred_element_type=F32,
    )
    turned_ref[...] = turned.reshape(4, quarter, quarter)
    for i in range(2):
        turned_keep_ref[i] = turned_ref[2 * i + core].astype(BF16)
        turned_send_ref[i] = turned_ref[2 * i + 1 - core].astype(BF16)


def last_kernel(which_ref, base_ref, kept_ref, swapped_ref, mirror_ref, out_ref):
    quarter = mirror_ref.shape[2]
    odd = which_ref[0]
    for n in range(4):
        columns = slice((n % 2) * quarter, (n % 2 + 1) * quarter)
        total = jnp.where(
            odd == n // 2, kept_ref[:, columns], swapped_ref[:, columns].astype(F32)
        )
        to = slice(n * quarter, (n + 1) * quarter)
        at = jnp.where(which_ref[1] == n % 2, n // 2, 2 + n // 2)
        out_ref[:, to] = base_ref[:, to] - (total + mirror_ref[at].astype(F32))


def rotate_pairs(array):
    return lax.ppermute(array, "h", [(i, i ^ 1) for i in range(H)])


def apply_inverse(inverse, shaped):
    parts = []
    for row in range(3):
        total = inverse[:, row * 3] * shaped[:, 0]
        total = total + inverse[:, row * 3 + 1] * shaped[:, 1]
        total = total + inverse[:, row * 3 + 2] * shaped[:, 2]
        parts.append(total)
    return jnp.stack(parts, axis=1)


def product_kernel(first, last, at, *refs):
    where_ref, seen_ref, own_ref, mate_ref, next_ref, far_ref, inv_ref = refs[:7]
    refs = refs[7:]
    if not first:
        before_ref, refs = refs[0], refs[1:]
    if last:
        send_ref, keep_ref, left_ref, scaled_ref, sums_ref = refs
    else:
        sums_ref, left_ref, scaled_ref = refs
    blocks, width, rows = own_ref.shape
    points = inv_ref.shape[2]
    fars = far_ref.shape[0]
    core, upper = where_ref[0], where_ref[1]
    for block in range(blocks):
        for side, ref in enumerate((own_ref, mate_ref)):
            seen = seen_ref[side, at + block].astype(F32)
            parts = [
                ref[block, :, c * points : (c + 1) * points].astype(F32) for c in range(3)
            ]
            for a in range(3):
                total = (inv_ref[block, 3 * a : 3 * a + 1, :] * seen) * parts[0]
                total = total + (inv_ref[block, 3 * a + 1 : 3 * a + 2, :] * seen) * parts[1]
                total = total + (inv_ref[block, 3 * a + 2 : 3 * a + 3, :] * seen) * parts[2]
                to = block * rows + a * points
                scaled_ref[side * width : (side + 1) * width, to : to + points] = (
                    total.astype(BF16)
                )
        columns = slice(block * rows, (block + 1) * rows)
        for kind, ref in enumerate((own_ref, next_ref)):
            seen = seen_ref[2 * kind, at + block].astype(F32).astype(BF16)
            left_ref[kind, :, columns] = ref[block] * seen
    for block in range(fars):
        columns = slice(block * rows, (block + 1) * rows)
        seen = seen_ref[3, at + upper * fars + block].astype(F32).astype(BF16)
        left_ref[2, :, columns] = far_ref[block] * seen
    half_start = pl.multiple_of(upper * (fars * rows), rows)
    for start in range(0, 2 * width, 256):
        stop = min(start + 256, 2 * width)
        columns = slice(start, stop)
        for kind in range(3):
            if kind < 2:
                left = left_ref[kind]
                right = scaled_ref[columns, :]
            else:
                left = left_ref[kind, :, : fars * rows]
                right = scaled_ref[columns, pl.ds(half_start, fars * rows)]
            term = lax.dot_general(
                left, right, (((1,), (1,)), ((), ())), preferred_element_type=F32
            ).reshape(2, 2, width // 4, stop - start)
            if not first:
                term = term + before_ref[kind, :, :, :, columns]
            sums_ref[kind, :, :, :, columns] = term
            if last:
                for i in range(2):
                    send_ref[kind, i, :, columns] = sums_ref[
                        kind, i, 1 - core, :, columns
                    ].astype(BF16)
                    keep_ref[kind, i, :, columns] = sums_ref[
                        kind, i, core, :, columns
                    ].astype(BF16)


def product(first, last, at, where, seen, own, mate, following, far, inverse, before=None):
    blocks, width, rows = own.shape
    sums = (3, 2, 2, width // 4, 2 * width)
    half = (3, 2, width // 4, 2 * width)
    vmem = pl.BlockSpec(memory_space=pltpu.VMEM)
    smem = pl.BlockSpec(memory_space=pltpu.SMEM)
    scratch = [
        pltpu.VMEM((3, width, blocks * rows), BF16),
        pltpu.VMEM((2 * width, blocks * rows), BF16),
    ]
    if last:
        out_shape = (jax.ShapeDtypeStruct(half, BF16), jax.ShapeDtypeStruct(half, BF16))
        out_specs = (vmem, vmem)
        scratch.append(pltpu.VMEM(sums, F32))
    else:
        out_shape = jax.ShapeDtypeStruct(sums, F32)
        out_specs = vmem
    operands = [where, seen, own, mate, following, far, inverse]
    specs = [smem, smem] + [vmem] * 5
    if not first:
        operands.append(before)
        specs.append(vmem)
    flops = 2 * width * 2 * width * rows * (2 * blocks + far.shape[0])
    return pl.pallas_call(
        functools.partial(product_kernel, first, last, at),
        out_shape=out_shape,
        in_specs=specs,
        out_specs=out_specs,
        scratch_shapes=scratch,
        compiler_params=pltpu.CompilerParams(vmem_limit_bytes=34 * 2**20),
        cost_estimate=pl.CostEstimate(
            flops=flops, bytes_accessed=16 * 2**20, transcendentals=0
        ),
        name="product",
    )(*operands)


def shards(panels, pattern, point_inverse, camera_hessian, damping, camera_grad, point_grad):
    count = panels.shape[0]
    width = panels.shape[2]
    points = point_inverse.shape[2]
    x, l = lax.axis_index("x"), lax.axis_index("l")
    y, h, c = lax.axis_index("y"), lax.axis_index("h"), lax.axis_index("c")
    upper = x // 2
    raw = jnp.transpose(panels, (0, 2, 1))

    chunks = []
    start = 0
    for size in CHUNKS:
        own = raw[start : start + size]
        half = size // 2
        sent = lax.dynamic_slice_in_dim(raw, start + (1 - upper) * half, half, 0)
        far = rotate(sent, "x", X, 1)
        mate = rotate(own, "l", L, 1)
        following = rotate(own, "x", X, -1)
        chunks.append([start, own, mate, following, far, point_inverse[start : start + size]])
        start += size
    for chunk in chunks:
        chunk[4] = rotate(chunk[4], "x", X, 1)
    seen = pattern[:, 0]
    seen = jnp.stack(
        [seen, rotate(seen, "l", L, 1), rotate(seen, "x", X, -1), rotate(seen, "x", X, 2)]
    )

    grads = point_grad.reshape(count, 3, points)
    step = apply_inverse(point_inverse, grads).astype(BF16).astype(F32)
    step = step.reshape(count, 1, 3 * points)
    masked = raw * pattern.astype(BF16)[:, :, None]
    terms = jnp.sum(masked.astype(F32) * step, axis=(0, 2))
    terms = terms + rotate(terms, "c", C, 1)
    terms = terms + sum(rotate(terms, "y", Y, k) for k in range(1, Y))
    terms, seen = lax.optimization_barrier((terms, seen))

    where = jnp.stack([c, upper]).astype(jnp.int32)
    sums = None
    for n, chunk in enumerate(chunks):
        sums = product(
            n == 0, n == len(CHUNKS) - 1, chunk[0], where, seen, *chunk[1:], before=sums
        )
    send, keep = sums
    other = rotate(send, "c", C, 1)
    terms, keep = lax.optimization_barrier((terms, keep))

    def of_kind(kind):
        at = jnp.minimum(kind, 2)
        return lax.dynamic_index_in_dim(keep, at, 0, False).astype(
            F32
        ) + lax.dynamic_index_in_dim(other, at, 0, False).astype(F32)

    kind = (y - x) % Y
    held = [jnp.where(kind < 3, of_kind(kind), 0.0).astype(BF16)]
    for k in range(1, Y):
        pairs = [
            (a * Y + b, a * Y + (b + k) % Y)
            for a in range(X)
            for b in range(Y)
            if (b + k - a) % Y < 3
        ]
        piece = of_kind((y + k - x) % Y).astype(BF16)
        held.append(lax.ppermute(piece, ("x", "y"), pairs))
    terms = terms + sum(rotate(terms, "h", H, k) for k in range(1, H))
    reduced_rhs = camera_grad - terms
    reduced_rhs, held[0] = lax.optimization_barrier((reduced_rhs, held[0]))

    quarter = width // 4
    picked = [h ^ m for m in range(4)]
    piece_shape = jax.ShapeDtypeStruct((quarter, width), BF16)
    pieces = small_call(
        pieces_kernel,
        [piece_shape] * 4,
        [((p % 2) ^ l) * 2 + p // 2 for p in picked],
        held,
        [pltpu.VMEM((4, quarter, width), F32)],
    )
    came = []
    for m in range(4):
        pairs = [
            (a * H + b, ((b ^ m) & 1) * H + 2 * a + ((b ^ m) >> 1))
            for a in range(L)
            for b in range(H)
        ]
        came.append(lax.ppermute(pieces[m], ("l", "h"), pairs))

    half_shape = (quarter, width // 2)
    tile_shape = jax.ShapeDtypeStruct((2, quarter, quarter), BF16)
    kept, swap, turned_keep, turned_send = small_call(
        turn_kernel,
        [
            jax.ShapeDtypeStruct(half_shape, F32),
            jax.ShapeDtypeStruct(half_shape, BF16),
            tile_shape,
            tile_shape,
        ],
        [h % 2, c],
        came,
        [pltpu.VMEM((4, quarter, quarter), F32)],
    )
    got = rotate(turned_send, "c", C, 1)
    swapped = rotate_pairs(swap)
    parts = jnp.concatenate([turned_keep, got], axis=0)
    pairs = []
    for a in range(X):
        for e in range(Y):
            if (e - a) % Y not in (1, 2):
                continue
            for l0 in range(L):
                for h0 in range(H):
                    source = ((a * L + l0) * Y + e) * H + h0
                    target = ((e * L + h0 // 2) * Y + a) * H + 2 * l0 + h0 % 2
                    pairs.append((source, target))
    mirror = lax.ppermute(parts, ("x", "l", "y", "h"), pairs)
    low = (h % 2) * 2 + c

    levels = 0.1 * jnp.power(2.0, damping.astype(F32))
    on_diagonal = jnp.eye(width, dtype=bool)
    damped = camera_hessian + jnp.where(on_diagonal, camera_hessian * levels[:, None], 0.0)
    own_rows = lax.dynamic_slice_in_dim(damped, low * quarter, quarter, 0)
    inside = jnp.logical_and(x == y, h // 2 == l)
    base = jnp.where(inside, own_rows, 0.0)
    schur = small_call(
        last_kernel,
        jax.ShapeDtypeStruct((quarter, width), F32),
        [h % 2, c],
        [base, kept, swapped, mirror],
        (),
    )
    return (schur, reduced_rhs)


def solution(mesh):
    finer = Mesh(mesh.devices.reshape(X, L, Y, H, C), ("x", "l", "y", "h", "c"))
    in_specs = (
        P(PAIR, None, BLK),
        P(PAIR, BLK),
        P(PAIR, None, None),
        P(BLK, None),
        P(BLK),
        P(BLK),
        P(PAIR, None),
    )
    out_specs = (P(PAIR, BLK), P(BLK))
    return jax.shard_map(
        shards, mesh=finer, in_specs=in_specs, out_specs=out_specs, check_vma=False
    )
```

time: 202 us -> 201 us (level)
  the two profiles are of different devices: /device:TPU:59 before, /device:TPU:46 now
where the time goes in v2:
time: 201 us; the launch traced here: 200 us
  waiting for transfers between devices  104 us (52%)
  starting transfers between devices  56.6 us (28%)
  Pallas kernels  21 us (10%)
  other arithmetic  9.58 us (5%)
  local copies, waits for them, and re-layouts  8.28 us (4%)
    ppermute x20, waiting for transfers between devices, rotate(): lax.ppermute(array, axis, [(i, (i + step) % size) for i in range(size)])  50.4 us
    ppermute x20, starting transfers between devices, rotate(): lax.ppermute(array, axis, [(i, (i + step) % size) for i in range(size)])  28.7 us
    ppermute x1, waiting for transfers between devices, shards(): mirror = lax.ppermute(parts, ('x', 'l', 'y', 'h'), pairs)  23 us
    pallas_call x2, Pallas kernels, product(): pl.pallas_call(functools.partial(product_kernel, first, last, at), out_sh...  17.4 us
    ppermute x4, waiting for transfers between devices, shards(): came.append(lax.ppermute(pieces[m], ('l', 'h'), pairs))  16.3 us
    ppermute x3, waiting for transfers between devices, shards(): held.append(lax.ppermute(piece, ('x', 'y'), pairs))  13.9 us
    ppermute x4, starting transfers between devices, shards(): came.append(lax.ppermute(pieces[m], ('l', 'h'), pairs))  12.1 us
    ppermute x3, starting transfers between devices, shards(): held.append(lax.ppermute(piece, ('x', 'y'), pairs))  9.91 us
  transfers between devices with their start and end apart: 29, of which 19 were waited for; matrix products, arithmetic and copies ran while one was open for 6% of the time, Pallas kernels for 5%

profile of v2, /device:TPU:46, one launch (start us, length us, event | category | flops | bytes accessed | tf_op | source)
XLA Modules:
  0.0 200.4 jit_solution(4211027085763371153)
XLA Ops:
  0.7 1.3 dynamic-slice_bitcast_fusion
  2.5 1.7 slice.74.refs_2_
  4.3 1.5 collective-permute-start.12
  5.9 1.9 dynamic-slice_bitcast_fusion.1
  7.8 1.7 collective-permute-start.9
  9.5 15.1 %collective-permute-done.13 = bf16[2,576,384]{2,1,0:T(8,128)(2,1)} collective-permute-done((bf16[2,576,384]{2,1,0:T(8,128)(2,1)S(1)}, bf16[2,576,384]{2,1,0:T(8,128)(2,1)}, u32[]{:S(2)}, u32[]{:S(2)}) %collective-permute-start.13) | collective-permute-done | bytes 884768 | tf_op jit(solution)/shard_map/ppermute | solution.py:20
  24.6 1.7 collective-permute-start.14
  26.3 2.6 %multiply_reduce_fusion = f32[576]{0:T(1024)S(1)} fusion(f32[6,384]{1,0:T(8,128)S(1)} %fusion.4, bf16[6]{0:T(256)(128)(2,1)S(1)} %convert_bitcast_fusion, bf16[6,384,576]{1,2,0:T(8,128)(2,1)} %param.7), kind=kLoop, calls=%fused_computation | loop fusion | flops 5307840 | bytes 2665740 | tf_op jit(solution)/shard_map/reduce_sum | solution.py:231
  29.0 1.2 collective-permute-done
  30.3 14.1 %collective-permute-done.4 = s32[6]{0:T(128)S(1)} collective-permute-done((s32[6]{0:T(128)S(1)}, s32[6]{0:T(128)S(1)}, u32[]{:S(2)}, u32[]{:S(2)}) %collective-permute-start.4) | collective-permute-done | bytes 56 | tf_op jit(solution)/shard_map/ppermute | solution.py:20
  44.4 1.5 collective-permute-start.5
  46.0 3.2 %collective-permute-done.5 = s32[6]{0:T(128)S(1)} collective-permute-done((s32[6]{0:T(128)S(1)}, s32[6]{0:T(128)S(1)}, u32[]{:S(2)}, u32[]{:S(2)}) %collective-permute-start.5) | collective-permute-done | bytes 56 | tf_op jit(solution)/shard_map/ppermute | solution.py:20
  49.2 1.2 collective-permute-start.6
  50.4 3.9 %collective-permute-done.6 = s32[6]{0:T(128)S(1)} collective-permute-done((s32[6]{0:T(128)S(1)}, s32[6]{0:T(128)S(1)}, u32[]{:S(2)}, u32[]{:S(2)}) %collective-permute-start.6) | collective-permute-done | bytes 56 | tf_op jit(solution)/shard_map/ppermute | solution.py:20
  54.3 1.6 collective-permute-start.1
  55.8 2.1 %collective-permute-done.1 = f32[576]{0:T(1024)} collective-permute-done((f32[576]{0:T(1024)S(1)}, f32[576]{0:T(1024)}, u32[]{:S(2)}, u32[]{:S(2)}) %collective-permute-start.1) | collective-permute-done | bytes 2336 | tf_op jit(solution)/shard_map/ppermute | solution.py:20
  58.0 2.3 %collective-permute-start.2 = (f32[576]{0:T(1024)S(1)}, f32[576]{0:T(1024)S(1)}, u32[]{:S(2)}, u32[]{:S(2)}) collective-permute-start(f32[576]{0:T(1024)S(1)} %add.169), channel_id=1, source_target_pairs={{0,16},{8,24},{16,0},{24,8},{1,17},{9,25},{17,1},{25,9},{2,18},{10... | collective-permute-start | bytes 6920 | tf_op jit(solution)/shard_map/ppermute | solution.py:20
  60.3 2.8 %collective-permute-done.2 = f32[576]{0:T(1024)S(1)} collective-permute-done((f32[576]{0:T(1024)S(1)}, f32[576]{0:T(1024)S(1)}, u32[]{:S(2)}, u32[]{:S(2)}) %collective-permute-start.2) | collective-permute-done | bytes 2336 | tf_op jit(solution)/shard_map/ppermute | solution.py:20
  63.1 1.7 collective-permute-start.3
  65.4 1.3 slice.73.refs_2_
  70.3 3.0 %collective-permute-start.10 = (bf16[1,576,384]{2,1,0:T(8,128)(2,1)}, bf16[1,576,384]{2,1,0:T(8,128)(2,1)S(1)}, u32[]{:S(2)}, u32[]{:S(2)}) collective-permute-start(bf16[1,576,384]{2,1,0:T(8,128)(2,1)} %collective-permute-done.9), channel_id=1, source_target_pairs={{0,64},{64,128},{128,192},{192,0},{1,65},{65,129},{129,193},{193,1... | collective-permute-start | bytes 1327112 | tf_op jit(solution)/shard_map/ppermute | solution.py:20
  73.3 10.3 %product.2.refs_7_ = f32[3,2,2,144,1152]{4,3,2,1,0:T(8,128)S(1)} custom-call(s32[2]{0:T(128)S(1)} %pad_add_fusion.3.refs_0_, s32[4,6]{1,0:T(4,128)S(1)} %pad_add_fusion.refs_1_, bf16[4,576,384]{2,1,0:T(8,128)(2,1)S(1)} %slice.74.refs_2_, bf16[4,576,384]{2,1,0:T(8,128)(2,1)} %collective-permute-done.11.refs_3_, ...), custom_call_target="tpu_custom_call" | custom-call | flops 5096079360 | bytes 16777216 | tf_op jit(solution)/shard_map/product/pallas_call | solution.py:186
  83.7 1.7 collective-permute-done.8.refs_4_
  85.4 7.1 %product.3 = (bf16[3,2,144,1152]{3,2,1,0:T(8,128)(2,1)}, bf16[3,2,144,1152]{3,2,1,0:T(8,128)(2,1)S(1)}) custom-call(s32[2]{0:T(128)S(1)} %pad_add_fusion.3.refs_0_, s32[4,6]{1,0:T(4,128)S(1)} %pad_add_fusion.refs_1_, bf16[2,576,384]{2,1,0:T(8,128)(2,1)S(1)} %slice.73.refs_2_, bf16[2,576,384]{2,1,0:T(8,128)(2,1)S(1)} %collective-permute-done.7.refs_3_, ...), custom_call_target="tpu_custom_call" | custom-call | flops 2548039680 | bytes 16777216 | tf_op jit(solution)/shard_map/product/pallas_call | solution.py:186
  92.5 4.3 %collective-permute-done.18 = bf16[3,2,144,1152]{3,2,1,0:T(8,128)(2,1)} collective-permute-done((bf16[3,2,144,1152]{3,2,1,0:T(8,128)(2,1)}, bf16[3,2,144,1152]{3,2,1,0:T(8,128)(2,1)}, u32[]{:S(2)}, u32[]{:S(2)}) %collective-permute-start.18) | collective-permute-done | bytes 1990688 | tf_op jit(solution)/shard_map/ppermute | solution.py:20
  96.8 3.5 %fusion.3 = (bf16[2,144,1152]{2,1,0:T(8,128)(2,1)S(1)}, bf16[2,144,1152]{2,1,0:T(8,128)(2,1)}, bf16[2,144,1152]{2,1,0:T(8,128)(2,1)}, bf16[2,144,1152]{2,1,0:T(8,128)(2,1)S(1)}) fusion(bf16[3,2,144,1152]{3,2,1,0:T(8,128)(2,1)} %collective-permute-done.18, s32[]{:T(128)S(6)} %select_n.129, bf16[3,2,144,1152]{3,2,1,0:T(8,128)(2,1)S(1)} %get-tuple-element.22, ...), kind=kLoop, calls=%fused_computation.9 | loop fusion | flops 5640192 | bytes 7962641 | tf_op jit(solution)/shard_map/convert_element_type | solution.py:261
  100.4 1.3 collective-permute-start.19
  101.7 6.7 %collective-permute-start.20 = (bf16[2,144,1152]{2,1,0:T(8,128)(2,1)}, bf16[2,144,1152]{2,1,0:T(8,128)(2,1)S(1)}, u32[]{:S(2)}, u32[]{:S(2)}) collective-permute-start(bf16[2,144,1152]{2,1,0:T(8,128)(2,1)} %get-tuple-element.35), channel_id=1, source_target_pairs={{0,16},{16,0},{24,8},{64,80},{72,88},{88,72},{128,144},{136,152},{... | collective-permute-start | bytes 1990664 | tf_op jit(solution)/shard_map/ppermute | solution.py:262
  108.4 1.9 collective-permute-start.21
  110.4 3.4 %collective-permute-start.15 = (f32[576]{0:T(1024)S(1)}, f32[576]{0:T(1024)S(1)}, u32[]{:S(2)}, u32[]{:S(2)}) collective-permute-start(f32[576]{0:T(1024)S(1)} %add_add_fusion), channel_id=1, source_target_pairs={{0,2},{2,4},{4,6},{6,0},{1,3},{3,5},{5,7},{7,1},{8,10},{10,12},{12... | collective-permute-start | bytes 6920 | tf_op jit(solution)/shard_map/ppermute | solution.py:20
  113.7 4.8 %collective-permute-start.16 = (f32[576]{0:T(1024)S(1)}, f32[576]{0:T(1024)S(1)}, u32[]{:S(2)}, u32[]{:S(2)}) collective-permute-start(f32[576]{0:T(1024)S(1)} %add_add_fusion), channel_id=1, source_target_pairs={{0,4},{2,6},{4,0},{6,2},{1,5},{3,7},{5,1},{7,3},{8,12},{10,14},{12... | collective-permute-start | bytes 6920 | tf_op jit(solution)/shard_map/ppermute | solution.py:20
  118.5 2.7 %collective-permute-start.17 = (f32[576]{0:T(1024)S(1)}, f32[576]{0:T(1024)S(1)}, u32[]{:S(2)}, u32[]{:S(2)}) collective-permute-start(f32[576]{0:T(1024)S(1)} %add_add_fusion), channel_id=1, source_target_pairs={{0,6},{2,0},{4,2},{6,4},{1,7},{3,1},{5,3},{7,5},{8,14},{10,8},{12,... | collective-permute-start | bytes 6920 | tf_op jit(solution)/shard_map/ppermute | solution.py:20
  121.3 1.8 collective-permute-done.17
  123.8 13.7 %collective-permute-done.21.c_ref = bf16[2,144,1152]{2,1,0:T(8,128)(2,1)S(1)} collective-permute-done((bf16[2,144,1152]{2,1,0:T(8,128)(2,1)S(1)}, bf16[2,144,1152]{2,1,0:T(8,128)(2,1)S(1)}, u32[]{:S(2)}, u32[]{:S(2)}) %collective-permute-start.21) | collective-permute-done | bytes 663584 | tf_op jit(solution)/shard_map/ppermute | solution.py:262
  137.5 1.1 shard_map.86
  138.6 8.0 %collective-permute-start.22 = (bf16[144,576]{1,0:T(8,128)(2,1)S(1)}, bf16[144,576]{1,0:T(8,128)(2,1)S(1)}, u32[]{:S(2)}, u32[]{:S(2)}) collective-permute-start(bf16[144,576]{1,0:T(8,128)(2,1)S(1)} %get-tuple-element.25), channel_id=1, source_target_pairs={{0,0},{2,32},{4,2},{6,34},{32,4},{34,36},{36,6},{38,38},{1,1},{3,3... | collective-permute-start | bytes 497672 | tf_op jit(solution)/shard_map/ppermute | solution.py:284
  146.7 1.5 collective-permute-start.23
  148.2 2.5 %collective-permute-start.25 = (bf16[144,576]{1,0:T(8,128)(2,1)S(1)}, bf16[144,576]{1,0:T(8,128)(2,1)S(1)}, u32[]{:S(2)}, u32[]{:S(2)}) collective-permute-start(bf16[144,576]{1,0:T(8,128)(2,1)S(1)} %get-tuple-element.28), channel_id=1, source_target_pairs={{0,34},{2,2},{4,32},{6,0},{32,38},{34,6},{36,36},{38,4},{1,35},{3,... | collective-permute-start | bytes 497672 | tf_op jit(solution)/shard_map/ppermute | solution.py:284
  150.8 3.7 %collective-permute-done.22.refs_0_ = bf16[144,576]{1,0:T(8,128)(2,1)S(1)} collective-permute-done((bf16[144,576]{1,0:T(8,128)(2,1)S(1)}, bf16[144,576]{1,0:T(8,128)(2,1)S(1)}, u32[]{:S(2)}, u32[]{:S(2)}) %collective-permute-start.22) | collective-permute-done | bytes 165920 | tf_op jit(solution)/shard_map/ppermute | solution.py:284
  154.6 4.8 %collective-permute-done.23.refs_1_ = bf16[144,576]{1,0:T(8,128)(2,1)S(1)} collective-permute-done((bf16[144,576]{1,0:T(8,128)(2,1)S(1)}, bf16[144,576]{1,0:T(8,128)(2,1)S(1)}, u32[]{:S(2)}, u32[]{:S(2)}) %collective-permute-start.23) | collective-permute-done | bytes 165920 | tf_op jit(solution)/shard_map/ppermute | solution.py:284
  159.3 5.5 %collective-permute-done.24.refs_2_ = bf16[144,576]{1,0:T(8,128)(2,1)S(1)} collective-permute-done((bf16[144,576]{1,0:T(8,128)(2,1)S(1)}, bf16[144,576]{1,0:T(8,128)(2,1)S(1)}, u32[]{:S(2)}, u32[]{:S(2)}) %collective-permute-start.24) | collective-permute-done | bytes 165920 | tf_op jit(solution)/shard_map/ppermute | solution.py:284
  164.8 2.3 %collective-permute-done.25.refs_3_ = bf16[144,576]{1,0:T(8,128)(2,1)S(1)} collective-permute-done((bf16[144,576]{1,0:T(8,128)(2,1)S(1)}, bf16[144,576]{1,0:T(8,128)(2,1)S(1)}, u32[]{:S(2)}, u32[]{:S(2)}) %collective-permute-start.25) | collective-permute-done | bytes 165920 | tf_op jit(solution)/shard_map/ppermute | solution.py:284
  167.1 1.0 shard_map.87
  168.4 3.8 %collective-permute-start.26 = (bf16[144,288]{1,0:T(8,128)(2,1)S(1)}, bf16[144,288]{1,0:T(8,128)(2,1)S(1)}, u32[]{:S(2)}, u32[]{:S(2)}) collective-permute-start(bf16[144,288]{1,0:T(8,128)(2,1)S(1)} %get-tuple-element.30), channel_id=1, source_target_pairs={{0,2},{2,0},{4,6},{6,4},{1,3},{3,1},{5,7},{7,5},{8,10},{10,8},{12,... | collective-permute-start | bytes 248840 | tf_op jit(solution)/shard_map/ppermute | solution.py:88
  172.2 2.1 %collective-permute-start.28 = (bf16[4,144,144]{2,1,0:T(8,128)(2,1)S(1)}, bf16[4,144,144]{2,1,0:T(8,128)(2,1)S(1)}, u32[]{:S(2)}, u32[]{:S(2)}) collective-permute-start(bf16[4,144,144]{2,1,0:T(8,128)(2,1)S(1)} %pad_maximum_fusion), channel_id=1, source_target_pairs={{8,64},{10,66},{12,96},{14,98},{40,68},{42,70},{44,100},{46,102},{... | collective-permute-start | bytes 497672 | tf_op jit(solution)/shard_map/ppermute | solution.py:313
  174.3 1.1 add_select_fusion.base_ref
  175.9 23.0 %collective-permute-done.28.mirror_ref = bf16[4,144,144]{2,1,0:T(8,128)(2,1)S(1)} collective-permute-done((bf16[4,144,144]{2,1,0:T(8,128)(2,1)S(1)}, bf16[4,144,144]{2,1,0:T(8,128)(2,1)S(1)}, u32[]{:S(2)}, u32[]{:S(2)}) %collective-permute-start.28) | collective-permute-done | bytes 165920 | tf_op jit(solution)/shard_map/ppermute | solution.py:313
  198.9 1.5 shard_map.88
  (57 shorter events, 7.1 us)
Async XLA Ops:
  1.9 22.7 %collective-permute-start.13 = (bf16[2,576,384]{2,1,0:T(8,128)(2,1)S(1)}, bf16[2,576,384]{2,1,0:T(8,128)(2,1)}, u32[]{:S(2)}, u32[]{:S(2)}) collective-permute-start(bf16[2,576,384]{2,1,0:T(8,128)(2,1)S(1)} %dynamic-slice_bitcast_fusion), channel_id=1, source_target_pairs={{0,64},{64,128},{128,192},{192,0},{1,65},{65,129},{129,193},{193,1... | collective-permute-start | bytes 2654216 | tf_op jit(solution)/shard_map/ppermute | solution.py:20
  2.5 7.0 %copy-start = (f32[6,9,128]{2,0,1:T(8,128)S(1)}, f32[6,9,128]{2,0,1:T(8,128)}, u32[]{:S(2)}) copy-start(f32[6,9,128]{2,0,1:T(8,128)} %param.9) | copy-start | bytes 82948
  2.5 7.0 %copy-start.1 = (f32[6,384]{1,0:T(8,128)S(1)}, f32[6,384]{1,0:T(8,128)}, u32[]{:S(2)}) copy-start(f32[6,384]{1,0:T(8,128)} %param.13) | copy-start | bytes 27652
  2.5 23.8 %copy-start.5 = (s32[6,1]{0,1:T(1,128)S(1)}, s32[6,1]{0,1:T(1,128)}, u32[]{:S(2)}) copy-start(s32[6,1]{0,1:T(1,128)} %param.8) | copy-start | bytes 76
  4.1 69.2 %collective-permute-start.11 = (bf16[4,576,384]{2,1,0:T(8,128)(2,1)S(1)}, bf16[4,576,384]{2,1,0:T(8,128)(2,1)}, u32[]{:S(2)}, u32[]{:S(2)}) collective-permute-start(bf16[4,576,384]{2,1,0:T(8,128)(2,1)S(1)} %slice.74.refs_2_), channel_id=1, source_target_pairs={{0,32},{32,0},{1,33},{33,1},{2,34},{34,2},{3,35},{35,3},{4,36},{36... | collective-permute-start | bytes 5308424 | tf_op jit(solution)/shard_map/ppermute | solution.py:20
  4.3 69.0 %collective-permute-start.12 = (bf16[4,576,384]{2,1,0:T(8,128)(2,1)S(1)}, bf16[4,576,384]{2,1,0:T(8,128)(2,1)}, u32[]{:S(2)}, u32[]{:S(2)}) collective-permute-start(bf16[4,576,384]{2,1,0:T(8,128)(2,1)S(1)} %slice.74.refs_2_), channel_id=1, source_target_pairs={{0,192},{64,0},{128,64},{192,128},{1,193},{65,1},{129,65},{193,129... | collective-permute-start | bytes 5308424 | tf_op jit(solution)/shard_map/ppermute | solution.py:20
  7.8 60.8 %collective-permute-start.9 = (bf16[1,576,384]{2,1,0:T(8,128)(2,1)}, bf16[1,576,384]{2,1,0:T(8,128)(2,1)}, u32[]{:S(2)}, u32[]{:S(2)}) collective-permute-start(bf16[1,576,384]{2,1,0:T(8,128)(2,1)} %dynamic-slice_bitcast_fusion.1), channel_id=1, source_target_pairs={{0,64},{64,128},{128,192},{192,0},{1,65},{65,129},{129,193},{193,1... | collective-permute-start | bytes 1327112 | tf_op jit(solution)/shard_map/ppermute | solution.py:20
  24.6 45.7 %collective-permute-start.14 = (bf16[2,576,384]{2,1,0:T(8,128)(2,1)}, bf16[2,576,384]{2,1,0:T(8,128)(2,1)S(1)}, u32[]{:S(2)}, u32[]{:S(2)}) collective-permute-start(bf16[2,576,384]{2,1,0:T(8,128)(2,1)} %collective-permute-done.13), channel_id=1, source_target_pairs={{0,64},{64,128},{128,192},{192,0},{1,65},{65,129},{129,193},{193,1... | collective-permute-start | bytes 2654216 | tf_op jit(solution)/shard_map/ppermute | solution.py:20
  28.9 1.2 collective-permute-start
  30.2 14.2 %collective-permute-start.4 = (s32[6]{0:T(128)S(1)}, s32[6]{0:T(128)S(1)}, u32[]{:S(2)}, u32[]{:S(2)}) collective-permute-start(s32[6]{0:T(128)S(1)} %bitcast.38), channel_id=1, source_target_pairs={{0,32},{32,0},{1,33},{33,1},{2,34},{34,2},{3,35},{35,3},{4,36},{36... | collective-permute-start | bytes 80 | tf_op jit(solution)/shard_map/ppermute | solution.py:20
  44.4 20.4 %copy-start.6 = (s32[6]{0:T(128)}, s32[6]{0:T(128)S(1)}, u32[]{:S(2)}) copy-start(s32[6]{0:T(128)S(1)} %collective-permute-done.4) | copy-start | bytes 76
  44.4 4.8 %collective-permute-start.5 = (s32[6]{0:T(128)S(1)}, s32[6]{0:T(128)S(1)}, u32[]{:S(2)}, u32[]{:S(2)}) collective-permute-start(s32[6]{0:T(128)S(1)} %bitcast.39), channel_id=1, source_target_pairs={{0,192},{64,0},{128,64},{192,128},{1,193},{65,1},{129,65},{193,129... | collective-permute-start | bytes 80 | tf_op jit(solution)/shard_map/ppermute | solution.py:20
  49.2 6.7 %copy-start.7 = (s32[6]{0:T(128)}, s32[6]{0:T(128)S(1)}, u32[]{:S(2)}) copy-start(s32[6]{0:T(128)S(1)} %collective-permute-done.5) | copy-start | bytes 76
  49.2 5.1 %collective-permute-start.6 = (s32[6]{0:T(128)S(1)}, s32[6]{0:T(128)S(1)}, u32[]{:S(2)}, u32[]{:S(2)}) collective-permute-start(s32[6]{0:T(128)S(1)} %bitcast.40), channel_id=1, source_target_pairs={{0,128},{64,192},{128,0},{192,64},{1,129},{65,193},{129,1},{193,65... | collective-permute-start | bytes 80 | tf_op jit(solution)/shard_map/ppermute | solution.py:20
  54.3 10.5 %copy-start.8 = (s32[6]{0:T(128)}, s32[6]{0:T(128)S(1)}, u32[]{:S(2)}) copy-start(s32[6]{0:T(128)S(1)} %collective-permute-done.6) | copy-start | bytes 76
  54.3 3.7 %collective-permute-start.1 = (f32[576]{0:T(1024)S(1)}, f32[576]{0:T(1024)}, u32[]{:S(2)}, u32[]{:S(2)}) collective-permute-start(f32[576]{0:T(1024)S(1)} %add.169), channel_id=1, source_target_pairs={{0,8},{8,16},{16,24},{24,0},{1,9},{9,17},{17,25},{25,1},{2,10},{10... | collective-permute-start | bytes 6920 | tf_op jit(solution)/shard_map/ppermute | solution.py:20
  58.0 5.1 %collective-permute-start.2 = (f32[576]{0:T(1024)S(1)}, f32[576]{0:T(1024)S(1)}, u32[]{:S(2)}, u32[]{:S(2)}) collective-permute-start(f32[576]{0:T(1024)S(1)} %add.169), channel_id=1, source_target_pairs={{0,16},{8,24},{16,0},{24,8},{1,17},{9,25},{17,1},{25,9},{2,18},{10... | collective-permute-start | bytes 6920 | tf_op jit(solution)/shard_map/ppermute | solution.py:20
  63.1 1.7 copy-start.2
  63.1 5.0 %collective-permute-start.3 = (f32[576]{0:T(1024)S(1)}, f32[576]{0:T(1024)}, u32[]{:S(2)}, u32[]{:S(2)}) collective-permute-start(f32[576]{0:T(1024)S(1)} %add.169), channel_id=1, source_target_pairs={{0,24},{8,0},{16,8},{24,16},{1,25},{9,1},{17,9},{25,17},{2,26},{10... | collective-permute-start | bytes 6920 | tf_op jit(solution)/shard_map/ppermute | solution.py:20
  68.1 15.5 %collective-permute-start.7 = (bf16[2,576,384]{2,1,0:T(8,128)(2,1)S(1)}, bf16[2,576,384]{2,1,0:T(8,128)(2,1)S(1)}, u32[]{:S(2)}, u32[]{:S(2)}) collective-permute-start(bf16[2,576,384]{2,1,0:T(8,128)(2,1)S(1)} %slice.73.refs_2_), channel_id=1, source_target_pairs={{0,32},{32,0},{1,33},{33,1},{2,34},{34,2},{3,35},{35,3},{4,36},{36... | collective-permute-start | bytes 2654216 | tf_op jit(solution)/shard_map/ppermute | solution.py:20
  68.5 16.8 %collective-permute-start.8 = (bf16[2,576,384]{2,1,0:T(8,128)(2,1)S(1)}, bf16[2,576,384]{2,1,0:T(8,128)(2,1)S(1)}, u32[]{:S(2)}, u32[]{:S(2)}) collective-permute-start(bf16[2,576,384]{2,1,0:T(8,128)(2,1)S(1)} %slice.73.refs_2_), channel_id=1, source_target_pairs={{0,192},{64,0},{128,64},{192,128},{1,193},{65,1},{129,65},{193,129... | collective-permute-start | bytes 2654216 | tf_op jit(solution)/shard_map/ppermute | solution.py:20
  70.3 13.2 %collective-permute-start.10 = (bf16[1,576,384]{2,1,0:T(8,128)(2,1)}, bf16[1,576,384]{2,1,0:T(8,128)(2,1)S(1)}, u32[]{:S(2)}, u32[]{:S(2)}) collective-permute-start(bf16[1,576,384]{2,1,0:T(8,128)(2,1)} %collective-permute-done.9), channel_id=1, source_target_pairs={{0,64},{64,128},{128,192},{192,0},{1,65},{65,129},{129,193},{193,1... | collective-permute-start | bytes 1327112 | tf_op jit(solution)/shard_map/ppermute | solution.py:20
  92.5 4.3 %collective-permute-start.18 = (bf16[3,2,144,1152]{3,2,1,0:T(8,128)(2,1)}, bf16[3,2,144,1152]{3,2,1,0:T(8,128)(2,1)}, u32[]{:S(2)}, u32[]{:S(2)}) collective-permute-start(bf16[3,2,144,1152]{3,2,1,0:T(8,128)(2,1)} %get-tuple-element.23), channel_id=1, source_target_pairs={{0,1},{1,0},{2,3},{3,2},{4,5},{5,4},{6,7},{7,6},{8,9},{9,8},{10,11... | collective-permute-start | bytes 5971976 | tf_op jit(solution)/shard_map/ppermute | solution.py:20
  92.5 30.5 %copy-start.4 = (f32[576]{0:T(1024)S(1)}, f32[576]{0:T(1024)}, u32[]{:S(2)}) copy-start(f32[576]{0:T(1024)} %param.12) | copy-start | bytes 6916
  100.4 23.2 %collective-permute-start.19 = (bf16[2,144,1152]{2,1,0:T(8,128)(2,1)}, bf16[2,144,1152]{2,1,0:T(8,128)(2,1)S(1)}, u32[]{:S(2)}, u32[]{:S(2)}) collective-permute-start(bf16[2,144,1152]{2,1,0:T(8,128)(2,1)} %get-tuple-element.36), channel_id=1, source_target_pairs={{0,8},{8,16},{24,0},{64,72},{72,80},{80,88},{136,144},{144,152},{1... | collective-permute-start | bytes 1990664 | tf_op jit(solution)/shard_map/ppermute | solution.py:262
  101.7 22.1 %collective-permute-start.20 = (bf16[2,144,1152]{2,1,0:T(8,128)(2,1)}, bf16[2,144,1152]{2,1,0:T(8,128)(2,1)S(1)}, u32[]{:S(2)}, u32[]{:S(2)}) collective-permute-start(bf16[2,144,1152]{2,1,0:T(8,128)(2,1)} %get-tuple-element.35), channel_id=1, source_target_pairs={{0,16},{16,0},{24,8},{64,80},{72,88},{88,72},{128,144},{136,152},{... | collective-permute-start | bytes 1990664 | tf_op jit(solution)/shard_map/ppermute | solution.py:262
  108.4 29.1 %collective-permute-start.21 = (bf16[2,144,1152]{2,1,0:T(8,128)(2,1)S(1)}, bf16[2,144,1152]{2,1,0:T(8,128)(2,1)S(1)}, u32[]{:S(2)}, u32[]{:S(2)}) collective-permute-start(bf16[2,144,1152]{2,1,0:T(8,128)(2,1)S(1)} %get-tuple-element.34), channel_id=1, source_target_pairs={{8,0},{16,8},{24,16},{64,88},{80,72},{88,80},{128,152},{136,128},{... | collective-permute-start | bytes 1990664 | tf_op jit(solution)/shard_map/ppermute | solution.py:262
  110.4 57.9 %copy-start.3 = (s32[576]{0:T(1024)S(1)}, s32[576]{0:T(1024)}, u32[]{:S(2)}) copy-start(s32[576]{0:T(1024)} %param.11) | copy-start | bytes 6916
  110.4 8.1 %collective-permute-start.15 = (f32[576]{0:T(1024)S(1)}, f32[576]{0:T(1024)S(1)}, u32[]{:S(2)}, u32[]{:S(2)}) collective-permute-start(f32[576]{0:T(1024)S(1)} %add_add_fusion), channel_id=1, source_target_pairs={{0,2},{2,4},{4,6},{6,0},{1,3},{3,5},{5,7},{7,1},{8,10},{10,12},{12... | collective-permute-start | bytes 6920 | tf_op jit(solution)/shard_map/ppermute | solution.py:20
  113.7 7.5 %collective-permute-start.16 = (f32[576]{0:T(1024)S(1)}, f32[576]{0:T(1024)S(1)}, u32[]{:S(2)}, u32[]{:S(2)}) collective-permute-start(f32[576]{0:T(1024)S(1)} %add_add_fusion), channel_id=1, source_target_pairs={{0,4},{2,6},{4,0},{6,2},{1,5},{3,7},{5,1},{7,3},{8,12},{10,14},{12... | collective-permute-start | bytes 6920 | tf_op jit(solution)/shard_map/ppermute | solution.py:20
  118.5 4.5 %collective-permute-start.17 = (f32[576]{0:T(1024)S(1)}, f32[576]{0:T(1024)S(1)}, u32[]{:S(2)}, u32[]{:S(2)}) collective-permute-start(f32[576]{0:T(1024)S(1)} %add_add_fusion), channel_id=1, source_target_pairs={{0,6},{2,0},{4,2},{6,4},{1,7},{3,1},{5,3},{7,5},{8,14},{10,8},{12,... | collective-permute-start | bytes 6920 | tf_op jit(solution)/shard_map/ppermute | solution.py:20
  138.6 16.0 %collective-permute-start.22 = (bf16[144,576]{1,0:T(8,128)(2,1)S(1)}, bf16[144,576]{1,0:T(8,128)(2,1)S(1)}, u32[]{:S(2)}, u32[]{:S(2)}) collective-permute-start(bf16[144,576]{1,0:T(8,128)(2,1)S(1)} %get-tuple-element.25), channel_id=1, source_target_pairs={{0,0},{2,32},{4,2},{6,34},{32,4},{34,36},{36,6},{38,38},{1,1},{3,3... | collective-permute-start | bytes 497672 | tf_op jit(solution)/shard_map/ppermute | solution.py:284
  146.7 12.7 %collective-permute-start.23 = (bf16[144,576]{1,0:T(8,128)(2,1)S(1)}, bf16[144,576]{1,0:T(8,128)(2,1)S(1)}, u32[]{:S(2)}, u32[]{:S(2)}) collective-permute-start(bf16[144,576]{1,0:T(8,128)(2,1)S(1)} %get-tuple-element.26), channel_id=1, source_target_pairs={{0,32},{2,0},{4,34},{6,2},{32,36},{34,4},{36,38},{38,6},{1,33},{3,... | collective-permute-start | bytes 497672 | tf_op jit(solution)/shard_map/ppermute | solution.py:284
  148.2 16.6 %collective-permute-start.24 = (bf16[144,576]{1,0:T(8,128)(2,1)S(1)}, bf16[144,576]{1,0:T(8,128)(2,1)S(1)}, u32[]{:S(2)}, u32[]{:S(2)}) collective-permute-start(bf16[144,576]{1,0:T(8,128)(2,1)S(1)} %get-tuple-element.27), channel_id=1, source_target_pairs={{0,2},{2,34},{4,0},{6,32},{32,6},{34,38},{36,4},{38,36},{1,3},{3,3... | collective-permute-start | bytes 497672 | tf_op jit(solution)/shard_map/ppermute | solution.py:284
  148.2 18.9 %collective-permute-start.25 = (bf16[144,576]{1,0:T(8,128)(2,1)S(1)}, bf16[144,576]{1,0:T(8,128)(2,1)S(1)}, u32[]{:S(2)}, u32[]{:S(2)}) collective-permute-start(bf16[144,576]{1,0:T(8,128)(2,1)S(1)} %get-tuple-element.28), channel_id=1, source_target_pairs={{0,34},{2,2},{4,32},{6,0},{32,38},{34,6},{36,36},{38,4},{1,35},{3,... | collective-permute-start | bytes 497672 | tf_op jit(solution)/shard_map/ppermute | solution.py:284
  168.2 4.0 %collective-permute-start.27 = (bf16[2,144,144]{2,1,0:T(8,128)(2,1)S(1)}, bf16[2,144,144]{2,1,0:T(8,128)(2,1)S(1)}, u32[]{:S(2)}, u32[]{:S(2)}) collective-permute-start(bf16[2,144,144]{2,1,0:T(8,128)(2,1)S(1)} %get-tuple-element.32), channel_id=1, source_target_pairs={{0,1},{1,0},{2,3},{3,2},{4,5},{5,4},{6,7},{7,6},{8,9},{9,8},{10,11... | collective-permute-start | bytes 248840 | tf_op jit(solution)/shard_map/ppermute | solution.py:20
  168.4 7.5 %collective-permute-start.26 = (bf16[144,288]{1,0:T(8,128)(2,1)S(1)}, bf16[144,288]{1,0:T(8,128)(2,1)S(1)}, u32[]{:S(2)}, u32[]{:S(2)}) collective-permute-start(bf16[144,288]{1,0:T(8,128)(2,1)S(1)} %get-tuple-element.30), channel_id=1, source_target_pairs={{0,2},{2,0},{4,6},{6,4},{1,3},{3,1},{5,7},{7,5},{8,10},{10,8},{12,... | collective-permute-start | bytes 248840 | tf_op jit(solution)/shard_map/ppermute | solution.py:88
  172.2 26.7 %collective-permute-start.28 = (bf16[4,144,144]{2,1,0:T(8,128)(2,1)S(1)}, bf16[4,144,144]{2,1,0:T(8,128)(2,1)S(1)}, u32[]{:S(2)}, u32[]{:S(2)}) collective-permute-start(bf16[4,144,144]{2,1,0:T(8,128)(2,1)S(1)} %pad_maximum_fusion), channel_id=1, source_target_pairs={{8,64},{10,66},{12,96},{14,98},{40,68},{42,70},{44,100},{46,102},{... | collective-permute-start | bytes 497672 | tf_op jit(solution)/shard_map/ppermute | solution.py:313

commit v3 on v2

--- a/solution.py
+++ b/solution.py
@@ -36,52 +36,73 @@
 
 def pieces_kernel(which_ref, own_ref, a_ref, b_ref, c_ref, *rest):
     outs, cut_ref = rest[:4], rest[4]
-    width = own_ref.shape[2] // 2
-    half = width // 2
-    for i in range(2):
-        total = own_ref[i].astype(F32) + a_ref[i].astype(F32)
-        total = total + b_ref[i].astype(F32) + c_ref[i].astype(F32)
-        for n in range(4):
-            cut_ref[n, :, i * half : (i + 1) * half] = total[:, n * half : (n + 1) * half]
+    quarter, width = own_ref.shape
+    half, rows = width // 4, quarter // 2
+    total = own_ref[...].astype(F32) + a_ref[...].astype(F32)
+    total = total + b_ref[...].astype(F32) + c_ref[...].astype(F32)
+    for n in range(4):
+        for p in range(2):
+            cut_ref[n, :, p * half : (p + 1) * half] = total[
+                p * rows : (p + 1) * rows, n * half : (n + 1) * half
+            ]
     for m in range(4):
         outs[m][...] = cut_ref[which_ref[m]].astype(BF16)
 
 
 def turn_kernel(which_ref, *refs):
-    ins, (kept_ref, swap_ref, turned_keep_ref, turned_send_ref, turned_ref) = refs[:4], refs[4:]
-    quarter, width = ins[0].shape
-    half = width // 2
-    odd, core = which_ref[0] == 1, which_ref[1]
-    wide = ins[0][...].astype(F32) + ins[1][...].astype(F32)
-    wide = wide + ins[2][...].astype(F32) + ins[3][...].astype(F32)
-    low, high = wide[:, :half], wide[:, half:]
-    kept_ref[...] = jnp.where(odd, high, low)
-    swap_ref[...] = jnp.where(odd, low, high).astype(BF16)
-    shape = (width, width)
+    ins = refs[:8]
+    kept_ref, swap_ref, turned_keep_ref, turned_send_ref, wide_ref, turned_ref = refs[8:]
+    rows, width = ins[0].shape
+    half, quarter = width // 2, 2 * rows
+    odd, core = which_ref[0], which_ref[1]
+    for i in range(2):
+        total = ins[4 * i][...].astype(F32) + ins[4 * i + 1][...].astype(F32)
+        total = total + ins[4 * i + 2][...].astype(F32) + ins[4 * i + 3][...].astype(F32)
+        for p in range(2):
+            wide_ref[i, p * rows : (p + 1) * rows, :] = total[:, p * half : (p + 1) * half]
+    kept_ref[...] = wide_ref[odd]
+    other = wide_ref[1 - odd].astype(BF16)
+    for p in range(2):
+        swap_ref[:, p * half : (p + 1) * half] = other[p * rows : (p + 1) * rows]
+    shape = (half, half)
     same = lax.broadcasted_iota(jnp.int32, shape, 0) == lax.broadcasted_iota(jnp.int32, shape, 1)
-    turned = lax.dot_general(
-        same.astype(F32).astype(BF16),
-        wide.astype(BF16),
-        (((1,), (1,)), ((), ())),
-        preferred_element_type=F32,
-    )
-    turned_ref[...] = turned.reshape(4, quarter, quarter)
-    for i in range(2):
-        turned_keep_ref[i] = turned_ref[2 * i + core].astype(BF16)
-        turned_send_ref[i] = turned_ref[2 * i + 1 - core].astype(BF16)
-
-
-def last_kernel(which_ref, base_ref, kept_ref, swapped_ref, mirror_ref, out_ref):
-    quarter = mirror_ref.shape[2]
-    odd = which_ref[0]
+    same = same.astype(F32).astype(BF16)
+    for i in range(2):
+        turned = lax.dot_general(
+            same, wide_ref[i].astype(BF16), (((1,), (1,)), ((), ())), preferred_element_type=F32
+        )
+        turned_ref[...] = turned.reshape(2, quarter, quarter)
+        turned_keep_ref[i] = turned_ref[core].astype(BF16)
+        turned_send_ref[i] = turned_ref[1 - core].astype(BF16)
+
+
+def pack_kernel(which_ref, keep_ref, got_ref, out_ref):
+    del which_ref
+    quarter = keep_ref.shape[1]
+    for n in range(4):
+        ref = keep_ref if n < 2 else got_ref
+        out_ref[:, n * quarter : (n + 1) * quarter] = ref[n % 2]
+
+
+def last_kernel(which_ref, base_ref, kept_ref, swapped_ref, mirror_ref, out_ref, full_ref):
+    quarter, half = kept_ref.shape
+    rows = quarter // 2
+    odd, core = which_ref[0], which_ref[1]
+    for p in range(2):
+        full_ref[p * rows : (p + 1) * rows, :] = swapped_ref[
+            :, p * half : (p + 1) * half
+        ].astype(F32)
     for n in range(4):
         columns = slice((n % 2) * quarter, (n % 2 + 1) * quarter)
-        total = jnp.where(
-            odd == n // 2, kept_ref[:, columns], swapped_ref[:, columns].astype(F32)
+        total = jnp.where(odd == n // 2, kept_ref[:, columns], full_ref[:, columns])
+        at, other = n // 2, 2 + n // 2
+        mirror = jnp.where(
+            core == n % 2,
+            mirror_ref[:, at * quarter : (at + 1) * quarter].astype(F32),
+            mirror_ref[:, other * quarter : (other + 1) * quarter].astype(F32),
         )
         to = slice(n * quarter, (n + 1) * quarter)
-        at = jnp.where(which_ref[1] == n % 2, n // 2, 2 + n // 2)
-        out_ref[:, to] = base_ref[:, to] - (total + mirror_ref[at].astype(F32))
+        out_ref[:, to] = base_ref[:, to] - (total + mirror)
 
 
 def rotate_pairs(array):
@@ -104,7 +125,7 @@
     if not first:
         before_ref, refs = refs[0], refs[1:]
     if last:
-        send_ref, keep_ref, left_ref, scaled_ref, sums_ref = refs
+        sends, keeps, (left_ref, scaled_ref, sums_ref) = refs[:2], refs[2:4], refs[4:]
     else:
         sums_ref, left_ref, scaled_ref = refs
     blocks, width, rows = own_ref.shape
@@ -152,10 +173,10 @@
             sums_ref[kind, :, :, :, columns] = term
             if last:
                 for i in range(2):
-                    send_ref[kind, i, :, columns] = sums_ref[
+                    sends[i][kind, :, columns] = sums_ref[
                         kind, i, 1 - core, :, columns
                     ].astype(BF16)
-                    keep_ref[kind, i, :, columns] = sums_ref[
+                    keeps[i][kind, :, columns] = sums_ref[
                         kind, i, core, :, columns
                     ].astype(BF16)
 
@@ -163,7 +184,7 @@
 def product(first, last, at, where, seen, own, mate, following, far, inverse, before=None):
     blocks, width, rows = own.shape
     sums = (3, 2, 2, width // 4, 2 * width)
-    half = (3, 2, width // 4, 2 * width)
+    half = (3, width // 4, 2 * width)
     vmem = pl.BlockSpec(memory_space=pltpu.VMEM)
     smem = pl.BlockSpec(memory_space=pltpu.SMEM)
     scratch = [
@@ -171,8 +192,8 @@
         pltpu.VMEM((2 * width, blocks * rows), BF16),
     ]
     if last:
-        out_shape = (jax.ShapeDtypeStruct(half, BF16), jax.ShapeDtypeStruct(half, BF16))
-        out_specs = (vmem, vmem)
+        out_shape = [jax.ShapeDtypeStruct(half, BF16)] * 4
+        out_specs = [vmem] * 4
         scratch.append(pltpu.VMEM(sums, F32))
     else:
         out_shape = jax.ShapeDtypeStruct(sums, F32)
@@ -239,49 +260,57 @@
         sums = product(
             n == 0, n == len(CHUNKS) - 1, chunk[0], where, seen, *chunk[1:], before=sums
         )
-    send, keep = sums
-    other = rotate(send, "c", C, 1)
-    terms, keep = lax.optimization_barrier((terms, keep))
-
-    def of_kind(kind):
-        at = jnp.minimum(kind, 2)
-        return lax.dynamic_index_in_dim(keep, at, 0, False).astype(
-            F32
-        ) + lax.dynamic_index_in_dim(other, at, 0, False).astype(F32)
+    sends, keeps = sums[:2], list(sums[2:])
+    others = []
+    for i in range(2):
+        others.append(rotate(sends[i], "c", C, 1))
 
     kind = (y - x) % Y
-    held = [jnp.where(kind < 3, of_kind(kind), 0.0).astype(BF16)]
-    for k in range(1, Y):
-        pairs = [
-            (a * Y + b, a * Y + (b + k) % Y)
-            for a in range(X)
-            for b in range(Y)
-            if (b + k - a) % Y < 3
-        ]
-        piece = of_kind((y + k - x) % Y).astype(BF16)
-        held.append(lax.ppermute(piece, ("x", "y"), pairs))
+    held = []
+    for i in range(2):
+
+        def of_kind(kind):
+            at = jnp.minimum(kind, 2)
+            return lax.dynamic_index_in_dim(keeps[i], at, 0, False).astype(
+                F32
+            ) + lax.dynamic_index_in_dim(others[i], at, 0, False).astype(F32)
+
+        parts = [jnp.where(kind < 3, of_kind(kind), 0.0).astype(BF16)]
+        for k in range(1, Y):
+            pairs = [
+                (a * Y + b, a * Y + (b + k) % Y)
+                for a in range(X)
+                for b in range(Y)
+                if (b + k - a) % Y < 3
+            ]
+            piece = of_kind((y + k - x) % Y).astype(BF16)
+            if i == 0 and k == Y - 1:
+                terms, piece = lax.optimization_barrier((terms, piece))
+            parts.append(lax.ppermute(piece, ("x", "y"), pairs))
+        held.append(parts)
     terms = terms + sum(rotate(terms, "h", H, k) for k in range(1, H))
     reduced_rhs = camera_grad - terms
-    reduced_rhs, held[0] = lax.optimization_barrier((reduced_rhs, held[0]))
+    reduced_rhs, held[1][0] = lax.optimization_barrier((reduced_rhs, held[1][0]))
 
     quarter = width // 4
     picked = [h ^ m for m in range(4)]
-    piece_shape = jax.ShapeDtypeStruct((quarter, width), BF16)
-    pieces = small_call(
-        pieces_kernel,
-        [piece_shape] * 4,
-        [((p % 2) ^ l) * 2 + p // 2 for p in picked],
-        held,
-        [pltpu.VMEM((4, quarter, width), F32)],
-    )
+    piece_shape = jax.ShapeDtypeStruct((quarter // 2, width), BF16)
     came = []
-    for m in range(4):
-        pairs = [
-            (a * H + b, ((b ^ m) & 1) * H + 2 * a + ((b ^ m) >> 1))
-            for a in range(L)
-            for b in range(H)
-        ]
-        came.append(lax.ppermute(pieces[m], ("l", "h"), pairs))
+    for i in range(2):
+        pieces = small_call(
+            pieces_kernel,
+            [piece_shape] * 4,
+            [((p % 2) ^ l) * 2 + p // 2 for p in picked],
+            held[i],
+            [pltpu.VMEM((4, quarter // 2, width), F32)],
+        )
+        for m in range(4):
+            pairs = [
+                (a * H + b, ((b ^ m) & 1) * H + 2 * a + ((b ^ m) >> 1))
+                for a in range(L)
+                for b in range(H)
+            ]
+            came.append(lax.ppermute(pieces[m], ("l", "h"), pairs))
 
     half_shape = (quarter, width // 2)
     tile_shape = jax.ShapeDtypeStruct((2, quarter, quarter), BF16)
@@ -289,17 +318,19 @@
         turn_kernel,
         [
             jax.ShapeDtypeStruct(half_shape, F32),
-            jax.ShapeDtypeStruct(half_shape, BF16),
+            piece_shape,
             tile_shape,
             tile_shape,
         ],
         [h % 2, c],
         came,
-        [pltpu.VMEM((4, quarter, quarter), F32)],
+        [pltpu.VMEM((2, *half_shape), F32), pltpu.VMEM((2, quarter, quarter), F32)],
     )
     got = rotate(turned_send, "c", C, 1)
     swapped = rotate_pairs(swap)
-    parts = jnp.concatenate([turned_keep, got], axis=0)
+    mirrored = small_call(
+        pack_kernel, jax.ShapeDtypeStruct((quarter, width), BF16), [c], [turned_keep, got], ()
+    )
     pairs = []
     for a in range(X):
         for e in range(Y):
@@ -310,7 +341,7 @@
                     source = ((a * L + l0) * Y + e) * H + h0
                     target = ((e * L + h0 // 2) * Y + a) * H + 2 * l0 + h0 % 2
                     pairs.append((source, target))
-    mirror = lax.ppermute(parts, ("x", "l", "y", "h"), pairs)
+    mirror = lax.ppermute(mirrored, ("x", "l", "y", "h"), pairs)
     low = (h % 2) * 2 + c
 
     levels = 0.1 * jnp.power(2.0, damping.astype(F32))
@@ -324,7 +355,7 @@
         jax.ShapeDtypeStruct((quarter, width), F32),
         [h % 2, c],
         [base, kept, swapped, mirror],
-        (),
+        [pltpu.VMEM(half_shape, F32)],
     )
     return (schur, reduced_rhs)
 

time: 201 us -> 199 us (0.990)
  waiting for transfers between devices: 104 us -> 81.1 us
  starting transfers between devices: 56.6 us -> 74 us
    ppermute x4 -> x7, starting transfers between devices: 12 us -> 22.3 us  [the longest x6 18.9 us: shards(): parts.append(lax.ppermute(piece, ('x', 'y'), pairs))]
    ppermute x4 -> x7, waiting for transfers between devices: 36.9 us -> 27.5 us  [the longest x1 15.8 us: shards(): mirror = lax.ppermute(mirrored, ('x', 'l', 'y', 'h'), pairs)]
    ppermute x4 -> x8, waiting for transfers between devices: 16.3 us -> 6.99 us  [shards(): came.append(lax.ppermute(pieces[m], ('l', 'h'), pairs))]
    ppermute x4 -> x8, starting transfers between devices: 12.1 us -> 20.6 us  [shards(): came.append(lax.ppermute(pieces[m], ('l', 'h'), pairs))]
    ppermute x20 -> x21, waiting for transfers between devices: 50.4 us -> 46.6 us  [rotate(): lax.ppermute(array, axis, [(i, (i + step) % size) for i in range(size)])]
    convert_element_type x1 -> x2, other arithmetic: 3.55 us -> 4.76 us  [shards(): piece = of_kind((y + k - x) % Y).astype(BF16)]
    pallas_call x3 -> x5, Pallas kernels: 3.63 us -> 4.6 us  [small_call(): pl.pallas_call(kernel, out_shape=out_shape, in_specs=[smem] + [vmem] * le...]
    ppermute x20 -> x21, starting transfers between devices: 28.7 us -> 29.1 us  [rotate(): lax.ppermute(array, axis, [(i, (i + step) % size) for i in range(size)])]
  transfers between devices with their start and end apart: 29 -> 37, of which waited for: 19 -> 15; matrix products, arithmetic and copies ran while one was open for 6% -> 9% of each run, Pallas kernels for 5% -> 6%
where the time goes in v3:
time: 199 us
  waiting for transfers between devices  81.1 us (41%)
  starting transfers between devices  74 us (37%)
  Pallas kernels  22.7 us (11%)
  other arithmetic  10.7 us (5%)
  local copies, waits for them, and re-layouts  9 us (5%)
    ppermute x21, waiting for transfers between devices, rotate(): lax.ppermute(array, axis, [(i, (i + step) % size) for i in range(size)])  46.6 us
    ppermute x21, starting transfers between devices, rotate(): lax.ppermute(array, axis, [(i, (i + step) % size) for i in range(size)])  29.1 us
    ppermute x8, starting transfers between devices, shards(): came.append(lax.ppermute(pieces[m], ('l', 'h'), pairs))  20.6 us
    ppermute x6, starting transfers between devices, shards(): parts.append(lax.ppermute(piece, ('x', 'y'), pairs))  18.9 us
    pallas_call x2, Pallas kernels, product(): pl.pallas_call(functools.partial(product_kernel, first, last, at), out_sh...  18.1 us
    ppermute x1, waiting for transfers between devices, shards(): mirror = lax.ppermute(mirrored, ('x', 'l', 'y', 'h'), pairs)  15.8 us
    ppermute x6, waiting for transfers between devices, shards(): parts.append(lax.ppermute(piece, ('x', 'y'), pairs))  11.6 us
    ppermute x8, waiting for transfers between devices, shards(): came.append(lax.ppermute(pieces[m], ('l', 'h'), pairs))  6.99 us
  transfers between devices with their start and end apart: 37, of which 15 were waited for; matrix products, arithmetic and copies ran while one was open for 9% of the time, Pallas kernels for 6%

profile of v3, /device:TPU:46, one launch (start us, length us, event | category | flops | bytes accessed | tf_op | source)
XLA Modules:
  0.0 198.6 jit_solution(15859360820265212203)
XLA Ops:
  0.7 1.3 dynamic-slice_bitcast_fusion
  2.5 1.7 slice.74.refs_2_
  4.4 1.5 collective-permute-start.12
  5.9 1.8 dynamic-slice_bitcast_fusion.1
  7.7 1.7 collective-permute-start.9
  9.4 15.2 %collective-permute-done.13 = bf16[2,576,384]{2,1,0:T(8,128)(2,1)} collective-permute-done((bf16[2,576,384]{2,1,0:T(8,128)(2,1)S(1)}, bf16[2,576,384]{2,1,0:T(8,128)(2,1)}, u32[]{:S(2)}, u32[]{:S(2)}) %collective-permute-start.13) | collective-permute-done | bytes 884768 | tf_op jit(solution)/shard_map/ppermute | solution.py:20
  24.7 1.7 collective-permute-start.14
  26.4 2.6 %multiply_reduce_fusion = f32[576]{0:T(1024)S(1)} fusion(f32[6,384]{1,0:T(8,128)S(1)} %fusion.8, bf16[6]{0:T(256)(128)(2,1)S(1)} %convert_bitcast_fusion, bf16[6,384,576]{1,2,0:T(8,128)(2,1)} %param.7), kind=kLoop, calls=%fused_computation | loop fusion | flops 5307840 | bytes 2665740 | tf_op jit(solution)/shard_map/reduce_sum | solution.py:252
  30.3 14.1 %collective-permute-done.4 = s32[6]{0:T(128)S(1)} collective-permute-done((s32[6]{0:T(128)S(1)}, s32[6]{0:T(128)S(1)}, u32[]{:S(2)}, u32[]{:S(2)}) %collective-permute-start.4) | collective-permute-done | bytes 56 | tf_op jit(solution)/shard_map/ppermute | solution.py:20
  44.4 1.5 collective-permute-start.5
  46.0 3.2 %collective-permute-done.5 = s32[6]{0:T(128)S(1)} collective-permute-done((s32[6]{0:T(128)S(1)}, s32[6]{0:T(128)S(1)}, u32[]{:S(2)}, u32[]{:S(2)}) %collective-permute-start.5) | collective-permute-done | bytes 56 | tf_op jit(solution)/shard_map/ppermute | solution.py:20
  50.4 3.9 %collective-permute-done.6 = s32[6]{0:T(128)S(1)} collective-permute-done((s32[6]{0:T(128)S(1)}, s32[6]{0:T(128)S(1)}, u32[]{:S(2)}, u32[]{:S(2)}) %collective-permute-start.6) | collective-permute-done | bytes 56 | tf_op jit(solution)/shard_map/ppermute | solution.py:20
  54.3 1.6 collective-permute-start.1
  55.9 2.0 %collective-permute-done.1 = f32[576]{0:T(1024)S(1)} collective-permute-done((f32[576]{0:T(1024)S(1)}, f32[576]{0:T(1024)S(1)}, u32[]{:S(2)}, u32[]{:S(2)}) %collective-permute-start.1) | collective-permute-done | bytes 2336 | tf_op jit(solution)/shard_map/ppermute | solution.py:20
  57.9 2.3 %collective-permute-start.2 = (f32[576]{0:T(1024)S(1)}, f32[576]{0:T(1024)S(1)}, u32[]{:S(2)}, u32[]{:S(2)}) collective-permute-start(f32[576]{0:T(1024)S(1)} %add.208), channel_id=1, source_target_pairs={{0,16},{8,24},{16,0},{24,8},{1,17},{9,25},{17,1},{25,9},{2,18},{10... | collective-permute-start | bytes 6920 | tf_op jit(solution)/shard_map/ppermute | solution.py:20
  60.2 2.8 %collective-permute-done.2 = f32[576]{0:T(1024)S(1)} collective-permute-done((f32[576]{0:T(1024)S(1)}, f32[576]{0:T(1024)S(1)}, u32[]{:S(2)}, u32[]{:S(2)}) %collective-permute-start.2) | collective-permute-done | bytes 2336 | tf_op jit(solution)/shard_map/ppermute | solution.py:20
  63.0 1.7 collective-permute-start.3
  64.7 1.4 slice.69
  71.0 2.9 %collective-permute-start.10 = (bf16[1,576,384]{2,1,0:T(8,128)(2,1)}, bf16[1,576,384]{2,1,0:T(8,128)(2,1)S(1)}, u32[]{:S(2)}, u32[]{:S(2)}) collective-permute-start(bf16[1,576,384]{2,1,0:T(8,128)(2,1)} %collective-permute-done.9), channel_id=1, source_target_pairs={{0,64},{64,128},{128,192},{192,0},{1,65},{65,129},{129,193},{193,1... | collective-permute-start | bytes 1327112 | tf_op jit(solution)/shard_map/ppermute | solution.py:20
  74.0 10.3 %product.2.refs_7_ = f32[3,2,2,144,1152]{4,3,2,1,0:T(8,128)S(1)} custom-call(s32[2]{0:T(128)S(1)} %pad_add_fusion.3.refs_0_, s32[4,6]{1,0:T(4,128)S(1)} %pad_add_fusion.refs_1_, bf16[4,576,384]{2,1,0:T(8,128)(2,1)S(1)} %slice.74.refs_2_, bf16[4,576,384]{2,1,0:T(8,128)(2,1)} %collective-permute-done.11.refs_3_, ...), custom_call_target="tpu_custom_call" | custom-call | flops 5096079360 | bytes 16777216 | tf_op jit(solution)/shard_map/product/pallas_call | solution.py:207
  84.4 1.7 collective-permute-done.8.refs_4_
  86.0 7.8 %product.3 = (bf16[3,144,1152]{2,1,0:T(8,128)(2,1)}, bf16[3,144,1152]{2,1,0:T(8,128)(2,1)}, bf16[3,144,1152]{2,1,0:T(8,128)(2,1)S(1)}, bf16[3,144,1152]{2,1,0:T(8,128)(2,1)S(1)}) custom-call(s32[2]{0:T(128)S(1)} %pad_add_fusion.3.refs_0_, s32[4,6]{1,0:T(4,128)S(1)} %pad_add_fusion.refs_1_, bf16[2,576,384]{2,1,0:T(8,128)(2,1)S(1)} %slice.73.refs_2_, ...), custom_call_target="tpu_custom_call" | custom-call | flops 2548039680 | bytes 16777216 | tf_op jit(solution)/shard_map/product/pallas_call | solution.py:207
  94.4 2.4 %collective-permute-done.26 = bf16[3,144,1152]{2,1,0:T(8,128)(2,1)} collective-permute-done((bf16[3,144,1152]{2,1,0:T(8,128)(2,1)}, bf16[3,144,1152]{2,1,0:T(8,128)(2,1)}, u32[]{:S(2)}, u32[]{:S(2)}) %collective-permute-start.26) | collective-permute-done | bytes 995360 | tf_op jit(solution)/shard_map/ppermute | solution.py:20
  96.8 2.4 %fusion.7 = (bf16[144,1152]{1,0:T(8,128)(2,1)S(1)}, bf16[144,1152]{1,0:T(8,128)(2,1)S(1)}, bf16[144,1152]{1,0:T(8,128)(2,1)}, bf16[144,1152]{1,0:T(8,128)(2,1)S(1)}) fusion(bf16[3,144,1152]{2,1,0:T(8,128)(2,1)} %collective-permute-done.26, s32[]{:T(128)S(6)} %select_n.160, bf16[3,144,1152]{2,1,0:T(8,128)(2,1)S(1)} %get-tuple-element.34, s32[]{:T(128)S(6)} %select_n.158, ...), kind=kLoop, calls=%fused_computation.20 | loop fusion | flops 2820096 | bytes 3981329 | tf_op jit(solution)/shard_map/convert_element_type | solution.py:286
  99.1 1.4 collective-permute-start.27
  100.6 2.4 %fusion.3 = (bf16[144,1152]{1,0:T(8,128)(2,1)}, bf16[144,1152]{1,0:T(8,128)(2,1)S(1)}, bf16[144,1152]{1,0:T(8,128)(2,1)S(1)}, bf16[144,1152]{1,0:T(8,128)(2,1)S(1)}) fusion(bf16[3,144,1152]{2,1,0:T(8,128)(2,1)} %collective-permute-done.15, s32[]{:T(128)S(6)} %select_n.160, bf16[3,144,1152]{2,1,0:T(8,128)(2,1)S(1)} %get-tuple-element.25, s32[]{:T(128)S(6)} %select_n.158, ...), kind=kLoop, calls=%fused_computation.16 | loop fusion | flops 2820096 | bytes 3981329 | tf_op jit(solution)/shard_map/convert_element_type | solution.py:286
  103.0 3.3 %collective-permute-start.23 = (f32[576]{0:T(1024)S(1)}, f32[576]{0:T(1024)S(1)}, u32[]{:S(2)}, u32[]{:S(2)}) collective-permute-start(f32[576]{0:T(1024)S(1)} %add_add_fusion), channel_id=1, source_target_pairs={{0,2},{2,4},{4,6},{6,0},{1,3},{3,5},{5,7},{7,1},{8,10},{10,12},{12... | collective-permute-start | bytes 6920 | tf_op jit(solution)/shard_map/ppermute | solution.py:20
  106.3 4.8 %collective-permute-start.24 = (f32[576]{0:T(1024)S(1)}, f32[576]{0:T(1024)S(1)}, u32[]{:S(2)}, u32[]{:S(2)}) collective-permute-start(f32[576]{0:T(1024)S(1)} %add_add_fusion), channel_id=1, source_target_pairs={{0,4},{2,6},{4,0},{6,2},{1,5},{3,7},{5,1},{7,3},{8,12},{10,14},{12... | collective-permute-start | bytes 6920 | tf_op jit(solution)/shard_map/ppermute | solution.py:20
  111.1 2.7 %collective-permute-start.25 = (f32[576]{0:T(1024)S(1)}, f32[576]{0:T(1024)S(1)}, u32[]{:S(2)}, u32[]{:S(2)}) collective-permute-start(f32[576]{0:T(1024)S(1)} %add_add_fusion), channel_id=1, source_target_pairs={{0,6},{2,0},{4,2},{6,4},{1,7},{3,1},{5,3},{7,5},{8,14},{10,8},{12,... | collective-permute-start | bytes 6920 | tf_op jit(solution)/shard_map/ppermute | solution.py:20
  113.7 6.6 %collective-permute-start.28 = (bf16[144,1152]{1,0:T(8,128)(2,1)S(1)}, bf16[144,1152]{1,0:T(8,128)(2,1)S(1)}, u32[]{:S(2)}, u32[]{:S(2)}) collective-permute-start(bf16[144,1152]{1,0:T(8,128)(2,1)S(1)} %get-tuple-element.47), channel_id=1, source_target_pairs={{0,16},{16,0},{24,8},{64,80},{72,88},{88,72},{128,144},{136,152},{... | collective-permute-start | bytes 995336 | tf_op jit(solution)/shard_map/ppermute | solution.py:289
  120.3 1.9 collective-permute-start.29
  122.3 3.1 %collective-permute-start.18 = (bf16[144,1152]{1,0:T(8,128)(2,1)}, bf16[144,1152]{1,0:T(8,128)(2,1)S(1)}, u32[]{:S(2)}, u32[]{:S(2)}) collective-permute-start(bf16[144,1152]{1,0:T(8,128)(2,1)} %get-tuple-element.28), channel_id=1, source_target_pairs={{8,0},{16,8},{24,16},{64,88},{80,72},{88,80},{128,152},{136,128},{... | collective-permute-start | bytes 995336 | tf_op jit(solution)/shard_map/ppermute | solution.py:289
  125.4 1.3 collective-permute-start.16
  126.7 4.6 %collective-permute-start.17 = (bf16[144,1152]{1,0:T(8,128)(2,1)S(1)}, bf16[144,1152]{1,0:T(8,128)(2,1)S(1)}, u32[]{:S(2)}, u32[]{:S(2)}) collective-permute-start(bf16[144,1152]{1,0:T(8,128)(2,1)S(1)} %get-tuple-element.51), channel_id=1, source_target_pairs={{0,16},{16,0},{24,8},{64,80},{72,88},{88,72},{128,144},{136,152},{... | collective-permute-start | bytes 995336 | tf_op jit(solution)/shard_map/ppermute | solution.py:289
  132.0 9.6 %collective-permute-done.29.c_ref = bf16[144,1152]{1,0:T(8,128)(2,1)S(1)} collective-permute-done((bf16[144,1152]{1,0:T(8,128)(2,1)S(1)}, bf16[144,1152]{1,0:T(8,128)(2,1)S(1)}, u32[]{:S(2)}, u32[]{:S(2)}) %collective-permute-start.29) | collective-permute-done | bytes 331808 | tf_op jit(solution)/shard_map/ppermute | solution.py:289
  142.5 2.7 %collective-permute-start.30 = (bf16[72,576]{1,0:T(8,128)(2,1)S(1)}, bf16[72,576]{1,0:T(8,128)(2,1)S(1)}, u32[]{:S(2)}, u32[]{:S(2)}) collective-permute-start(bf16[72,576]{1,0:T(8,128)(2,1)S(1)} %get-tuple-element.37), channel_id=1, source_target_pairs={{0,0},{2,32},{4,2},{6,34},{32,4},{34,36},{36,6},{38,38},{1,1},{3,3... | collective-permute-start | bytes 248840 | tf_op jit(solution)/shard_map/ppermute | solution.py:313
  145.1 1.5 collective-permute-start.31
  146.7 2.0 collective-permute-done.18.c_ref
  148.6 2.3 %collective-permute-start.32 = (bf16[72,576]{1,0:T(8,128)(2,1)S(1)}, bf16[72,576]{1,0:T(8,128)(2,1)S(1)}, u32[]{:S(2)}, u32[]{:S(2)}) collective-permute-start(bf16[72,576]{1,0:T(8,128)(2,1)S(1)} %get-tuple-element.39), channel_id=1, source_target_pairs={{0,2},{2,34},{4,0},{6,32},{32,6},{34,38},{36,4},{38,36},{1,3},{3,3... | collective-permute-start | bytes 248840 | tf_op jit(solution)/shard_map/ppermute | solution.py:313
  151.0 1.9 collective-permute-start.33
  153.7 6.9 %collective-permute-start.19 = (bf16[72,576]{1,0:T(8,128)(2,1)S(1)}, bf16[72,576]{1,0:T(8,128)(2,1)S(1)}, u32[]{:S(2)}, u32[]{:S(2)}) collective-permute-start(bf16[72,576]{1,0:T(8,128)(2,1)S(1)} %get-tuple-element.29), channel_id=1, source_target_pairs={{0,0},{2,32},{4,2},{6,34},{32,4},{34,36},{36,6},{38,38},{1,1},{3,3... | collective-permute-start | bytes 248840 | tf_op jit(solution)/shard_map/ppermute | solution.py:313
  160.8 2.8 %collective-permute-start.21 = (bf16[72,576]{1,0:T(8,128)(2,1)S(1)}, bf16[72,576]{1,0:T(8,128)(2,1)S(1)}, u32[]{:S(2)}, u32[]{:S(2)}) collective-permute-start(bf16[72,576]{1,0:T(8,128)(2,1)S(1)} %get-tuple-element.31), channel_id=1, source_target_pairs={{0,2},{2,34},{4,0},{6,32},{32,6},{34,38},{36,4},{38,36},{1,3},{3,3... | collective-permute-start | bytes 248840 | tf_op jit(solution)/shard_map/ppermute | solution.py:313
  163.6 2.4 %collective-permute-start.22 = (bf16[72,576]{1,0:T(8,128)(2,1)S(1)}, bf16[72,576]{1,0:T(8,128)(2,1)S(1)}, u32[]{:S(2)}, u32[]{:S(2)}) collective-permute-start(bf16[72,576]{1,0:T(8,128)(2,1)S(1)} %get-tuple-element.32), channel_id=1, source_target_pairs={{0,34},{2,2},{4,32},{6,0},{32,38},{34,6},{36,36},{38,4},{1,35},{3,... | collective-permute-start | bytes 248840 | tf_op jit(solution)/shard_map/ppermute | solution.py:313
  166.1 6.0 %collective-permute-done.21.refs_2_ = bf16[72,576]{1,0:T(8,128)(2,1)S(1)} collective-permute-done((bf16[72,576]{1,0:T(8,128)(2,1)S(1)}, bf16[72,576]{1,0:T(8,128)(2,1)S(1)}, u32[]{:S(2)}, u32[]{:S(2)}) %collective-permute-start.21) | collective-permute-done | bytes 82976 | tf_op jit(solution)/shard_map/ppermute | solution.py:313
  174.3 2.0 %collective-permute-start.34 = (bf16[72,576]{1,0:T(8,128)(2,1)S(1)}, bf16[72,576]{1,0:T(8,128)(2,1)S(1)}, u32[]{:S(2)}, u32[]{:S(2)}) collective-permute-start(bf16[72,576]{1,0:T(8,128)(2,1)S(1)} %get-tuple-element.42), channel_id=1, source_target_pairs={{0,2},{2,0},{4,6},{6,4},{1,3},{3,1},{5,7},{7,5},{8,10},{10,8},{12,... | collective-permute-start | bytes 248840 | tf_op jit(solution)/shard_map/ppermute | solution.py:109
  176.4 3.4 %collective-permute-start.36 = (bf16[144,576]{1,0:T(8,128)(2,1)S(1)}, bf16[144,576]{1,0:T(8,128)(2,1)S(1)}, u32[]{:S(2)}, u32[]{:S(2)}) collective-permute-start(bf16[144,576]{1,0:T(8,128)(2,1)S(1)} %shard_map.89), channel_id=1, source_target_pairs={{8,64},{10,66},{12,96},{14,98},{40,68},{42,70},{44,100},{46,102},{... | collective-permute-start | bytes 497672 | tf_op jit(solution)/shard_map/ppermute | solution.py:344
  180.9 15.8 %collective-permute-done.36.mirror_ref = bf16[144,576]{1,0:T(8,128)(2,1)S(1)} collective-permute-done((bf16[144,576]{1,0:T(8,128)(2,1)S(1)}, bf16[144,576]{1,0:T(8,128)(2,1)S(1)}, u32[]{:S(2)}, u32[]{:S(2)}) %collective-permute-start.36) | collective-permute-done | bytes 165920 | tf_op jit(solution)/shard_map/ppermute | solution.py:344
  196.8 1.8 shard_map.90
  (77 shorter events, 14.9 us)
Async XLA Ops:
  1.9 7.5 %copy-start = (f32[6,9,128]{2,0,1:T(8,128)S(1)}, f32[6,9,128]{2,0,1:T(8,128)}, u32[]{:S(2)}) copy-start(f32[6,9,128]{2,0,1:T(8,128)} %param.9) | copy-start | bytes 82948
  1.9 7.5 %copy-start.1 = (f32[6,384]{1,0:T(8,128)S(1)}, f32[6,384]{1,0:T(8,128)}, u32[]{:S(2)}) copy-start(f32[6,384]{1,0:T(8,128)} %param.13) | copy-start | bytes 27652
  1.9 24.4 %copy-start.6 = (s32[6,1]{0,1:T(1,128)S(1)}, s32[6,1]{0,1:T(1,128)}, u32[]{:S(2)}) copy-start(s32[6,1]{0,1:T(1,128)} %param.8) | copy-start | bytes 76
  2.0 22.7 %collective-permute-start.13 = (bf16[2,576,384]{2,1,0:T(8,128)(2,1)S(1)}, bf16[2,576,384]{2,1,0:T(8,128)(2,1)}, u32[]{:S(2)}, u32[]{:S(2)}) collective-permute-start(bf16[2,576,384]{2,1,0:T(8,128)(2,1)S(1)} %dynamic-slice_bitcast_fusion), channel_id=1, source_target_pairs={{0,64},{64,128},{128,192},{192,0},{1,65},{65,129},{129,193},{193,1... | collective-permute-start | bytes 2654216 | tf_op jit(solution)/shard_map/ppermute | solution.py:20
  4.2 69.8 %collective-permute-start.11 = (bf16[4,576,384]{2,1,0:T(8,128)(2,1)S(1)}, bf16[4,576,384]{2,1,0:T(8,128)(2,1)}, u32[]{:S(2)}, u32[]{:S(2)}) collective-permute-start(bf16[4,576,384]{2,1,0:T(8,128)(2,1)S(1)} %slice.74.refs_2_), channel_id=1, source_target_pairs={{0,32},{32,0},{1,33},{33,1},{2,34},{34,2},{3,35},{35,3},{4,36},{36... | collective-permute-start | bytes 5308424 | tf_op jit(solution)/shard_map/ppermute | solution.py:20
  4.4 69.6 %collective-permute-start.12 = (bf16[4,576,384]{2,1,0:T(8,128)(2,1)S(1)}, bf16[4,576,384]{2,1,0:T(8,128)(2,1)}, u32[]{:S(2)}, u32[]{:S(2)}) collective-permute-start(bf16[4,576,384]{2,1,0:T(8,128)(2,1)S(1)} %slice.74.refs_2_), channel_id=1, source_target_pairs={{0,192},{64,0},{128,64},{192,128},{1,193},{65,1},{129,65},{193,129... | collective-permute-start | bytes 5308424 | tf_op jit(solution)/shard_map/ppermute | solution.py:20
  7.7 61.5 %collective-permute-start.9 = (bf16[1,576,384]{2,1,0:T(8,128)(2,1)}, bf16[1,576,384]{2,1,0:T(8,128)(2,1)}, u32[]{:S(2)}, u32[]{:S(2)}) collective-permute-start(bf16[1,576,384]{2,1,0:T(8,128)(2,1)} %dynamic-slice_bitcast_fusion.1), channel_id=1, source_target_pairs={{0,64},{64,128},{128,192},{192,0},{1,65},{65,129},{129,193},{193,1... | collective-permute-start | bytes 1327112 | tf_op jit(solution)/shard_map/ppermute | solution.py:20
  24.7 46.4 %collective-permute-start.14 = (bf16[2,576,384]{2,1,0:T(8,128)(2,1)}, bf16[2,576,384]{2,1,0:T(8,128)(2,1)S(1)}, u32[]{:S(2)}, u32[]{:S(2)}) collective-permute-start(bf16[2,576,384]{2,1,0:T(8,128)(2,1)} %collective-permute-done.13), channel_id=1, source_target_pairs={{0,64},{64,128},{128,192},{192,0},{1,65},{65,129},{129,193},{193,1... | collective-permute-start | bytes 2654216 | tf_op jit(solution)/shard_map/ppermute | solution.py:20
  29.0 1.2 collective-permute-start
  30.2 14.2 %collective-permute-start.4 = (s32[6]{0:T(128)S(1)}, s32[6]{0:T(128)S(1)}, u32[]{:S(2)}, u32[]{:S(2)}) collective-permute-start(s32[6]{0:T(128)S(1)} %bitcast.46), channel_id=1, source_target_pairs={{0,32},{32,0},{1,33},{33,1},{2,34},{34,2},{3,35},{35,3},{4,36},{36... | collective-permute-start | bytes 80 | tf_op jit(solution)/shard_map/ppermute | solution.py:20
  44.4 21.6 %copy-start.7 = (s32[6]{0:T(128)}, s32[6]{0:T(128)S(1)}, u32[]{:S(2)}) copy-start(s32[6]{0:T(128)S(1)} %collective-permute-done.4) | copy-start | bytes 76
  44.4 4.8 %collective-permute-start.5 = (s32[6]{0:T(128)S(1)}, s32[6]{0:T(128)S(1)}, u32[]{:S(2)}, u32[]{:S(2)}) collective-permute-start(s32[6]{0:T(128)S(1)} %bitcast.47), channel_id=1, source_target_pairs={{0,192},{64,0},{128,64},{192,128},{1,193},{65,1},{129,65},{193,129... | collective-permute-start | bytes 80 | tf_op jit(solution)/shard_map/ppermute | solution.py:20
  49.2 1.2 copy-start.8
  49.2 5.1 %collective-permute-start.6 = (s32[6]{0:T(128)S(1)}, s32[6]{0:T(128)S(1)}, u32[]{:S(2)}, u32[]{:S(2)}) collective-permute-start(s32[6]{0:T(128)S(1)} %bitcast.48), channel_id=1, source_target_pairs={{0,128},{64,192},{128,0},{192,64},{1,129},{65,193},{129,1},{193,65... | collective-permute-start | bytes 80 | tf_op jit(solution)/shard_map/ppermute | solution.py:20
  54.3 8.7 %copy-start.9 = (s32[6]{0:T(128)}, s32[6]{0:T(128)S(1)}, u32[]{:S(2)}) copy-start(s32[6]{0:T(128)S(1)} %collective-permute-done.6) | copy-start | bytes 76
  54.3 3.6 %collective-permute-start.1 = (f32[576]{0:T(1024)S(1)}, f32[576]{0:T(1024)S(1)}, u32[]{:S(2)}, u32[]{:S(2)}) collective-permute-start(f32[576]{0:T(1024)S(1)} %add.208), channel_id=1, source_target_pairs={{0,8},{8,16},{16,24},{24,0},{1,9},{9,17},{17,25},{25,1},{2,10},{10... | collective-permute-start | bytes 6920 | tf_op jit(solution)/shard_map/ppermute | solution.py:20
  57.9 8.2 %copy-start.2 = (f32[576]{0:T(1024)}, f32[576]{0:T(1024)S(1)}, u32[]{:S(2)}) copy-start(f32[576]{0:T(1024)S(1)} %collective-permute-done.1) | copy-start | bytes 6916
  57.9 5.1 %collective-permute-start.2 = (f32[576]{0:T(1024)S(1)}, f32[576]{0:T(1024)S(1)}, u32[]{:S(2)}, u32[]{:S(2)}) collective-permute-start(f32[576]{0:T(1024)S(1)} %add.208), channel_id=1, source_target_pairs={{0,16},{8,24},{16,0},{24,8},{1,17},{9,25},{17,1},{25,9},{2,18},{10... | collective-permute-start | bytes 6920 | tf_op jit(solution)/shard_map/ppermute | solution.py:20
  63.0 3.0 %copy-start.3 = (f32[576]{0:T(1024)}, f32[576]{0:T(1024)S(1)}, u32[]{:S(2)}) copy-start(f32[576]{0:T(1024)S(1)} %collective-permute-done.2) | copy-start | bytes 6916
  63.0 5.8 %collective-permute-start.3 = (f32[576]{0:T(1024)S(1)}, f32[576]{0:T(1024)}, u32[]{:S(2)}, u32[]{:S(2)}) collective-permute-start(f32[576]{0:T(1024)S(1)} %add.208), channel_id=1, source_target_pairs={{0,24},{8,0},{16,8},{24,16},{1,25},{9,1},{17,9},{25,17},{2,26},{10... | collective-permute-start | bytes 6920 | tf_op jit(solution)/shard_map/ppermute | solution.py:20
  68.8 15.5 %collective-permute-start.7 = (bf16[2,576,384]{2,1,0:T(8,128)(2,1)S(1)}, bf16[2,576,384]{2,1,0:T(8,128)(2,1)S(1)}, u32[]{:S(2)}, u32[]{:S(2)}) collective-permute-start(bf16[2,576,384]{2,1,0:T(8,128)(2,1)S(1)} %slice.73.refs_2_), channel_id=1, source_target_pairs={{0,32},{32,0},{1,33},{33,1},{2,34},{34,2},{3,35},{35,3},{4,36},{36... | collective-permute-start | bytes 2654216 | tf_op jit(solution)/shard_map/ppermute | solution.py:20
  69.2 16.8 %collective-permute-start.8 = (bf16[2,576,384]{2,1,0:T(8,128)(2,1)S(1)}, bf16[2,576,384]{2,1,0:T(8,128)(2,1)S(1)}, u32[]{:S(2)}, u32[]{:S(2)}) collective-permute-start(bf16[2,576,384]{2,1,0:T(8,128)(2,1)S(1)} %slice.73.refs_2_), channel_id=1, source_target_pairs={{0,192},{64,0},{128,64},{192,128},{1,193},{65,1},{129,65},{193,129... | collective-permute-start | bytes 2654216 | tf_op jit(solution)/shard_map/ppermute | solution.py:20
  71.0 13.2 %collective-permute-start.10 = (bf16[1,576,384]{2,1,0:T(8,128)(2,1)}, bf16[1,576,384]{2,1,0:T(8,128)(2,1)S(1)}, u32[]{:S(2)}, u32[]{:S(2)}) collective-permute-start(bf16[1,576,384]{2,1,0:T(8,128)(2,1)} %collective-permute-done.9), channel_id=1, source_target_pairs={{0,64},{64,128},{128,192},{192,0},{1,65},{65,129},{129,193},{193,1... | collective-permute-start | bytes 1327112 | tf_op jit(solution)/shard_map/ppermute | solution.py:20
  93.8 2.9 %collective-permute-start.26 = (bf16[3,144,1152]{2,1,0:T(8,128)(2,1)}, bf16[3,144,1152]{2,1,0:T(8,128)(2,1)}, u32[]{:S(2)}, u32[]{:S(2)}) collective-permute-start(bf16[3,144,1152]{2,1,0:T(8,128)(2,1)} %get-tuple-element.35), channel_id=1, source_target_pairs={{0,1},{1,0},{2,3},{3,2},{4,5},{5,4},{6,7},{7,6},{8,9},{9,8},{10,11... | collective-permute-start | bytes 2985992 | tf_op jit(solution)/shard_map/ppermute | solution.py:20
  93.8 6.8 %collective-permute-start.15 = (bf16[3,144,1152]{2,1,0:T(8,128)(2,1)}, bf16[3,144,1152]{2,1,0:T(8,128)(2,1)}, u32[]{:S(2)}, u32[]{:S(2)}) collective-permute-start(bf16[3,144,1152]{2,1,0:T(8,128)(2,1)} %get-tuple-element.26), channel_id=1, source_target_pairs={{0,1},{1,0},{2,3},{3,2},{4,5},{5,4},{6,7},{7,6},{8,9},{9,8},{10,11... | collective-permute-start | bytes 2985992 | tf_op jit(solution)/shard_map/ppermute | solution.py:20
  99.1 32.2 %copy-start.5 = (f32[576]{0:T(1024)S(1)}, f32[576]{0:T(1024)}, u32[]{:S(2)}) copy-start(f32[576]{0:T(1024)} %param.12) | copy-start | bytes 6916
  99.1 27.5 %collective-permute-start.27 = (bf16[144,1152]{1,0:T(8,128)(2,1)}, bf16[144,1152]{1,0:T(8,128)(2,1)S(1)}, u32[]{:S(2)}, u32[]{:S(2)}) collective-permute-start(bf16[144,1152]{1,0:T(8,128)(2,1)} %get-tuple-element.48), channel_id=1, source_target_pairs={{0,8},{8,16},{24,0},{64,72},{72,80},{80,88},{136,144},{144,152},{1... | collective-permute-start | bytes 995336 | tf_op jit(solution)/shard_map/ppermute | solution.py:289
  103.0 71.1 %copy-start.4 = (s32[576]{0:T(1024)S(1)}, s32[576]{0:T(1024)}, u32[]{:S(2)}) copy-start(s32[576]{0:T(1024)} %param.11) | copy-start | bytes 6916
  103.0 17.3 %collective-permute-start.23 = (f32[576]{0:T(1024)S(1)}, f32[576]{0:T(1024)S(1)}, u32[]{:S(2)}, u32[]{:S(2)}) collective-permute-start(f32[576]{0:T(1024)S(1)} %add_add_fusion), channel_id=1, source_target_pairs={{0,2},{2,4},{4,6},{6,0},{1,3},{3,5},{5,7},{7,1},{8,10},{10,12},{12... | collective-permute-start | bytes 6920 | tf_op jit(solution)/shard_map/ppermute | solution.py:20
  106.3 16.0 %collective-permute-start.24 = (f32[576]{0:T(1024)S(1)}, f32[576]{0:T(1024)S(1)}, u32[]{:S(2)}, u32[]{:S(2)}) collective-permute-start(f32[576]{0:T(1024)S(1)} %add_add_fusion), channel_id=1, source_target_pairs={{0,4},{2,6},{4,0},{6,2},{1,5},{3,7},{5,1},{7,3},{8,12},{10,14},{12... | collective-permute-start | bytes 6920 | tf_op jit(solution)/shard_map/ppermute | solution.py:20
  111.1 14.3 %collective-permute-start.25 = (f32[576]{0:T(1024)S(1)}, f32[576]{0:T(1024)S(1)}, u32[]{:S(2)}, u32[]{:S(2)}) collective-permute-start(f32[576]{0:T(1024)S(1)} %add_add_fusion), channel_id=1, source_target_pairs={{0,6},{2,0},{4,2},{6,4},{1,7},{3,1},{5,3},{7,5},{8,14},{10,8},{12,... | collective-permute-start | bytes 6920 | tf_op jit(solution)/shard_map/ppermute | solution.py:20
  113.7 18.2 %collective-permute-start.28 = (bf16[144,1152]{1,0:T(8,128)(2,1)S(1)}, bf16[144,1152]{1,0:T(8,128)(2,1)S(1)}, u32[]{:S(2)}, u32[]{:S(2)}) collective-permute-start(bf16[144,1152]{1,0:T(8,128)(2,1)S(1)} %get-tuple-element.47), channel_id=1, source_target_pairs={{0,16},{16,0},{24,8},{64,80},{72,88},{88,72},{128,144},{136,152},{... | collective-permute-start | bytes 995336 | tf_op jit(solution)/shard_map/ppermute | solution.py:289
  120.3 21.3 %collective-permute-start.29 = (bf16[144,1152]{1,0:T(8,128)(2,1)S(1)}, bf16[144,1152]{1,0:T(8,128)(2,1)S(1)}, u32[]{:S(2)}, u32[]{:S(2)}) collective-permute-start(bf16[144,1152]{1,0:T(8,128)(2,1)S(1)} %get-tuple-element.46), channel_id=1, source_target_pairs={{8,0},{16,8},{24,16},{64,88},{80,72},{88,80},{128,152},{136,128},{... | collective-permute-start | bytes 995336 | tf_op jit(solution)/shard_map/ppermute | solution.py:289
  122.3 26.3 %collective-permute-start.18 = (bf16[144,1152]{1,0:T(8,128)(2,1)}, bf16[144,1152]{1,0:T(8,128)(2,1)S(1)}, u32[]{:S(2)}, u32[]{:S(2)}) collective-permute-start(bf16[144,1152]{1,0:T(8,128)(2,1)} %get-tuple-element.28), channel_id=1, source_target_pairs={{8,0},{16,8},{24,16},{64,88},{80,72},{88,80},{128,152},{136,128},{... | collective-permute-start | bytes 995336 | tf_op jit(solution)/shard_map/ppermute | solution.py:289
  125.4 25.6 %collective-permute-start.16 = (bf16[144,1152]{1,0:T(8,128)(2,1)S(1)}, bf16[144,1152]{1,0:T(8,128)(2,1)S(1)}, u32[]{:S(2)}, u32[]{:S(2)}) collective-permute-start(bf16[144,1152]{1,0:T(8,128)(2,1)S(1)} %get-tuple-element.52), channel_id=1, source_target_pairs={{0,8},{8,16},{24,0},{64,72},{72,80},{80,88},{136,144},{144,152},{1... | collective-permute-start | bytes 995336 | tf_op jit(solution)/shard_map/ppermute | solution.py:289
  126.7 26.2 %collective-permute-start.17 = (bf16[144,1152]{1,0:T(8,128)(2,1)S(1)}, bf16[144,1152]{1,0:T(8,128)(2,1)S(1)}, u32[]{:S(2)}, u32[]{:S(2)}) collective-permute-start(bf16[144,1152]{1,0:T(8,128)(2,1)S(1)} %get-tuple-element.51), channel_id=1, source_target_pairs={{0,16},{16,0},{24,8},{64,80},{72,88},{88,72},{128,144},{136,152},{... | collective-permute-start | bytes 995336 | tf_op jit(solution)/shard_map/ppermute | solution.py:289
  142.5 18.2 %collective-permute-start.30 = (bf16[72,576]{1,0:T(8,128)(2,1)S(1)}, bf16[72,576]{1,0:T(8,128)(2,1)S(1)}, u32[]{:S(2)}, u32[]{:S(2)}) collective-permute-start(bf16[72,576]{1,0:T(8,128)(2,1)S(1)} %get-tuple-element.37), channel_id=1, source_target_pairs={{0,0},{2,32},{4,2},{6,34},{32,4},{34,36},{36,6},{38,38},{1,1},{3,3... | collective-permute-start | bytes 248840 | tf_op jit(solution)/shard_map/ppermute | solution.py:313
  145.1 15.6 %collective-permute-start.31 = (bf16[72,576]{1,0:T(8,128)(2,1)S(1)}, bf16[72,576]{1,0:T(8,128)(2,1)S(1)}, u32[]{:S(2)}, u32[]{:S(2)}) collective-permute-start(bf16[72,576]{1,0:T(8,128)(2,1)S(1)} %get-tuple-element.38), channel_id=1, source_target_pairs={{0,32},{2,0},{4,34},{6,2},{32,36},{34,4},{36,38},{38,6},{1,33},{3,... | collective-permute-start | bytes 248840 | tf_op jit(solution)/shard_map/ppermute | solution.py:313
  148.6 15.0 %collective-permute-start.32 = (bf16[72,576]{1,0:T(8,128)(2,1)S(1)}, bf16[72,576]{1,0:T(8,128)(2,1)S(1)}, u32[]{:S(2)}, u32[]{:S(2)}) collective-permute-start(bf16[72,576]{1,0:T(8,128)(2,1)S(1)} %get-tuple-element.39), channel_id=1, source_target_pairs={{0,2},{2,34},{4,0},{6,32},{32,6},{34,38},{36,4},{38,36},{1,3},{3,3... | collective-permute-start | bytes 248840 | tf_op jit(solution)/shard_map/ppermute | solution.py:313
  151.0 15.1 %collective-permute-start.33 = (bf16[72,576]{1,0:T(8,128)(2,1)S(1)}, bf16[72,576]{1,0:T(8,128)(2,1)S(1)}, u32[]{:S(2)}, u32[]{:S(2)}) collective-permute-start(bf16[72,576]{1,0:T(8,128)(2,1)S(1)} %get-tuple-element.40), channel_id=1, source_target_pairs={{0,34},{2,2},{4,32},{6,0},{32,38},{34,6},{36,36},{38,4},{1,35},{3,... | collective-permute-start | bytes 248840 | tf_op jit(solution)/shard_map/ppermute | solution.py:313
  153.7 12.3 %collective-permute-start.19 = (bf16[72,576]{1,0:T(8,128)(2,1)S(1)}, bf16[72,576]{1,0:T(8,128)(2,1)S(1)}, u32[]{:S(2)}, u32[]{:S(2)}) collective-permute-start(bf16[72,576]{1,0:T(8,128)(2,1)S(1)} %get-tuple-element.29), channel_id=1, source_target_pairs={{0,0},{2,32},{4,2},{6,34},{32,4},{34,36},{36,6},{38,38},{1,1},{3,3... | collective-permute-start | bytes 248840 | tf_op jit(solution)/shard_map/ppermute | solution.py:313
  160.7 5.4 %collective-permute-start.20 = (bf16[72,576]{1,0:T(8,128)(2,1)S(1)}, bf16[72,576]{1,0:T(8,128)(2,1)S(1)}, u32[]{:S(2)}, u32[]{:S(2)}) collective-permute-start(bf16[72,576]{1,0:T(8,128)(2,1)S(1)} %get-tuple-element.30), channel_id=1, source_target_pairs={{0,32},{2,0},{4,34},{6,2},{32,36},{34,4},{36,38},{38,6},{1,33},{3,... | collective-permute-start | bytes 248840 | tf_op jit(solution)/shard_map/ppermute | solution.py:313
  160.8 11.3 %collective-permute-start.21 = (bf16[72,576]{1,0:T(8,128)(2,1)S(1)}, bf16[72,576]{1,0:T(8,128)(2,1)S(1)}, u32[]{:S(2)}, u32[]{:S(2)}) collective-permute-start(bf16[72,576]{1,0:T(8,128)(2,1)S(1)} %get-tuple-element.31), channel_id=1, source_target_pairs={{0,2},{2,34},{4,0},{6,32},{32,6},{34,38},{36,4},{38,36},{1,3},{3,3... | collective-permute-start | bytes 248840 | tf_op jit(solution)/shard_map/ppermute | solution.py:313
  163.6 9.4 %collective-permute-start.22 = (bf16[72,576]{1,0:T(8,128)(2,1)S(1)}, bf16[72,576]{1,0:T(8,128)(2,1)S(1)}, u32[]{:S(2)}, u32[]{:S(2)}) collective-permute-start(bf16[72,576]{1,0:T(8,128)(2,1)S(1)} %get-tuple-element.32), channel_id=1, source_target_pairs={{0,34},{2,2},{4,32},{6,0},{32,38},{34,6},{36,36},{38,4},{1,35},{3,... | collective-permute-start | bytes 248840 | tf_op jit(solution)/shard_map/ppermute | solution.py:313
  174.0 2.2 %collective-permute-start.35 = (bf16[2,144,144]{2,1,0:T(8,128)(2,1)S(1)}, bf16[2,144,144]{2,1,0:T(8,128)(2,1)S(1)}, u32[]{:S(2)}, u32[]{:S(2)}) collective-permute-start(bf16[2,144,144]{2,1,0:T(8,128)(2,1)S(1)} %get-tuple-element.44), channel_id=1, source_target_pairs={{0,1},{1,0},{2,3},{3,2},{4,5},{5,4},{6,7},{7,6},{8,9},{9,8},{10,11... | collective-permute-start | bytes 248840 | tf_op jit(solution)/shard_map/ppermute | solution.py:20
  174.3 6.7 %collective-permute-start.34 = (bf16[72,576]{1,0:T(8,128)(2,1)S(1)}, bf16[72,576]{1,0:T(8,128)(2,1)S(1)}, u32[]{:S(2)}, u32[]{:S(2)}) collective-permute-start(bf16[72,576]{1,0:T(8,128)(2,1)S(1)} %get-tuple-element.42), channel_id=1, source_target_pairs={{0,2},{2,0},{4,6},{6,4},{1,3},{3,1},{5,7},{7,5},{8,10},{10,8},{12,... | collective-permute-start | bytes 248840 | tf_op jit(solution)/shard_map/ppermute | solution.py:109
  176.4 20.4 %collective-permute-start.36 = (bf16[144,576]{1,0:T(8,128)(2,1)S(1)}, bf16[144,576]{1,0:T(8,128)(2,1)S(1)}, u32[]{:S(2)}, u32[]{:S(2)}) collective-permute-start(bf16[144,576]{1,0:T(8,128)(2,1)S(1)} %shard_map.89), channel_id=1, source_target_pairs={{8,64},{10,66},{12,96},{14,98},{40,68},{42,70},{44,100},{46,102},{... | collective-permute-start | bytes 497672 | tf_op jit(solution)/shard_map/ppermute | solution.py:344

commit v4 on v3

--- a/solution.py
+++ b/solution.py
@@ -7,6 +7,7 @@
 from jax.experimental.pallas import tpu as pltpu
 from jax.sharding import Mesh
 from jax.sharding import PartitionSpec as P
+
 
 X, L, Y, H, C = 4, 2, 4, 4, 2
 BLK = ("x", "l")
@@ -34,32 +35,43 @@
     )(jnp.stack(scalars).astype(jnp.int32), *operands)
 
 
-def pieces_kernel(which_ref, own_ref, a_ref, b_ref, c_ref, *rest):
-    outs, cut_ref = rest[:4], rest[4]
-    quarter, width = own_ref.shape
+def pieces_kernel(which_ref, *refs):
+    halves, terms_ref, outs, cut_ref = (refs[:4], refs[4:8]), refs[8], refs[9:13], refs[13]
+    quarter, width = halves[0][0].shape
     half, rows = width // 4, quarter // 2
-    total = own_ref[...].astype(F32) + a_ref[...].astype(F32)
-    total = total + b_ref[...].astype(F32) + c_ref[...].astype(F32)
-    for n in range(4):
+    for i, parts in enumerate(halves):
+        total = parts[0][...].astype(F32) + parts[1][...].astype(F32)
+        total = total + parts[2][...].astype(F32) + parts[3][...].astype(F32)
+        for n in range(4):
+            for p in range(2):
+                cut_ref[n, i * rows : (i + 1) * rows, p * half : (p + 1) * half] = total[
+                    p * rows : (p + 1) * rows, n * half : (n + 1) * half
+                ]
+    for m in range(4):
+        outs[m][:quarter] = cut_ref[which_ref[m]].astype(BF16)
+        more = outs[m].shape[0] - quarter
+        term = terms_ref[pl.ds(which_ref[4 + m], 1), :]
+        high = term.astype(BF16).astype(F32)
+        row = lax.broadcasted_iota(jnp.int32, (more, width // 2), 0)
+        both = jnp.where(row == 0, high, jnp.where(row == 1, term - high, 0.0))
+        outs[m][quarter:] = both.astype(BF16)
+
+
+def turn_kernel(which_ref, *refs):
+    ins = refs[:4]
+    kept_ref, swap_ref, turned_keep_ref, turned_send_ref, terms_ref = refs[4:9]
+    wide_ref, turned_ref = refs[9:]
+    quarter, half = kept_ref.shape
+    rows = quarter // 2
+    odd, core = which_ref[0], which_ref[1]
+    total = ins[0][...].astype(F32) + ins[1][...].astype(F32)
+    total = total + ins[2][...].astype(F32) + ins[3][...].astype(F32)
+    for i in range(2):
         for p in range(2):
-            cut_ref[n, :, p * half : (p + 1) * half] = total[
-                p * rows : (p + 1) * rows, n * half : (n + 1) * half
+            wide_ref[i, p * rows : (p + 1) * rows, :] = total[
+                i * rows : (i + 1) * rows, p * half : (p + 1) * half
             ]
-    for m in range(4):
-        outs[m][...] = cut_ref[which_ref[m]].astype(BF16)
-
-
-def turn_kernel(which_ref, *refs):
-    ins = refs[:8]
-    kept_ref, swap_ref, turned_keep_ref, turned_send_ref, wide_ref, turned_ref = refs[8:]
-    rows, width = ins[0].shape
-    half, quarter = width // 2, 2 * rows
-    odd, core = which_ref[0], which_ref[1]
-    for i in range(2):
-        total = ins[4 * i][...].astype(F32) + ins[4 * i + 1][...].astype(F32)
-        total = total + ins[4 * i + 2][...].astype(F32) + ins[4 * i + 3][...].astype(F32)
-        for p in range(2):
-            wide_ref[i, p * rows : (p + 1) * rows, :] = total[:, p * half : (p + 1) * half]
+    terms_ref[...] = total[quarter:]
     kept_ref[...] = wide_ref[odd]
     other = wide_ref[1 - odd].astype(BF16)
     for p in range(2):
@@ -125,15 +137,24 @@
     if not first:
         before_ref, refs = refs[0], refs[1:]
     if last:
-        sends, keeps, (left_ref, scaled_ref, sums_ref) = refs[:2], refs[2:4], refs[4:]
+        sends, keeps, refs = refs[:2], refs[2:4], refs[4:]
+        sums_ref, refs = refs[-1], refs[:-1]
     else:
-        sums_ref, left_ref, scaled_ref = refs
+        sums_ref, refs = refs[0], refs[1:]
+    left_ref, scaled_ref, mate_here, next_here, arrived = refs
+    loads = [
+        pltpu.make_async_copy(mate_ref, mate_here, arrived.at[0]),
+        pltpu.make_async_copy(next_ref, next_here, arrived.at[1]),
+    ]
+    for load in loads:
+        load.start()
     blocks, width, rows = own_ref.shape
     points = inv_ref.shape[2]
     fars = far_ref.shape[0]
     core, upper = where_ref[0], where_ref[1]
-    for block in range(blocks):
-        for side, ref in enumerate((own_ref, mate_ref)):
+
+    def scale(side, ref):
+        for block in range(blocks):
             seen = seen_ref[side, at + block].astype(F32)
             parts = [
                 ref[block, :, c * points : (c + 1) * points].astype(F32) for c in range(3)
@@ -146,14 +167,19 @@
                 scaled_ref[side * width : (side + 1) * width, to : to + points] = (
                     total.astype(BF16)
                 )
-        columns = slice(block * rows, (block + 1) * rows)
-        for kind, ref in enumerate((own_ref, next_ref)):
-            seen = seen_ref[2 * kind, at + block].astype(F32).astype(BF16)
-            left_ref[kind, :, columns] = ref[block] * seen
-    for block in range(fars):
-        columns = slice(block * rows, (block + 1) * rows)
-        seen = seen_ref[3, at + upper * fars + block].astype(F32).astype(BF16)
-        left_ref[2, :, columns] = far_ref[block] * seen
+
+    def place(kind, ref, row, shift):
+        for block in range(ref.shape[0]):
+            seen = seen_ref[row, at + shift + block].astype(F32).astype(BF16)
+            left_ref[kind, :, block * rows : (block + 1) * rows] = ref[block] * seen
+
+    scale(0, own_ref)
+    place(0, own_ref, 0, 0)
+    place(2, far_ref, 3, upper * fars)
+    loads[0].wait()
+    scale(1, mate_here)
+    loads[1].wait()
+    place(1, next_here, 2, 0)
     half_start = pl.multiple_of(upper * (fars * rows), rows)
     for start in range(0, 2 * width, 256):
         stop = min(start + 256, 2 * width)
@@ -170,15 +196,14 @@
             ).reshape(2, 2, width // 4, stop - start)
             if not first:
                 term = term + before_ref[kind, :, :, :, columns]
-            sums_ref[kind, :, :, :, columns] = term
             if last:
+                wide = stop - start
+                sums_ref[:, :, :, :wide] = term
                 for i in range(2):
-                    sends[i][kind, :, columns] = sums_ref[
-                        kind, i, 1 - core, :, columns
-                    ].astype(BF16)
-                    keeps[i][kind, :, columns] = sums_ref[
-                        kind, i, core, :, columns
-                    ].astype(BF16)
+                    sends[i][kind, :, columns] = sums_ref[i, 1 - core, :, :wide].astype(BF16)
+                    keeps[i][kind, :, columns] = sums_ref[i, core, :, :wide].astype(BF16)
+            else:
+                sums_ref[kind, :, :, :, columns] = term
 
 
 def product(first, last, at, where, seen, own, mate, following, far, inverse, before=None):
@@ -190,16 +215,20 @@
     scratch = [
         pltpu.VMEM((3, width, blocks * rows), BF16),
         pltpu.VMEM((2 * width, blocks * rows), BF16),
+        pltpu.VMEM(own.shape, BF16),
+        pltpu.VMEM(own.shape, BF16),
+        pltpu.SemaphoreType.DMA((2,)),
     ]
     if last:
         out_shape = [jax.ShapeDtypeStruct(half, BF16)] * 4
         out_specs = [vmem] * 4
-        scratch.append(pltpu.VMEM(sums, F32))
+        scratch.append(pltpu.VMEM((2, 2, width // 4, 256), F32))
     else:
         out_shape = jax.ShapeDtypeStruct(sums, F32)
         out_specs = vmem
     operands = [where, seen, own, mate, following, far, inverse]
-    specs = [smem, smem] + [vmem] * 5
+    specs = [smem, smem, vmem, pl.BlockSpec(memory_space=pltpu.HBM)]
+    specs += [pl.BlockSpec(memory_space=pltpu.HBM), vmem, vmem]
     if not first:
         operands.append(before)
         specs.append(vmem)
@@ -210,7 +239,7 @@
         in_specs=specs,
         out_specs=out_specs,
         scratch_shapes=scratch,
-        compiler_params=pltpu.CompilerParams(vmem_limit_bytes=34 * 2**20),
+        compiler_params=pltpu.CompilerParams(vmem_limit_bytes=(18 if last else 28) * 2**20),
         cost_estimate=pl.CostEstimate(
             flops=flops, bytes_accessed=16 * 2**20, transcendentals=0
         ),
@@ -261,6 +290,9 @@
             n == 0, n == len(CHUNKS) - 1, chunk[0], where, seen, *chunk[1:], before=sums
         )
     sends, keeps = sums[:2], list(sums[2:])
+    terms, keeps[0] = lax.optimization_barrier((terms, keeps[0]))
+    across = rotate(terms, "l", L, 1)
+    terms = jnp.stack([jnp.where(l == 0, terms, across), jnp.where(l == 0, across, terms)])
     others = []
     for i in range(2):
         others.append(rotate(sends[i], "c", C, 1))
@@ -284,48 +316,43 @@
                 if (b + k - a) % Y < 3
             ]
             piece = of_kind((y + k - x) % Y).astype(BF16)
-            if i == 0 and k == Y - 1:
-                terms, piece = lax.optimization_barrier((terms, piece))
             parts.append(lax.ppermute(piece, ("x", "y"), pairs))
         held.append(parts)
-    terms = terms + sum(rotate(terms, "h", H, k) for k in range(1, H))
-    reduced_rhs = camera_grad - terms
-    reduced_rhs, held[1][0] = lax.optimization_barrier((reduced_rhs, held[1][0]))
-
     quarter = width // 4
     picked = [h ^ m for m in range(4)]
     piece_shape = jax.ShapeDtypeStruct((quarter // 2, width), BF16)
+    pieces = small_call(
+        pieces_kernel,
+        [jax.ShapeDtypeStruct((quarter + 8, width), BF16)] * 4,
+        [((p % 2) ^ l) * 2 + p // 2 for p in picked] + [p % 2 for p in picked],
+        held[0] + held[1] + [terms],
+        [pltpu.VMEM((4, quarter, width), F32)],
+    )
     came = []
-    for i in range(2):
-        pieces = small_call(
-            pieces_kernel,
-            [piece_shape] * 4,
-            [((p % 2) ^ l) * 2 + p // 2 for p in picked],
-            held[i],
-            [pltpu.VMEM((4, quarter // 2, width), F32)],
-        )
-        for m in range(4):
-            pairs = [
-                (a * H + b, ((b ^ m) & 1) * H + 2 * a + ((b ^ m) >> 1))
-                for a in range(L)
-                for b in range(H)
-            ]
-            came.append(lax.ppermute(pieces[m], ("l", "h"), pairs))
+    for m in range(4):
+        pairs = [
+            (a * H + b, ((b ^ m) & 1) * H + 2 * a + ((b ^ m) >> 1))
+            for a in range(L)
+            for b in range(H)
+        ]
+        came.append(lax.ppermute(pieces[m], ("l", "h"), pairs))
 
     half_shape = (quarter, width // 2)
     tile_shape = jax.ShapeDtypeStruct((2, quarter, quarter), BF16)
-    kept, swap, turned_keep, turned_send = small_call(
+    kept, swap, turned_keep, turned_send, terms = small_call(
         turn_kernel,
         [
             jax.ShapeDtypeStruct(half_shape, F32),
             piece_shape,
             tile_shape,
             tile_shape,
+            jax.ShapeDtypeStruct((8, width), F32),
         ],
         [h % 2, c],
         came,
         [pltpu.VMEM((2, *half_shape), F32), pltpu.VMEM((2, quarter, quarter), F32)],
     )
+    reduced_rhs = camera_grad - (terms[0] + terms[1])
     got = rotate(turned_send, "c", C, 1)
     swapped = rotate_pairs(swap)
     mirrored = small_call(

time: 199 us -> 191 us (0.960)
  the two profiles are of different devices: /device:TPU:46 before, /device:TPU:110 now
where the time goes in v4:
time: 191 us
  waiting for transfers between devices  90.1 us (47%)
  starting transfers between devices  60.3 us (32%)
  Pallas kernels  20 us (10%)
  other arithmetic  9.94 us (5%)
  local copies, waits for them, and re-layouts  9.13 us (5%)
    ppermute x19, waiting for transfers between devices, rotate(): lax.ppermute(array, axis, [(i, (i + step) % size) for i in range(size)])  49.2 us
    ppermute x6, starting transfers between devices, shards(): parts.append(lax.ppermute(piece, ('x', 'y'), pairs))  21.7 us
    ppermute x19, starting transfers between devices, rotate(): lax.ppermute(array, axis, [(i, (i + step) % size) for i in range(size)])  19.8 us
    pallas_call x2, Pallas kernels, product(): pl.pallas_call(functools.partial(product_kernel, first, last, at), out_sh...  16 us
    ppermute x4, waiting for transfers between devices, shards(): came.append(lax.ppermute(pieces[m], ('l', 'h'), pairs))  15 us
    ppermute x4, starting transfers between devices, shards(): came.append(lax.ppermute(pieces[m], ('l', 'h'), pairs))  14.4 us
    ppermute x6, waiting for transfers between devices, shards(): parts.append(lax.ppermute(piece, ('x', 'y'), pairs))  13.2 us
    ppermute x1, waiting for transfers between devices, rotate_pairs(): return lax.ppermute(array, 'h', [(i, i ^ 1) for i in range(H)])  6.63 us
  transfers between devices with their start and end apart: 31, of which 18 were waited for; matrix products, arithmetic and copies ran while one was open for 9% of the time, Pallas kernels for 5%

profile of v4, /device:TPU:110, one launch (start us, length us, event | category | flops | bytes accessed | tf_op | source)
XLA Modules:
  0.0 190.6 jit_solution(12666661412571770967)
XLA Ops:
  0.7 1.3 dynamic-slice_bitcast_fusion
  2.5 1.7 slice.82.refs_2_
  4.4 1.5 collective-permute-start.12
  5.9 1.9 dynamic-slice_bitcast_fusion.1
  7.8 1.7 collective-permute-start.9
  9.5 15.2 %collective-permute-done.13 = bf16[2,576,384]{2,1,0:T(8,128)(2,1)} collective-permute-done((bf16[2,576,384]{2,1,0:T(8,128)(2,1)S(1)}, bf16[2,576,384]{2,1,0:T(8,128)(2,1)}, u32[]{:S(2)}, u32[]{:S(2)}) %collective-permute-start.13) | collective-permute-done | bytes 884768 | tf_op jit(solution)/shard_map/ppermute | solution.py:21
  24.7 1.7 collective-permute-start.14
  26.4 2.6 %multiply_reduce_fusion = f32[576]{0:T(1024)S(1)} fusion(f32[6,384]{1,0:T(8,128)S(1)} %fusion.8, bf16[6]{0:T(256)(128)(2,1)S(1)} %convert_bitcast_fusion, bf16[6,384,576]{1,2,0:T(8,128)(2,1)} %param.7), kind=kLoop, calls=%fused_computation | loop fusion | flops 5307840 | bytes 2665740 | tf_op jit(solution)/shard_map/reduce_sum | solution.py:281
  30.3 14.1 %collective-permute-done.4 = s32[6]{0:T(128)S(1)} collective-permute-done((s32[6]{0:T(128)S(1)}, s32[6]{0:T(128)S(1)}, u32[]{:S(2)}, u32[]{:S(2)}) %collective-permute-start.4) | collective-permute-done | bytes 56 | tf_op jit(solution)/shard_map/ppermute | solution.py:21
  44.4 1.5 collective-permute-start.5
  46.0 3.2 %collective-permute-done.5 = s32[6]{0:T(128)S(1)} collective-permute-done((s32[6]{0:T(128)S(1)}, s32[6]{0:T(128)S(1)}, u32[]{:S(2)}, u32[]{:S(2)}) %collective-permute-start.5) | collective-permute-done | bytes 56 | tf_op jit(solution)/shard_map/ppermute | solution.py:21
  49.2 1.2 collective-permute-start.6
  50.4 3.9 %collective-permute-done.6 = s32[6]{0:T(128)S(1)} collective-permute-done((s32[6]{0:T(128)S(1)}, s32[6]{0:T(128)S(1)}, u32[]{:S(2)}, u32[]{:S(2)}) %collective-permute-start.6) | collective-permute-done | bytes 56 | tf_op jit(solution)/shard_map/ppermute | solution.py:21
  54.3 1.6 collective-permute-start.1
  55.9 2.0 %collective-permute-done.1 = f32[576]{0:T(1024)S(1)} collective-permute-done((f32[576]{0:T(1024)S(1)}, f32[576]{0:T(1024)S(1)}, u32[]{:S(2)}, u32[]{:S(2)}) %collective-permute-start.1) | collective-permute-done | bytes 2336 | tf_op jit(solution)/shard_map/ppermute | solution.py:21
  57.9 2.3 %collective-permute-start.2 = (f32[576]{0:T(1024)S(1)}, f32[576]{0:T(1024)S(1)}, u32[]{:S(2)}, u32[]{:S(2)}) collective-permute-start(f32[576]{0:T(1024)S(1)} %add.201), channel_id=1, source_target_pairs={{0,16},{8,24},{16,0},{24,8},{1,17},{9,25},{17,1},{25,9},{2,18},{10... | collective-permute-start | bytes 6920 | tf_op jit(solution)/shard_map/ppermute | solution.py:21
  60.2 2.8 %collective-permute-done.2 = f32[576]{0:T(1024)S(1)} collective-permute-done((f32[576]{0:T(1024)S(1)}, f32[576]{0:T(1024)S(1)}, u32[]{:S(2)}, u32[]{:S(2)}) %collective-permute-start.2) | collective-permute-done | bytes 2336 | tf_op jit(solution)/shard_map/ppermute | solution.py:21
  63.0 1.7 collective-permute-start.3
  64.7 1.4 slice.75
  66.1 1.3 slice.81.refs_2_
  71.0 3.0 %collective-permute-start.10 = (bf16[1,576,384]{2,1,0:T(8,128)(2,1)}, bf16[1,576,384]{2,1,0:T(8,128)(2,1)S(1)}, u32[]{:S(2)}, u32[]{:S(2)}) collective-permute-start(bf16[1,576,384]{2,1,0:T(8,128)(2,1)} %collective-permute-done.9), channel_id=1, source_target_pairs={{0,64},{64,128},{128,192},{192,0},{1,65},{65,129},{129,193},{193,1... | collective-permute-start | bytes 1327112 | tf_op jit(solution)/shard_map/ppermute | solution.py:21
  74.0 8.8 %product.2.refs_7_ = f32[3,2,2,144,1152]{4,3,2,1,0:T(8,128)S(1)} custom-call(s32[2]{0:T(128)S(1)} %pad_add_fusion.2.refs_0_, s32[4,6]{1,0:T(4,128)S(1)} %pad_add_fusion.refs_1_, bf16[4,576,384]{2,1,0:T(8,128)(2,1)S(1)} %slice.82.refs_2_, bf16[4,576,384]{2,1,0:T(8,128)(2,1)} %collective-permute-done.11.refs_3_, ...), custom_call_target="tpu_custom_call" | custom-call | flops 5096079360 | bytes 16777216 | tf_op jit(solution)/shard_map/product/pallas_call | solution.py:236
  82.8 1.5 collective-permute-done.7.refs_3_
  84.4 1.7 collective-permute-done.8.refs_4_
  86.0 7.2 %product.3 = (bf16[3,144,1152]{2,1,0:T(8,128)(2,1)}, bf16[3,144,1152]{2,1,0:T(8,128)(2,1)}, bf16[3,144,1152]{2,1,0:T(8,128)(2,1)S(1)}, bf16[3,144,1152]{2,1,0:T(8,128)(2,1)S(1)}) custom-call(s32[2]{0:T(128)S(1)} %pad_add_fusion.2.refs_0_, s32[4,6]{1,0:T(4,128)S(1)} %pad_add_fusion.refs_1_, bf16[2,576,384]{2,1,0:T(8,128)(2,1)S(1)} %slice.81.refs_2_, ...), custom_call_target="tpu_custom_call" | custom-call | flops 2548039680 | bytes 16777216 | tf_op jit(solution)/shard_map/product/pallas_call | solution.py:236
  93.8 2.4 %collective-permute-done.19 = bf16[3,144,1152]{2,1,0:T(8,128)(2,1)} collective-permute-done((bf16[3,144,1152]{2,1,0:T(8,128)(2,1)}, bf16[3,144,1152]{2,1,0:T(8,128)(2,1)}, u32[]{:S(2)}, u32[]{:S(2)}) %collective-permute-start.19) | collective-permute-done | bytes 995360 | tf_op jit(solution)/shard_map/ppermute | solution.py:21
  96.2 2.4 %fusion.7 = (bf16[144,1152]{1,0:T(8,128)(2,1)S(1)}, bf16[144,1152]{1,0:T(8,128)(2,1)S(1)}, bf16[144,1152]{1,0:T(8,128)(2,1)}, bf16[144,1152]{1,0:T(8,128)(2,1)S(1)}) fusion(bf16[3,144,1152]{2,1,0:T(8,128)(2,1)} %collective-permute-done.19, s32[]{:T(128)S(6)} %select_n.168, bf16[3,144,1152]{2,1,0:T(8,128)(2,1)S(1)} %get-tuple-element.24, s32[]{:T(128)S(6)} %select_n.166, ...), kind=kLoop, calls=%fused_computation.20 | loop fusion | flops 2820096 | bytes 3981329 | tf_op jit(solution)/shard_map/convert_element_type | solution.py:318
  98.6 1.3 collective-permute-start.20
  100.1 1.3 collective-permute-start.23
  101.4 6.8 %collective-permute-start.21 = (bf16[144,1152]{1,0:T(8,128)(2,1)S(1)}, bf16[144,1152]{1,0:T(8,128)(2,1)S(1)}, u32[]{:S(2)}, u32[]{:S(2)}) collective-permute-start(bf16[144,1152]{1,0:T(8,128)(2,1)S(1)} %get-tuple-element.37), channel_id=1, source_target_pairs={{0,16},{16,0},{24,8},{64,80},{72,88},{88,72},{128,144},{136,152},{... | collective-permute-start | bytes 995336 | tf_op jit(solution)/shard_map/ppermute | solution.py:319
  108.3 1.9 %collective-permute-start.22 = (bf16[144,1152]{1,0:T(8,128)(2,1)S(1)}, bf16[144,1152]{1,0:T(8,128)(2,1)S(1)}, u32[]{:S(2)}, u32[]{:S(2)}) collective-permute-start(bf16[144,1152]{1,0:T(8,128)(2,1)S(1)} %get-tuple-element.36), channel_id=1, source_target_pairs={{8,0},{16,8},{24,16},{64,88},{80,72},{88,80},{128,152},{136,128},{... | collective-permute-start | bytes 995336 | tf_op jit(solution)/shard_map/ppermute | solution.py:319
  110.2 1.7 fusion.3
  111.9 1.3 collective-permute-start.16
  113.2 5.7 %collective-permute-start.17 = (bf16[144,1152]{1,0:T(8,128)(2,1)S(1)}, bf16[144,1152]{1,0:T(8,128)(2,1)S(1)}, u32[]{:S(2)}, u32[]{:S(2)}) collective-permute-start(bf16[144,1152]{1,0:T(8,128)(2,1)S(1)} %get-tuple-element.41), channel_id=1, source_target_pairs={{0,16},{16,0},{24,8},{64,80},{72,88},{88,72},{128,144},{136,152},{... | collective-permute-start | bytes 995336 | tf_op jit(solution)/shard_map/ppermute | solution.py:319
  119.0 4.7 %collective-permute-start.18 = (bf16[144,1152]{1,0:T(8,128)(2,1)S(1)}, bf16[144,1152]{1,0:T(8,128)(2,1)S(1)}, u32[]{:S(2)}, u32[]{:S(2)}) collective-permute-start(bf16[144,1152]{1,0:T(8,128)(2,1)S(1)} %get-tuple-element.40), channel_id=1, source_target_pairs={{8,0},{16,8},{24,16},{64,88},{80,72},{88,80},{128,152},{136,128},{... | collective-permute-start | bytes 995336 | tf_op jit(solution)/shard_map/ppermute | solution.py:319
  123.7 6.2 %collective-permute-done.22.refs_7_ = bf16[144,1152]{1,0:T(8,128)(2,1)S(1)} collective-permute-done((bf16[144,1152]{1,0:T(8,128)(2,1)S(1)}, bf16[144,1152]{1,0:T(8,128)(2,1)S(1)}, u32[]{:S(2)}, u32[]{:S(2)}) %collective-permute-start.22) | collective-permute-done | bytes 331808 | tf_op jit(solution)/shard_map/ppermute | solution.py:319
  130.5 6.4 %collective-permute-done.18.refs_3_ = bf16[144,1152]{1,0:T(8,128)(2,1)S(1)} collective-permute-done((bf16[144,1152]{1,0:T(8,128)(2,1)S(1)}, bf16[144,1152]{1,0:T(8,128)(2,1)S(1)}, u32[]{:S(2)}, u32[]{:S(2)}) %collective-permute-start.18) | collective-permute-done | bytes 331808 | tf_op jit(solution)/shard_map/ppermute | solution.py:319
  138.0 5.5 %collective-permute-start.24 = (bf16[152,576]{1,0:T(8,128)(2,1)S(1)}, bf16[152,576]{1,0:T(8,128)(2,1)S(1)}, u32[]{:S(2)}, u32[]{:S(2)}) collective-permute-start(bf16[152,576]{1,0:T(8,128)(2,1)S(1)} %get-tuple-element.27), channel_id=1, source_target_pairs={{0,0},{2,32},{4,2},{6,34},{32,4},{34,36},{36,6},{38,38},{1,1},{3,3... | collective-permute-start | bytes 525320 | tf_op jit(solution)/shard_map/ppermute | solution.py:338
  143.6 2.9 %collective-permute-start.26 = (bf16[152,576]{1,0:T(8,128)(2,1)S(1)}, bf16[152,576]{1,0:T(8,128)(2,1)S(1)}, u32[]{:S(2)}, u32[]{:S(2)}) collective-permute-start(bf16[152,576]{1,0:T(8,128)(2,1)S(1)} %get-tuple-element.29), channel_id=1, source_target_pairs={{0,2},{2,34},{4,0},{6,32},{32,6},{34,38},{36,4},{38,36},{1,3},{3,3... | collective-permute-start | bytes 525320 | tf_op jit(solution)/shard_map/ppermute | solution.py:338
  146.5 5.9 %collective-permute-start.27 = (bf16[152,576]{1,0:T(8,128)(2,1)S(1)}, bf16[152,576]{1,0:T(8,128)(2,1)S(1)}, u32[]{:S(2)}, u32[]{:S(2)}) collective-permute-start(bf16[152,576]{1,0:T(8,128)(2,1)S(1)} %get-tuple-element.30), channel_id=1, source_target_pairs={{0,34},{2,2},{4,32},{6,0},{32,38},{34,6},{36,36},{38,4},{1,35},{3,... | collective-permute-start | bytes 525320 | tf_op jit(solution)/shard_map/ppermute | solution.py:338
  152.5 4.8 %collective-permute-done.25.refs_1_ = bf16[152,576]{1,0:T(8,128)(2,1)S(1)} collective-permute-done((bf16[152,576]{1,0:T(8,128)(2,1)S(1)}, bf16[152,576]{1,0:T(8,128)(2,1)S(1)}, u32[]{:S(2)}, u32[]{:S(2)}) %collective-permute-start.25) | collective-permute-done | bytes 175136 | tf_op jit(solution)/shard_map/ppermute | solution.py:338
  157.3 10.2 %collective-permute-done.27.refs_3_ = bf16[152,576]{1,0:T(8,128)(2,1)S(1)} collective-permute-done((bf16[152,576]{1,0:T(8,128)(2,1)S(1)}, bf16[152,576]{1,0:T(8,128)(2,1)S(1)}, u32[]{:S(2)}, u32[]{:S(2)}) %collective-permute-start.27) | collective-permute-done | bytes 175136 | tf_op jit(solution)/shard_map/ppermute | solution.py:338
  168.7 1.2 collective-permute-done.29.got_ref
  170.1 1.9 %collective-permute-start.30 = (bf16[144,576]{1,0:T(8,128)(2,1)S(1)}, bf16[144,576]{1,0:T(8,128)(2,1)S(1)}, u32[]{:S(2)}, u32[]{:S(2)}) collective-permute-start(bf16[144,576]{1,0:T(8,128)(2,1)S(1)} %shard_map.88), channel_id=1, source_target_pairs={{8,64},{10,66},{12,96},{14,98},{40,68},{42,70},{44,100},{46,102},{... | collective-permute-start | bytes 497672 | tf_op jit(solution)/shard_map/ppermute | solution.py:371
  173.2 2.4 %collective-permute-start.28 = (bf16[72,576]{1,0:T(8,128)(2,1)S(1)}, bf16[72,576]{1,0:T(8,128)(2,1)S(1)}, u32[]{:S(2)}, u32[]{:S(2)}) collective-permute-start(bf16[72,576]{1,0:T(8,128)(2,1)S(1)} %get-tuple-element.32), channel_id=1, source_target_pairs={{0,2},{2,0},{4,6},{6,4},{1,3},{3,1},{5,7},{7,5},{8,10},{10,8},{12,... | collective-permute-start | bytes 248840 | tf_op jit(solution)/shard_map/ppermute | solution.py:121
  176.2 6.6 %collective-permute-done.28.swapped_ref = bf16[72,576]{1,0:T(8,128)(2,1)S(1)} collective-permute-done((bf16[72,576]{1,0:T(8,128)(2,1)S(1)}, bf16[72,576]{1,0:T(8,128)(2,1)S(1)}, u32[]{:S(2)}, u32[]{:S(2)}) %collective-permute-start.28) | collective-permute-done | bytes 82976 | tf_op jit(solution)/shard_map/ppermute | solution.py:121
  182.8 6.0 %collective-permute-done.30.mirror_ref = bf16[144,576]{1,0:T(8,128)(2,1)S(1)} collective-permute-done((bf16[144,576]{1,0:T(8,128)(2,1)S(1)}, bf16[144,576]{1,0:T(8,128)(2,1)S(1)}, u32[]{:S(2)}, u32[]{:S(2)}) %collective-permute-start.30) | collective-permute-done | bytes 165920 | tf_op jit(solution)/shard_map/ppermute | solution.py:371
  188.8 1.8 shard_map.89
  (69 shorter events, 11.5 us)
Async XLA Ops:
  1.9 7.5 %copy-start = (f32[6,9,128]{2,0,1:T(8,128)S(1)}, f32[6,9,128]{2,0,1:T(8,128)}, u32[]{:S(2)}) copy-start(f32[6,9,128]{2,0,1:T(8,128)} %param.9) | copy-start | bytes 82948
  1.9 7.5 %copy-start.1 = (f32[6,384]{1,0:T(8,128)S(1)}, f32[6,384]{1,0:T(8,128)}, u32[]{:S(2)}) copy-start(f32[6,384]{1,0:T(8,128)} %param.13) | copy-start | bytes 27652
  1.9 24.4 %copy-start.6 = (s32[6,1]{0,1:T(1,128)S(1)}, s32[6,1]{0,1:T(1,128)}, u32[]{:S(2)}) copy-start(s32[6,1]{0,1:T(1,128)} %param.8) | copy-start | bytes 76
  2.0 22.7 %collective-permute-start.13 = (bf16[2,576,384]{2,1,0:T(8,128)(2,1)S(1)}, bf16[2,576,384]{2,1,0:T(8,128)(2,1)}, u32[]{:S(2)}, u32[]{:S(2)}) collective-permute-start(bf16[2,576,384]{2,1,0:T(8,128)(2,1)S(1)} %dynamic-slice_bitcast_fusion), channel_id=1, source_target_pairs={{0,64},{64,128},{128,192},{192,0},{1,65},{65,129},{129,193},{193,1... | collective-permute-start | bytes 2654216 | tf_op jit(solution)/shard_map/ppermute | solution.py:21
  4.2 69.8 %collective-permute-start.11 = (bf16[4,576,384]{2,1,0:T(8,128)(2,1)S(1)}, bf16[4,576,384]{2,1,0:T(8,128)(2,1)}, u32[]{:S(2)}, u32[]{:S(2)}) collective-permute-start(bf16[4,576,384]{2,1,0:T(8,128)(2,1)S(1)} %slice.82.refs_2_), channel_id=1, source_target_pairs={{0,32},{32,0},{1,33},{33,1},{2,34},{34,2},{3,35},{35,3},{4,36},{36... | collective-permute-start | bytes 5308424 | tf_op jit(solution)/shard_map/ppermute | solution.py:21
  4.4 69.6 %collective-permute-start.12 = (bf16[4,576,384]{2,1,0:T(8,128)(2,1)S(1)}, bf16[4,576,384]{2,1,0:T(8,128)(2,1)}, u32[]{:S(2)}, u32[]{:S(2)}) collective-permute-start(bf16[4,576,384]{2,1,0:T(8,128)(2,1)S(1)} %slice.82.refs_2_), channel_id=1, source_target_pairs={{0,192},{64,0},{128,64},{192,128},{1,193},{65,1},{129,65},{193,129... | collective-permute-start | bytes 5308424 | tf_op jit(solution)/shard_map/ppermute | solution.py:21
  7.8 61.5 %collective-permute-start.9 = (bf16[1,576,384]{2,1,0:T(8,128)(2,1)}, bf16[1,576,384]{2,1,0:T(8,128)(2,1)}, u32[]{:S(2)}, u32[]{:S(2)}) collective-permute-start(bf16[1,576,384]{2,1,0:T(8,128)(2,1)} %dynamic-slice_bitcast_fusion.1), channel_id=1, source_target_pairs={{0,64},{64,128},{128,192},{192,0},{1,65},{65,129},{129,193},{193,1... | collective-permute-start | bytes 1327112 | tf_op jit(solution)/shard_map/ppermute | solution.py:21
  24.7 46.4 %collective-permute-start.14 = (bf16[2,576,384]{2,1,0:T(8,128)(2,1)}, bf16[2,576,384]{2,1,0:T(8,128)(2,1)S(1)}, u32[]{:S(2)}, u32[]{:S(2)}) collective-permute-start(bf16[2,576,384]{2,1,0:T(8,128)(2,1)} %collective-permute-done.13), channel_id=1, source_target_pairs={{0,64},{64,128},{128,192},{192,0},{1,65},{65,129},{129,193},{193,1... | collective-permute-start | bytes 2654216 | tf_op jit(solution)/shard_map/ppermute | solution.py:21
  29.0 1.2 collective-permute-start
  30.2 14.2 %collective-permute-start.4 = (s32[6]{0:T(128)S(1)}, s32[6]{0:T(128)S(1)}, u32[]{:S(2)}, u32[]{:S(2)}) collective-permute-start(s32[6]{0:T(128)S(1)} %bitcast.49), channel_id=1, source_target_pairs={{0,32},{32,0},{1,33},{33,1},{2,34},{34,2},{3,35},{35,3},{4,36},{36... | collective-permute-start | bytes 80 | tf_op jit(solution)/shard_map/ppermute | solution.py:21
  44.4 21.6 %copy-start.7 = (s32[6]{0:T(128)}, s32[6]{0:T(128)S(1)}, u32[]{:S(2)}) copy-start(s32[6]{0:T(128)S(1)} %collective-permute-done.4) | copy-start | bytes 76
  44.4 4.8 %collective-permute-start.5 = (s32[6]{0:T(128)S(1)}, s32[6]{0:T(128)S(1)}, u32[]{:S(2)}, u32[]{:S(2)}) collective-permute-start(s32[6]{0:T(128)S(1)} %bitcast.50), channel_id=1, source_target_pairs={{0,192},{64,0},{128,64},{192,128},{1,193},{65,1},{129,65},{193,129... | collective-permute-start | bytes 80 | tf_op jit(solution)/shard_map/ppermute | solution.py:21
  49.2 1.2 copy-start.8
  49.2 5.1 %collective-permute-start.6 = (s32[6]{0:T(128)S(1)}, s32[6]{0:T(128)S(1)}, u32[]{:S(2)}, u32[]{:S(2)}) collective-permute-start(s32[6]{0:T(128)S(1)} %bitcast.51), channel_id=1, source_target_pairs={{0,128},{64,192},{128,0},{192,64},{1,129},{65,193},{129,1},{193,65... | collective-permute-start | bytes 80 | tf_op jit(solution)/shard_map/ppermute | solution.py:21
  54.3 8.7 %copy-start.9 = (s32[6]{0:T(128)}, s32[6]{0:T(128)S(1)}, u32[]{:S(2)}) copy-start(s32[6]{0:T(128)S(1)} %collective-permute-done.6) | copy-start | bytes 76
  54.3 3.6 %collective-permute-start.1 = (f32[576]{0:T(1024)S(1)}, f32[576]{0:T(1024)S(1)}, u32[]{:S(2)}, u32[]{:S(2)}) collective-permute-start(f32[576]{0:T(1024)S(1)} %add.201), channel_id=1, source_target_pairs={{0,8},{8,16},{16,24},{24,0},{1,9},{9,17},{17,25},{25,1},{2,10},{10... | collective-permute-start | bytes 6920 | tf_op jit(solution)/shard_map/ppermute | solution.py:21
  57.9 8.2 %copy-start.3 = (f32[576]{0:T(1024)}, f32[576]{0:T(1024)S(1)}, u32[]{:S(2)}) copy-start(f32[576]{0:T(1024)S(1)} %collective-permute-done.1) | copy-start | bytes 6916
  57.9 5.1 %collective-permute-start.2 = (f32[576]{0:T(1024)S(1)}, f32[576]{0:T(1024)S(1)}, u32[]{:S(2)}, u32[]{:S(2)}) collective-permute-start(f32[576]{0:T(1024)S(1)} %add.201), channel_id=1, source_target_pairs={{0,16},{8,24},{16,0},{24,8},{1,17},{9,25},{17,1},{25,9},{2,18},{10... | collective-permute-start | bytes 6920 | tf_op jit(solution)/shard_map/ppermute | solution.py:21
  63.0 3.0 %copy-start.4 = (f32[576]{0:T(1024)}, f32[576]{0:T(1024)S(1)}, u32[]{:S(2)}) copy-start(f32[576]{0:T(1024)S(1)} %collective-permute-done.2) | copy-start | bytes 6916
  63.0 5.8 %collective-permute-start.3 = (f32[576]{0:T(1024)S(1)}, f32[576]{0:T(1024)}, u32[]{:S(2)}, u32[]{:S(2)}) collective-permute-start(f32[576]{0:T(1024)S(1)} %add.201), channel_id=1, source_target_pairs={{0,24},{8,0},{16,8},{24,16},{1,25},{9,1},{17,9},{25,17},{2,26},{10... | collective-permute-start | bytes 6920 | tf_op jit(solution)/shard_map/ppermute | solution.py:21
  68.8 15.5 %collective-permute-start.7 = (bf16[2,576,384]{2,1,0:T(8,128)(2,1)S(1)}, bf16[2,576,384]{2,1,0:T(8,128)(2,1)S(1)}, u32[]{:S(2)}, u32[]{:S(2)}) collective-permute-start(bf16[2,576,384]{2,1,0:T(8,128)(2,1)S(1)} %slice.81.refs_2_), channel_id=1, source_target_pairs={{0,32},{32,0},{1,33},{33,1},{2,34},{34,2},{3,35},{35,3},{4,36},{36... | collective-permute-start | bytes 2654216 | tf_op jit(solution)/shard_map/ppermute | solution.py:21
  69.2 16.8 %collective-permute-start.8 = (bf16[2,576,384]{2,1,0:T(8,128)(2,1)S(1)}, bf16[2,576,384]{2,1,0:T(8,128)(2,1)S(1)}, u32[]{:S(2)}, u32[]{:S(2)}) collective-permute-start(bf16[2,576,384]{2,1,0:T(8,128)(2,1)S(1)} %slice.81.refs_2_), channel_id=1, source_target_pairs={{0,192},{64,0},{128,64},{192,128},{1,193},{65,1},{129,65},{193,129... | collective-permute-start | bytes 2654216 | tf_op jit(solution)/shard_map/ppermute | solution.py:21
  71.0 11.8 %collective-permute-start.10 = (bf16[1,576,384]{2,1,0:T(8,128)(2,1)}, bf16[1,576,384]{2,1,0:T(8,128)(2,1)S(1)}, u32[]{:S(2)}, u32[]{:S(2)}) collective-permute-start(bf16[1,576,384]{2,1,0:T(8,128)(2,1)} %collective-permute-done.9), channel_id=1, source_target_pairs={{0,64},{64,128},{128,192},{192,0},{1,65},{65,129},{129,193},{193,1... | collective-permute-start | bytes 1327112 | tf_op jit(solution)/shard_map/ppermute | solution.py:21
  93.2 3.0 %collective-permute-start.19 = (bf16[3,144,1152]{2,1,0:T(8,128)(2,1)}, bf16[3,144,1152]{2,1,0:T(8,128)(2,1)}, u32[]{:S(2)}, u32[]{:S(2)}) collective-permute-start(bf16[3,144,1152]{2,1,0:T(8,128)(2,1)} %get-tuple-element.25), channel_id=1, source_target_pairs={{0,1},{1,0},{2,3},{3,2},{4,5},{5,4},{6,7},{7,6},{8,9},{9,8},{10,11... | collective-permute-start | bytes 2985992 | tf_op jit(solution)/shard_map/ppermute | solution.py:21
  93.3 16.9 %collective-permute-start.15 = (bf16[3,144,1152]{2,1,0:T(8,128)(2,1)}, bf16[3,144,1152]{2,1,0:T(8,128)(2,1)}, u32[]{:S(2)}, u32[]{:S(2)}) collective-permute-start(bf16[3,144,1152]{2,1,0:T(8,128)(2,1)} %get-tuple-element.23), channel_id=1, source_target_pairs={{0,1},{1,0},{2,3},{3,2},{4,5},{5,4},{6,7},{7,6},{8,9},{9,8},{10,11... | collective-permute-start | bytes 2985992 | tf_op jit(solution)/shard_map/ppermute | solution.py:21
  98.6 20.4 %collective-permute-start.20 = (bf16[144,1152]{1,0:T(8,128)(2,1)}, bf16[144,1152]{1,0:T(8,128)(2,1)S(1)}, u32[]{:S(2)}, u32[]{:S(2)}) collective-permute-start(bf16[144,1152]{1,0:T(8,128)(2,1)} %get-tuple-element.38), channel_id=1, source_target_pairs={{0,8},{8,16},{24,0},{64,72},{72,80},{80,88},{136,144},{144,152},{1... | collective-permute-start | bytes 995336 | tf_op jit(solution)/shard_map/ppermute | solution.py:319
  100.1 13.1 %collective-permute-start.23 = (f32[576]{0:T(1024)S(1)}, f32[576]{0:T(1024)S(1)}, u32[]{:S(2)}, u32[]{:S(2)}) collective-permute-start(f32[576]{0:T(1024)S(1)} %add_add_fusion), channel_id=1, source_target_pairs={{0,32},{32,0},{1,33},{33,1},{2,34},{34,2},{3,35},{35,3},{4,36},{36... | collective-permute-start | bytes 6920 | tf_op jit(solution)/shard_map/ppermute | solution.py:21
  101.4 22.3 %collective-permute-start.21 = (bf16[144,1152]{1,0:T(8,128)(2,1)S(1)}, bf16[144,1152]{1,0:T(8,128)(2,1)S(1)}, u32[]{:S(2)}, u32[]{:S(2)}) collective-permute-start(bf16[144,1152]{1,0:T(8,128)(2,1)S(1)} %get-tuple-element.37), channel_id=1, source_target_pairs={{0,16},{16,0},{24,8},{64,80},{72,88},{88,72},{128,144},{136,152},{... | collective-permute-start | bytes 995336 | tf_op jit(solution)/shard_map/ppermute | solution.py:319
  108.3 21.6 %collective-permute-start.22 = (bf16[144,1152]{1,0:T(8,128)(2,1)S(1)}, bf16[144,1152]{1,0:T(8,128)(2,1)S(1)}, u32[]{:S(2)}, u32[]{:S(2)}) collective-permute-start(bf16[144,1152]{1,0:T(8,128)(2,1)S(1)} %get-tuple-element.36), channel_id=1, source_target_pairs={{8,0},{16,8},{24,16},{64,88},{80,72},{88,80},{128,152},{136,128},{... | collective-permute-start | bytes 995336 | tf_op jit(solution)/shard_map/ppermute | solution.py:319
  111.9 56.8 %copy-start.5 = (s32[576]{0:T(1024)S(1)}, s32[576]{0:T(1024)}, u32[]{:S(2)}) copy-start(s32[576]{0:T(1024)} %param.11) | copy-start | bytes 6916
  111.9 63.7 %copy-start.2 = (f32[576]{0:T(1024)S(1)}, f32[576]{0:T(1024)}, u32[]{:S(2)}) copy-start(f32[576]{0:T(1024)} %param.12) | copy-start | bytes 6916
  111.9 18.0 %collective-permute-start.16 = (bf16[144,1152]{1,0:T(8,128)(2,1)S(1)}, bf16[144,1152]{1,0:T(8,128)(2,1)S(1)}, u32[]{:S(2)}, u32[]{:S(2)}) collective-permute-start(bf16[144,1152]{1,0:T(8,128)(2,1)S(1)} %get-tuple-element.42), channel_id=1, source_target_pairs={{0,8},{8,16},{24,0},{64,72},{72,80},{80,88},{136,144},{144,152},{1... | collective-permute-start | bytes 995336 | tf_op jit(solution)/shard_map/ppermute | solution.py:319
  113.2 17.3 %collective-permute-start.17 = (bf16[144,1152]{1,0:T(8,128)(2,1)S(1)}, bf16[144,1152]{1,0:T(8,128)(2,1)S(1)}, u32[]{:S(2)}, u32[]{:S(2)}) collective-permute-start(bf16[144,1152]{1,0:T(8,128)(2,1)S(1)} %get-tuple-element.41), channel_id=1, source_target_pairs={{0,16},{16,0},{24,8},{64,80},{72,88},{88,72},{128,144},{136,152},{... | collective-permute-start | bytes 995336 | tf_op jit(solution)/shard_map/ppermute | solution.py:319
  119.0 17.9 %collective-permute-start.18 = (bf16[144,1152]{1,0:T(8,128)(2,1)S(1)}, bf16[144,1152]{1,0:T(8,128)(2,1)S(1)}, u32[]{:S(2)}, u32[]{:S(2)}) collective-permute-start(bf16[144,1152]{1,0:T(8,128)(2,1)S(1)} %get-tuple-element.40), channel_id=1, source_target_pairs={{8,0},{16,8},{24,16},{64,88},{80,72},{88,80},{128,152},{136,128},{... | collective-permute-start | bytes 995336 | tf_op jit(solution)/shard_map/ppermute | solution.py:319
  138.0 14.5 %collective-permute-start.24 = (bf16[152,576]{1,0:T(8,128)(2,1)S(1)}, bf16[152,576]{1,0:T(8,128)(2,1)S(1)}, u32[]{:S(2)}, u32[]{:S(2)}) collective-permute-start(bf16[152,576]{1,0:T(8,128)(2,1)S(1)} %get-tuple-element.27), channel_id=1, source_target_pairs={{0,0},{2,32},{4,2},{6,34},{32,4},{34,36},{36,6},{38,38},{1,1},{3,3... | collective-permute-start | bytes 525320 | tf_op jit(solution)/shard_map/ppermute | solution.py:338
  143.5 13.8 %collective-permute-start.25 = (bf16[152,576]{1,0:T(8,128)(2,1)S(1)}, bf16[152,576]{1,0:T(8,128)(2,1)S(1)}, u32[]{:S(2)}, u32[]{:S(2)}) collective-permute-start(bf16[152,576]{1,0:T(8,128)(2,1)S(1)} %get-tuple-element.28), channel_id=1, source_target_pairs={{0,32},{2,0},{4,34},{6,2},{32,36},{34,4},{36,38},{38,6},{1,33},{3,... | collective-permute-start | bytes 525320 | tf_op jit(solution)/shard_map/ppermute | solution.py:338
  143.6 13.7 %collective-permute-start.26 = (bf16[152,576]{1,0:T(8,128)(2,1)S(1)}, bf16[152,576]{1,0:T(8,128)(2,1)S(1)}, u32[]{:S(2)}, u32[]{:S(2)}) collective-permute-start(bf16[152,576]{1,0:T(8,128)(2,1)S(1)} %get-tuple-element.29), channel_id=1, source_target_pairs={{0,2},{2,34},{4,0},{6,32},{32,6},{34,38},{36,4},{38,36},{1,3},{3,3... | collective-permute-start | bytes 525320 | tf_op jit(solution)/shard_map/ppermute | solution.py:338
  146.5 21.0 %collective-permute-start.27 = (bf16[152,576]{1,0:T(8,128)(2,1)S(1)}, bf16[152,576]{1,0:T(8,128)(2,1)S(1)}, u32[]{:S(2)}, u32[]{:S(2)}) collective-permute-start(bf16[152,576]{1,0:T(8,128)(2,1)S(1)} %get-tuple-element.30), channel_id=1, source_target_pairs={{0,34},{2,2},{4,32},{6,0},{32,38},{34,6},{36,36},{38,4},{1,35},{3,... | collective-permute-start | bytes 525320 | tf_op jit(solution)/shard_map/ppermute | solution.py:338
  168.5 1.5 collective-permute-start.29
  170.1 18.7 %collective-permute-start.30 = (bf16[144,576]{1,0:T(8,128)(2,1)S(1)}, bf16[144,576]{1,0:T(8,128)(2,1)S(1)}, u32[]{:S(2)}, u32[]{:S(2)}) collective-permute-start(bf16[144,576]{1,0:T(8,128)(2,1)S(1)} %shard_map.88), channel_id=1, source_target_pairs={{8,64},{10,66},{12,96},{14,98},{40,68},{42,70},{44,100},{46,102},{... | collective-permute-start | bytes 497672 | tf_op jit(solution)/shard_map/ppermute | solution.py:371
  173.2 9.6 %collective-permute-start.28 = (bf16[72,576]{1,0:T(8,128)(2,1)S(1)}, bf16[72,576]{1,0:T(8,128)(2,1)S(1)}, u32[]{:S(2)}, u32[]{:S(2)}) collective-permute-start(bf16[72,576]{1,0:T(8,128)(2,1)S(1)} %get-tuple-element.32), channel_id=1, source_target_pairs={{0,2},{2,0},{4,6},{6,4},{1,3},{3,1},{5,7},{7,5},{8,10},{10,8},{12,... | collective-permute-start | bytes 248840 | tf_op jit(solution)/shard_map/ppermute | solution.py:121
